TPU v7x, 32 devices: a whole 2x2x4 slice. The times are simulated.
32 devices in a mesh: dp: 8 (over y, x, core), mp: 4 (over z).
Axes of the slice: x: 2, y: 2, z: 4, core: 2. Of those that a mesh axis runs over, the one named last changes fastest.
Arguments:
- frames: bfloat16 [16384, 640], P('dp'), may hold values from -6 to 6
- seg_ids: int32 [16384], P('dp'), may hold values from 0 to 15, as said below
- qkv_weight: bfloat16 [3, 640, 768], P(None, 'dp', 'mp'), may hold values from -0.25 to 0.25
- qkv_bias: float32 [2, 768], P(None, 'mp'), may hold values from -3 to 3
- out_weight: bfloat16 [768, 640], P('mp', 'dp'), may hold values from -1.5 to 1.5
- out_bias: float32 [640], replicated, may hold values from -3 to 3
- gain_one: float32 [640], replicated, may hold values from 0.1 to 1.9
- shift_one: float32 [640], replicated, may hold values from -3 to 3
- up_weight: bfloat16 [640, 2240], P('dp', 'mp'), may hold values from -0.25 to 0.25
- up_bias: float32 [2240], P('mp'), may hold values from -3 to 3
- down_weight: bfloat16 [2240, 640], P('mp', 'dp'), may hold values from -0.125 to 0.125
- down_bias: float32 [640], replicated, may hold values from -3 to 3
- gain_two: float32 [640], replicated, may hold values from 0.1 to 1.9
- shift_two: float32 [640], replicated, may hold values from -3 to 3
- cotangent: bfloat16 [16384, 640], P('dp'), may hold values from -6 to 6
Outputs:
- output_frames: bfloat16 [16384, 640], P(('dp', 'mp'))
- frames_grad: bfloat16 [16384, 640], P(('dp', 'mp'))
- qkv_grad: float32 [3, 640, 768], P(None, 'dp', 'mp')
- qkv_bias_grad: float32 [2, 768], P(None, 'mp')
- out_grad: float32 [768, 640], P('mp', 'dp')
- out_bias_grad: float32 [640], replicated
- gain_one_grad: float32 [640], replicated
- shift_one_grad: float32 [640], replicated
- up_grad: float32 [640, 2240], P('dp', 'mp')
- up_bias_grad: float32 [2240], P('mp')
- down_grad: float32 [2240, 640], P('mp', 'dp')
- down_bias_grad: float32 [640], replicated
- gain_two_grad: float32 [640], replicated
- shift_two_grad: float32 [640], replicated
Inputs may be any that keep to these rules, and one draw needn't show every extreme that they name: `seg_ids`: each block of 2048 frames that one index of dp holds contains 1 to 16 whole utterances laid end to end; within the block the number starts at 0 and rises by one at each new utterance. In every draw some block holds a single utterance of 2048 frames and some block holds 16 utterances.
All inputs are finite; a program needn't handle non-finite values.
Results may differ from a plain program's by a relative error of at most 0.019.
Values may be sent and summed in bfloat16 or wider, within the bound.
A program may use at most 192 MiB of HBM per device.

v0:
```python
import functools
import math

import jax
import jax.numpy as jnp
from jax import lax
from jax.experimental import pallas as pl
from jax.experimental.pallas import tpu as pltpu
from jax.sharding import PartitionSpec as P

HEADS = 10
HD = 64
EPS = 1e-05
SCALE = 0.125
MAX_SEGS = 16
MASKED = -1e30
UNIT = SCALE * math.log2(math.e)
AUG = 256
VAUG = 128
NT = (((1,), (1,)), ((), ()))
TN = (((0,), (0,)), ((), ()))
F32 = jnp.float32
BF16 = jnp.bfloat16
VMEM_LIMIT = 56 << 20
MESH = pl.DeviceIdType.MESH
CHIPS = 3
HALF = 640


def thirds(wide):
    first = wide.astype(BF16)
    rest = wide - first.astype(F32)
    second = rest.astype(BF16)
    third = (rest - second.astype(F32)).astype(BF16)
    return first, second, third


def lane_marks(rows, width, count):
    return lax.broadcasted_iota(jnp.int32, (rows, width), 1) < count


def spread_rows(made, seg, slots, qs_ref, ka_ref, va_ref, kk_ref, rows):
    count = made.shape[0]
    width = slots * HD
    marks = seg == lax.broadcasted_iota(jnp.int32, (count, MAX_SEGS), 1)
    chosen = jnp.where(marks, 1.0, 0.0).astype(BF16)
    barred = jnp.where(marks, 0.0, MASKED).astype(BF16)
    tail = AUG - 3 * HD - MAX_SEGS
    q_tail = jnp.zeros((count, tail), BF16)
    minus = jnp.where(lane_marks(count, tail, 3), -1.0, 0.0).astype(BF16)
    v_tail = jnp.where(lane_marks(count, VAUG - HD, 3), -1.0, 0.0).astype(BF16)
    for slot in range(slots):
        at = slot * HD
        q = made[:, at : at + HD]
        k = made[:, width + at : width + at + HD]
        v = made[:, 2 * width + at : 2 * width + at + HD]
        one, two, three = thirds(k.astype(F32) * UNIT)
        qs_ref[slot, rows, :] = jnp.concatenate([q, q, q, chosen, q_tail], 1)
        ka_ref[slot, rows, :] = jnp.concatenate([one, two, three, barred, minus], 1)
        va_ref[slot, rows, :] = jnp.concatenate([v, v_tail], 1)
        kk_ref[slot, rows, :] = k


def plane_barrier(peers):
    barrier = pltpu.get_barrier_semaphore()
    for peer in peers:
        pl.semaphore_signal(barrier, inc=1, device_id=peer, device_id_type=MESH)
    pl.semaphore_wait(barrier, len(peers))


def remote(src, dst, send, recv, peer):
    return pltpu.make_async_remote_copy(
        src_ref=src, dst_ref=dst, send_sem=send, recv_sem=recv, device_id=peer, device_id_type=MESH
    )


def front_kernel(
    slots, sub,
    x_ref, wq_ref, pack_ref, bias_ref, off_ref, seg_ref,
    all_ref, wfull_ref, ball_ref, qs_ref, ka_ref, va_ref, kk_ref, mixed_ref, got_ref,
    stage, q_send, q_recv, z_send, z_recv, w_send, w_recv, b_send, b_recv, a_send, a_recv, here,
):
    dp = lax.axis_index("dp")
    mp = lax.axis_index("mp")
    plane = [dp ^ 2, dp ^ 4, dp ^ 6]
    sibling = (dp ^ 1, mp)
    tall = [(dp, mp ^ s) for s in range(1, 4)]
    plane_barrier([sibling] + [(d, mp) for d in plane] + tall)
    rows = x_ref.shape[0]
    share = rows // 4

    mine = pltpu.make_async_copy(wq_ref, wfull_ref.at[dp], here.at[0])
    mine.start()
    firsts = [
        remote(wq_ref, wfull_ref.at[dp], q_send.at[i], q_recv.at[i], (plane[i], mp))
        for i in range(CHIPS)
    ]
    for copy in firsts:
        copy.start()
    shared = [remote(wq_ref, wfull_ref.at[dp], q_send.at[3], q_recv.at[3], sibling)]
    shared[0].start()
    own = pltpu.make_async_copy(pack_ref, all_ref.at[mp, dp], here.at[1])
    own.start()
    lifts = [
        remote(pack_ref, all_ref.at[mp, dp], z_send.at[s], z_recv.at[s], tall[s]) for s in range(3)
    ]
    own_bias = pltpu.make_async_copy(bias_ref, ball_ref.at[mp], here.at[2])
    own_bias.start()
    for copy in lifts:
        copy.start()
    biases = [
        remote(bias_ref, ball_ref.at[mp], b_send.at[s], b_recv.at[s], tall[s]) for s in range(3)
    ]
    for copy in biases:
        copy.start()
    for i in range(CHIPS):
        firsts[i].wait_recv()
        passed = remote(
            wfull_ref.at[plane[i]], wfull_ref.at[plane[i]], q_send.at[4 + i], q_recv.at[4 + i], sibling
        )
        passed.start()
        shared.append(passed)
    own.wait()

    def weights(s, kind):
        group = mp ^ s
        block = {0: dp, 1: dp, 2: dp, 4: plane[0], 5: plane[1], 6: plane[2]}
        block[3] = plane[0] if s % 2 == 0 else plane[1]
        peer = {0: (plane[0], mp), 1: (plane[1], mp)}
        peer[3] = peer[1] if s % 2 == 0 else peer[0]
        ref = all_ref.at[group, block[kind]]
        return remote(ref, ref, w_send.at[s, kind], w_recv.at[s, kind], peer.get(kind, sibling))

    def start_weights(s):
        if s > 0:
            lifts[s - 1].wait_recv()
        for kind in (0, 1, 2):
            weights(s, kind).start()

    def pass_weights(s):
        weights(s, 0).wait_recv()
        weights(s, 1).wait_recv()
        for kind in (3, 4, 5):
            weights(s, kind).start()

    def last_weights(s):
        weights(s, 3).wait_recv()
        weights(s, 6).start()

    start_weights(0)
    mine.wait()
    for copy in shared:
        copy.wait_recv()

    block = 256

    def project_rows(step, carry):
        part = pl.ds(pl.multiple_of(step * block, block), block)
        x = x_ref[part, :]
        made = off_ref[...] + jnp.zeros((block, off_ref.shape[1]), F32)
        full = jnp.concatenate([wfull_ref[d] for d in range(wfull_ref.shape[0])], 0)
        made = made + jnp.dot(x, full, preferred_element_type=F32)
        spread_rows(made.astype(BF16), seg_ref[part, :], slots, qs_ref, ka_ref, va_ref, kk_ref, part)
        return carry

    lax.fori_loop(0, rows // block, project_rows, 0)

    live_count = HEADS // 4 + (mp < HEADS % 4).astype(jnp.int32)
    per_share = share // sub
    actions = {
        0: [(start_weights, 1), (pass_weights, 0)],
        1: [(start_weights, 2), (last_weights, 0)],
        2: [(pass_weights, 1)],
        3: [(start_weights, 3), (last_weights, 1)],
        4: [(pass_weights, 2)],
        5: [(last_weights, 2)],
        6: [(pass_weights, 3)],
    }

    def send_rows(step, stage_index):
        group = mp ^ stage_index
        offset = pl.multiple_of(lax.rem(step, per_share) * sub, sub)
        source = pl.ds(pl.multiple_of(group * share, share) + offset, sub)
        return remote(
            stage.at[source], got_ref.at[mp, pl.ds(offset, sub)], a_send.at[step], a_recv.at[step],
            (dp, group),
        )

    def attend_rows(step, carry):
        stage_index = 3 - step // per_share
        group = mp ^ stage_index
        offset = lax.rem(step, per_share) * sub
        part = pl.ds(pl.multiple_of(group * share + offset, sub), sub)
        for when, todo in actions.items():

            @pl.when(step == when)
            def _():
                for act, s in todo:
                    act(s)

        for slot in range(slots):
            x = lax.dot_general(
                qs_ref[slot, part, :], ka_ref[slot], NT, preferred_element_type=F32
            )
            top = jnp.max(x, -1, keepdims=True)
            p = jnp.exp2(x - top).astype(BF16)
            made = jnp.dot(p, va_ref[slot], preferred_element_type=F32)
            total = -made[:, HD : HD + 1]
            mixed = made[:, :HD] / total
            one, two, three = thirds(top + jnp.log2(total))
            base = 3 * HD + MAX_SEGS
            qs_ref[slot, part, base : base + 3] = jnp.concatenate([one, two, three], 1)
            mixed_ref[slot, part, :] = mixed
            alive = (slot < live_count).astype(F32)
            stage[part, slot * HD : (slot + 1) * HD] = (mixed * alive).astype(BF16)

        @pl.when(step < 3 * per_share)
        def _():
            send_rows(step, stage_index).start()

        return carry

    lax.fori_loop(0, rows // sub, attend_rows, 0)
    start = pl.ds(pl.multiple_of(mp * share, share), share)
    keep = pltpu.make_async_copy(stage.at[start], got_ref.at[mp], here.at[3])
    keep.start()
    last_weights(3)
    for s in range(4):
        weights(s, 2).wait_recv()
        for kind in (4, 5, 6):
            weights(s, kind).wait_recv()
        for kind in range(7):
            weights(s, kind).wait_send()
    for copy in firsts + shared + lifts:
        copy.wait_send()
    for copy in biases:
        copy.wait()
    for step in range(3 * per_share):
        send_rows(step, 3 - step // per_share).wait()
    own_bias.wait()
    keep.wait()


def front(frames, wq, packed, up_bias, offsets, seg_ids, slots):
    rows, _ = frames.shape
    piece, lanes = packed.shape
    sub = 256
    shape = lambda n: jax.ShapeDtypeStruct((slots, rows, n), BF16)
    vmem = pl.BlockSpec(memory_space=pltpu.VMEM)
    dma = pltpu.SemaphoreType.DMA
    steps = rows // sub
    return pl.pallas_call(
        functools.partial(front_kernel, slots, sub),
        in_specs=[vmem] * 6,
        out_specs=[vmem] * 9,
        out_shape=[
            jax.ShapeDtypeStruct((4, 8, piece, lanes), BF16),
            jax.ShapeDtypeStruct((8,) + wq.shape, BF16),
            jax.ShapeDtypeStruct((4,) + up_bias.shape, F32),
            shape(AUG), shape(AUG), shape(VAUG), shape(HD),
            jax.ShapeDtypeStruct((slots, rows, HD), F32),
            jax.ShapeDtypeStruct((4, rows // 4, slots * HD), BF16),
        ],
        scratch_shapes=[
            pltpu.VMEM((rows, slots * HD), BF16),
            dma((7,)), dma((7,)), dma((3,)), dma((3,)), dma((4, 7)), dma((4, 7)), dma((3,)), dma((3,)),
            dma((steps,)), dma((steps,)), dma((4,)),
        ],
        compiler_params=pltpu.CompilerParams(
            collective_id=1, has_side_effects=True, vmem_limit_bytes=VMEM_LIMIT
        ),
        name="front",
    )(frames, wq, packed, up_bias, offsets, seg_ids.reshape(rows, 1))


def project_kernel(slots, x_ref, w_ref, b_ref, seg_ref, qs_ref, ka_ref, va_ref, kk_ref):
    made = jnp.dot(x_ref[...], w_ref[...], preferred_element_type=F32) + b_ref[...]
    spread_rows(
        made.astype(BF16), seg_ref[...], slots, qs_ref, ka_ref, va_ref, kk_ref, slice(None)
    )


def project(frames, weight, offsets, seg_ids, slots):
    rows, depth = frames.shape
    block = min(512, rows)
    spread = lambda n: pl.BlockSpec((slots, block, n), lambda i: (0, i, 0))
    shape = lambda n: jax.ShapeDtypeStruct((slots, rows, n), BF16)
    return pl.pallas_call(
        functools.partial(project_kernel, slots),
        grid=(rows // block,),
        in_specs=[
            pl.BlockSpec((block, depth), lambda i: (i, 0)),
            pl.BlockSpec(weight.shape, lambda i: (0, 0)),
            pl.BlockSpec((1, offsets.shape[1]), lambda i: (0, 0)),
            pl.BlockSpec((block, 1), lambda i: (i, 0)),
        ],
        out_specs=[spread(AUG), spread(AUG), spread(VAUG), spread(HD)],
        out_shape=[shape(AUG), shape(AUG), shape(VAUG), shape(HD)],
        compiler_params=pltpu.CompilerParams(vmem_limit_bytes=VMEM_LIMIT),
        name="project",
    )(frames, weight, offsets, seg_ids.reshape(rows, 1))


def attend_kernel(sub, qs_ref, ka_ref, va_ref, qn_ref, mixed_ref):
    for at in range(0, qs_ref.shape[1], sub):
        part = slice(at, at + sub)
        x = lax.dot_general(qs_ref[0, part, :], ka_ref[0], NT, preferred_element_type=F32)
        top = jnp.max(x, -1, keepdims=True)
        p = jnp.exp2(x - top).astype(BF16)
        made = jnp.dot(p, va_ref[0], preferred_element_type=F32)
        total = -made[:, HD : HD + 1]
        mixed_ref[0, part, :] = made[:, :HD] / total
        one, two, three = thirds(top + jnp.log2(total))
        base = 3 * HD + MAX_SEGS
        blank = jnp.zeros((sub, AUG - base - 3), BF16)
        qn_ref[0, part, :] = jnp.concatenate(
            [qs_ref[0, part, :base], one, two, three, blank], 1
        )


def attend(qs, ka, va):
    slots, rows, _ = qs.shape
    block = min(512, rows)
    sub = min(256, block)
    whole = lambda n: pl.BlockSpec((1, rows, n), lambda h, i: (h, 0, 0))
    some = lambda n: pl.BlockSpec((1, block, n), lambda h, i: (h, i, 0))
    return pl.pallas_call(
        functools.partial(attend_kernel, sub),
        grid=(slots, rows // block),
        in_specs=[some(AUG), whole(AUG), whole(VAUG)],
        out_specs=[some(AUG), some(HD)],
        out_shape=[
            jax.ShapeDtypeStruct((slots, rows, AUG), BF16),
            jax.ShapeDtypeStruct((slots, rows, HD), F32),
        ],
        compiler_params=pltpu.CompilerParams(vmem_limit_bytes=VMEM_LIMIT),
        name="attend",
    )(qs, ka, va)


def attend_back_kernel(
    sub, qs_ref, ka_ref, va_ref, kk_ref, mixed_ref, up_ref, dq_ref, dk_ref, dv_ref, dk_acc, dv_acc
):
    step = pl.program_id(1)

    @pl.when(step == 0)
    def _():
        dk_acc[...] = jnp.zeros_like(dk_acc)
        dv_acc[...] = jnp.zeros_like(dv_acc)

    for at in range(0, qs_ref.shape[1], sub):
        part = slice(at, at + sub)
        q = qs_ref[0, part, :HD]
        up = up_ref[0, part, :]
        d_one, d_two, d_three = thirds(
            jnp.sum(up.astype(F32) * mixed_ref[0, part, :], -1, keepdims=True)
        )
        blank = lambda n: jnp.zeros((sub, n), BF16)
        upper = jnp.concatenate([up, d_one, d_two, d_three, blank(VAUG - HD - 3)], 1)
        x = lax.dot_general(qs_ref[0, part, :], ka_ref[0], NT, preferred_element_type=F32)
        p = jnp.exp2(x)
        dp = lax.dot_general(upper, va_ref[0], NT, preferred_element_type=F32)
        ds = (p * dp).astype(BF16)
        dv_acc[...] += lax.dot_general(up, p.astype(BF16), TN, preferred_element_type=F32)
        dk_acc[...] += lax.dot_general(q, ds, TN, preferred_element_type=F32)
        dq_ref[0, part, :] = (
            jnp.dot(ds, kk_ref[0], preferred_element_type=F32) * SCALE
        ).astype(BF16)

    @pl.when(step == pl.num_programs(1) - 1)
    def _():
        dk_ref[0] = (dk_acc[...] * SCALE).T.astype(BF16)
        dv_ref[0] = dv_acc[...].T.astype(BF16)


def attend_back(qs, ka, va, kk, mixed, up):
    slots, rows, _ = qs.shape
    block = min(512, rows)
    sub = min(256, block)
    whole = lambda n: pl.BlockSpec((1, rows, n), lambda h, i: (h, 0, 0))
    some = lambda n: pl.BlockSpec((1, block, n), lambda h, i: (h, i, 0))
    shape = jax.ShapeDtypeStruct((slots, rows, HD), BF16)
    return pl.pallas_call(
        functools.partial(attend_back_kernel, sub),
        grid=(slots, rows // block),
        in_specs=[
            some(AUG), whole(AUG), whole(VAUG), whole(HD), some(HD), some(HD),
        ],
        out_specs=[some(HD), whole(HD), whole(HD)],
        out_shape=[shape, shape, shape],
        scratch_shapes=[pltpu.VMEM((HD, rows), F32), pltpu.VMEM((HD, rows), F32)],
        compiler_params=pltpu.CompilerParams(vmem_limit_bytes=VMEM_LIMIT),
        name="attend_back",
    )(qs, ka, va, kk, mixed, up)


def norm_forward(summed):
    centre = summed - jnp.mean(summed, -1, keepdims=True)
    spread = jnp.mean(centre * centre, -1, keepdims=True)
    factor = lax.rsqrt(spread + EPS)
    return (centre * factor, factor)


def norm_backward(upper, normed, factor, gain):
    scaled = upper * gain
    return factor * (
        scaled
        - jnp.mean(scaled, -1, keepdims=True)
        - normed * jnp.mean(scaled * normed, -1, keepdims=True)
    )


def middle_kernel(
    groups, hidden_cols, block, at_ref,
    x_ref, y_ref, got_ref, w_ref, ub_ref, vec_ref,
    out_ref, s1_ref, back_ref, grad_ref, small_ref,
    ow, act, pre_low, slope, hid_low, two_low, one_low,
):
    share = out_ref.shape[0]
    width = got_ref.shape[2]
    gap = HALF - hidden_cols
    out_bias, gain_one, shift_one = vec_ref[0:1, :], vec_ref[1:2, :], vec_ref[2:3, :]
    down_bias, gain_two, shift_two = vec_ref[3:4, :], vec_ref[4:5, :], vec_ref[5:6, :]
    for g in range(groups):
        ow[g, :, :gap] = w_ref[g, :, hidden_cols:HALF]
        ow[g, :, gap:] = w_ref[g, :, HALF + hidden_cols : HALF + hidden_cols + width - gap]
    small_ref[...] = jnp.zeros_like(small_ref)
    real = lane_marks(1, HALF, hidden_cols)

    def some_rows(step, carry):
        part = pl.ds(pl.multiple_of(step * block, block), block)
        summed = x_ref[part, :].astype(F32) + out_bias
        for g in range(groups):
            summed += lax.dot_general(got_ref[g, part, :], ow[g], NT, preferred_element_type=F32)
        normed_one, factor_one = norm_forward(summed)
        hidden = normed_one * gain_one + shift_one
        hidden_low = hidden.astype(BF16)
        hid_low[part, :] = hidden_low
        feed = hidden + down_bias
        for g in range(groups):
            pre = jnp.dot(hidden_low, w_ref[g, :, :HALF], preferred_element_type=F32) + ub_ref[g]
            half = 0.5 + 0.5 * lax.erf(pre * math.sqrt(0.5))
            bell = jnp.exp(pre * pre * -0.5) * (pre * (1.0 / math.sqrt(2.0 * math.pi)))
            slope[g] = jnp.where(real, half + bell, 0.0)
            made = jnp.where(real, pre * half, 0.0).astype(BF16)
            act[g, part, :] = made
            feed += lax.dot_general(
                made, w_ref[g, :, HALF : 2 * HALF], NT, preferred_element_type=F32
            )
        normed_two, factor_two = norm_forward(feed)
        out_ref[part, :] = (normed_two * gain_two + shift_two).astype(BF16)
        upstream = y_ref[part, :].astype(F32)
        two_grad = norm_backward(upstream, normed_two, factor_two, gain_two)
        sum_two = two_grad.astype(BF16)
        two_low[part, :] = sum_two
        hidden_grad = two_grad
        for g in range(groups):
            act_grad = jnp.dot(
                sum_two, w_ref[g, :, HALF : 2 * HALF], preferred_element_type=F32
            )
            low = (slope[g] * act_grad).astype(BF16)
            pre_low[g, part, :] = low
            hidden_grad += lax.dot_general(
                low, w_ref[g, :, :HALF], NT, preferred_element_type=F32
            )
            small_ref[8 + g : 9 + g, :] += jnp.sum(low.astype(F32), 0, keepdims=True)
        one_grad = norm_backward(hidden_grad, normed_one, factor_one, gain_one)
        sum_one = one_grad.astype(BF16)
        s1_ref[part, :] = one_grad
        one_low[part, :] = sum_one
        for g in range(groups):
            back_ref[g, part, :] = jnp.dot(sum_one, ow[g], preferred_element_type=F32).astype(BF16)
        for at, term in enumerate((
            sum_one.astype(F32), hidden_grad * normed_one, hidden_grad,
            sum_two.astype(F32), upstream * normed_two, upstream,
        )):
            small_ref[at : at + 1, :] += jnp.sum(term, 0, keepdims=True)
        return carry

    lax.fori_loop(0, share // block, some_rows, 0)
    hid_flip, two_flip, one_flip = hid_low[...].T, two_low[...].T, one_low[...].T
    for g in range(groups):
        grad_up = jnp.dot(hid_flip, pre_low[g], preferred_element_type=F32).astype(BF16)
        grad_down = jnp.dot(two_flip, act[g], preferred_element_type=F32).astype(BF16)
        grad_out = jnp.dot(one_flip, got_ref[g], preferred_element_type=F32).astype(BF16)
        grad_ref[g, :, :HALF] = grad_up
        grad_ref[g, :, HALF : 2 * HALF] = grad_down
        grad_ref[g, :, hidden_cols:HALF] = grad_out[:, :gap]
        rest = width - gap
        grad_ref[g, :, HALF + hidden_cols : HALF + hidden_cols + rest] = grad_out[:, gap:]
        spare = grad_ref.shape[2] - HALF - hidden_cols - rest
        grad_ref[g, :, HALF + hidden_cols + rest :] = jnp.zeros((grad_ref.shape[1], spare), BF16)


def middle(frames, cotangent, got, weights, up_bias, vectors, mp_index, hidden_cols):
    groups, share, width = got.shape
    depth = frames.shape[1]
    block = min(256, share)
    whole = lambda a: pl.BlockSpec(a.shape, lambda i, at: (0,) * a.ndim)
    pick = pl.BlockSpec((share, depth), lambda i, at: (at[0], 0))
    same = lambda s: pl.BlockSpec(s.shape, lambda i, at: (0,) * len(s.shape))
    out_shape = [
        jax.ShapeDtypeStruct((share, depth), BF16),
        jax.ShapeDtypeStruct((share, depth), F32),
        jax.ShapeDtypeStruct((groups, share, width), BF16),
        jax.ShapeDtypeStruct(weights.shape, BF16),
        jax.ShapeDtypeStruct((16, HALF), F32),
    ]
    return pl.pallas_call(
        functools.partial(middle_kernel, groups, hidden_cols, block),
        grid_spec=pltpu.PrefetchScalarGridSpec(
            num_scalar_prefetch=1,
            grid=(1,),
            in_specs=[pick, pick, whole(got), whole(weights), whole(up_bias), whole(vectors)],
            out_specs=[same(s) for s in out_shape],
            scratch_shapes=[
                pltpu.VMEM((groups, depth, width), BF16),
                pltpu.VMEM((groups, share, HALF), BF16),
                pltpu.VMEM((groups, share, HALF), BF16),
                pltpu.VMEM((groups, block, HALF), F32),
                pltpu.VMEM((share, depth), BF16),
                pltpu.VMEM((share, depth), BF16),
                pltpu.VMEM((share, depth), BF16),
            ],
        ),
        out_shape=out_shape,
        compiler_params=pltpu.CompilerParams(vmem_limit_bytes=VMEM_LIMIT),
        name="middle",
    )(mp_index.reshape(1), frames, cotangent, got, weights, up_bias, vectors)


def body(
    frames, seg_ids, qkv_weight, qkv_bias, out_weight, out_bias, gain_one, shift_one,
    up_weight, up_bias, down_weight, down_bias, gain_two, shift_two, cotangent,
):
    rows, depth = frames.shape
    mp_size = lax.axis_size("mp")
    dp_size = lax.axis_size("dp")
    mp_index = lax.axis_index("mp")
    share = rows // mp_size
    slots = qkv_weight.shape[2] // HD
    width = slots * HD
    hidden_cols = up_weight.shape[1]
    piece = qkv_weight.shape[1]
    gap = HALF - hidden_cols
    spare = -(HALF + hidden_cols + width - gap) % 128
    live_count = HEADS // mp_size + (mp_index < HEADS % mp_size).astype(jnp.int32)
    live = (jnp.arange(slots) < live_count).astype(F32)

    wq = jnp.transpose(qkv_weight, (1, 0, 2)).reshape(piece, 3 * width)
    out_flip = out_weight.T
    packed = jnp.concatenate(
        [up_weight, out_flip[:, :gap], down_weight.T, out_flip[:, gap:], jnp.zeros((piece, spare), BF16)], 1
    )
    ub_pad = jnp.pad(up_bias, (0, gap))[None]
    offsets = jnp.concatenate([qkv_bias[0], jnp.zeros_like(qkv_bias[0]), qkv_bias[1]])[None]
    if (dp_size, mp_size) == (8, 4):
        weights, qkv_full, ub_full, qs, ka, va, kk, mixed, got = front(
            frames, wq, packed, ub_pad, offsets, seg_ids, slots
        )
        weights = weights.reshape(mp_size, depth, -1)
        qkv_full = qkv_full.reshape(depth, -1)
    else:
        qkv_full = lax.all_gather(wq, "dp", axis=0, tiled=True)
        weights = lax.all_gather(packed, "mp", axis=0, tiled=False)
        weights = lax.all_gather(weights, "dp", axis=1, tiled=True)
        ub_full = lax.all_gather(ub_pad, "mp", axis=0, tiled=False)
        qs, ka, va, kk = project(frames, qkv_full, offsets, seg_ids, slots)
        qs, mixed = attend(qs, ka, va)
        mixed_low = (mixed * live[:, None, None]).astype(BF16)
        sent = mixed_low.reshape(slots, mp_size, share, HD).transpose(1, 2, 0, 3)
        got = lax.all_to_all(sent.reshape(mp_size, share, width), "mp", 0, 0, tiled=True)
    vectors = jnp.stack(
        [out_bias, gain_one, shift_one, down_bias, gain_two, shift_two, out_bias, out_bias]
    )
    output_frames, sum_one_grad, back, partial, small = middle(
        frames, cotangent, got, weights, ub_full, vectors, mp_index, hidden_cols
    )
    back = lax.all_to_all(back, "mp", 0, 0, tiled=True)
    back = back.reshape(rows, slots, HD).transpose(1, 0, 2) * live.astype(BF16)[:, None, None]
    partial = lax.psum_scatter(partial, "dp", scatter_dimension=1, tiled=True)
    partial = lax.psum_scatter(partial, "mp", scatter_dimension=0, tiled=True)[0].astype(F32)
    small = lax.psum(small, ("dp", "mp"))

    dq, dk, dv = attend_back(qs, ka, va, kk, mixed, back)
    grads_low = jnp.stack([dq, dk, dv]).transpose(2, 0, 1, 3).reshape(rows, 3 * width)
    qkv_bias_grad = jnp.sum(grads_low.astype(F32), 0).reshape(3, width)
    qkv_bias_grad = lax.psum(jnp.stack([qkv_bias_grad[0], qkv_bias_grad[2]]), "dp")
    grad_qkv = jnp.einsum("rd,rs->ds", frames, grads_low, preferred_element_type=F32)
    arrived = lax.all_to_all(
        grad_qkv.astype(BF16).reshape(dp_size, piece, 3 * width), "dp", 0, 0, tiled=True
    )
    grad_qkv = arrived.astype(F32).sum(0).reshape(piece, 3, width).transpose(1, 0, 2)
    input_part = jnp.einsum("rs,ds->rd", grads_low, qkv_full, preferred_element_type=F32)
    input_sum = lax.psum_scatter(input_part.astype(BF16), "mp", scatter_dimension=0, tiled=True)
    frames_grad = (input_sum.astype(F32) + sum_one_grad).astype(BF16)
    out_grad = jnp.concatenate(
        [partial[:, hidden_cols:HALF], partial[:, HALF + hidden_cols : HALF + hidden_cols + width - gap]], 1
    )
    return (
        output_frames,
        frames_grad,
        grad_qkv,
        qkv_bias_grad,
        out_grad.T,
        small[0],
        small[1],
        small[2],
        partial[:, :hidden_cols],
        lax.dynamic_index_in_dim(small, 8 + mp_index, 0, False)[:hidden_cols],
        partial[:, HALF : HALF + hidden_cols].T,
        small[3],
        small[4],
        small[5],
    )


def solution(mesh):
    in_specs = (
        P("dp", None), P("dp"), P(None, "dp", "mp"), P(None, "mp"), P("mp", "dp"), P(), P(), P(),
        P("dp", "mp"), P("mp"), P("mp", "dp"), P(), P(), P(), P("dp", None),
    )
    out_specs = (
        P(("dp", "mp"), None), P(("dp", "mp"), None), P(None, "dp", "mp"), P(None, "mp"),
        P("mp", "dp"), P(), P(), P(), P("dp", "mp"), P("mp"), P("mp", "dp"), P(), P(), P(),
    )
    return jax.shard_map(body, mesh=mesh, in_specs=in_specs, out_specs=out_specs, check_vma=False)
```

profile of v0, /device:TPU:0, one launch (start us, length us, event | category | flops | bytes accessed | tf_op | source)
XLA Modules:
  0.0 286.3 jit_solution(6038643943992219113)
XLA Ops:
  7.2 0.7 slice.82
  8.0 0.9 slice.83
  8.8 0.8 fusion.3
  10.2 2.1 copy.46.seg_ref
  12.3 1.0 copy.45
  13.3 0.8 reshape.73.wq_ref
  19.5 1.7 concatenate.9.pack_ref
  21.2 69.5 %front.1 = (bf16[4,8,80,1408]{3,2,1,0:T(8,128)(2,1)}, bf16[8,80,576]{2,1,0:T(8,128)(2,1)}, f32[4,1,640]{2,1,0:T(1,128)}, bf16[3,2048,256]{2,1,0:T(8,128)(2,1)}, ...) custom-call(bf16[2048,640]{1,0:T(8,128)(2,1)} %x_ref.3, ...), custom_call_target="tpu_custom_call" | custom-call | tf_op jit(solution)/shard_map/front/pallas_call | solution.py:252
  91.3 27.6 %middle.1 = (bf16[512,640]{1,0:T(8,128)(2,1)}, f32[512,640]{1,0:T(8,128)}, bf16[4,512,192]{2,1,0:T(8,128)(2,1)}, bf16[4,640,1408]{2,1,0:T(8,128)(2,1)}, f32[16,640]{1,0:T(8,128)}) custom-call(s32[1]{0:T(128)} %bitcast.at_ref, bf16[2048,640]{1,0:T(8,128)(2,1)} %x_ref.3, bf16[2048,640]{1,0:T(8,128)(2,1)} %y_ref.1, ...), custom_call_target="tpu_custom_call" | custom-call | tf_op jit(solution)/shard_map/middle/pallas_call | solution.py:509
  119.0 1.2 copy-done.3
  120.2 1.2 copy.47
  121.4 3.5 %all-to-all-start = ((bf16[4,512,192]{1,2,0:T(8,128)(2,1)}), bf16[4,512,192]{1,2,0:T(8,128)(2,1)S(1)}, u32[]{:S(2)}, u32[]{:S(2)}) async-start(bf16[4,512,192]{1,2,0:T(8,128)(2,1)} %copy.47), calls=%async_computation | async-start | bytes 1572864 | tf_op jit(solution)/shard_map/all_to_all | solution.py:579
  125.0 20.9 %all-to-all-done = bf16[4,512,192]{1,2,0:T(8,128)(2,1)S(1)} async-done(((bf16[4,512,192]{1,2,0:T(8,128)(2,1)}), bf16[4,512,192]{1,2,0:T(8,128)(2,1)S(1)}, u32[]{:S(2)}, u32[]{:S(2)}) %all-to-all-start) | async-done | bytes 786464 | tf_op jit(solution)/shard_map/all_to_all | solution.py:579
  147.1 0.9 copy.49
  147.9 1.3 multiply_bitcast_fusion.up_ref
  149.3 35.7 %attend_back.1 = (bf16[3,2048,64]{2,1,0:T(8,128)(2,1)}, bf16[3,2048,64]{2,1,0:T(8,128)(2,1)}, bf16[3,2048,64]{2,1,0:T(8,128)(2,1)}) custom-call(bf16[3,2048,256]{2,1,0:T(8,128)(2,1)} %get-tuple-element.35.qs_ref, bf16[3,2048,256]{2,1,0:T(8,128)(2,1)} %get-tuple-element.36.ka_ref, bf16[3,2048,128]{2,1,0:T(8,128)(2,1)} %get-tuple-element.37.va_ref, ...), custom_call_target="tpu_custom_call" | custom-call | tf_op jit(solution)/shard_map/attend_back/pallas_call | solution.py:383
  185.0 4.6 %convert_reduce_fusion = (f32[3,3,64]{2,1,0:T(4,128)S(1)}, bf16[2048,3,3,64]{3,0,2,1:T(8,128)(2,1)}) fusion(bf16[1,3,2048,64]{3,2,1,0:T(8,128)(2,1)} %bitcast.40, bf16[1,3,2048,64]{3,2,1,0:T(8,128)(2,1)} %bitcast.39, bf16[1,3,2048,64]{3,2,1,0:T(8,128)(2,1)} %bitcast.38), kind=kLoop, calls=%fused_computation | loop fusion | flops 4718016 | bytes 4720896 | tf_op jit(solution)/shard_map/reduce_sum | solution.py:587
  189.6 4.7 %copy.51 = bf16[2048,3,3,64]{0,3,2,1:T(8,128)(2,1)S(1)} copy(bf16[2048,3,3,64]{3,0,2,1:T(8,128)(2,1)} %get-tuple-element.97) | data formatting | bytes 4718592 | tf_op jit(solution)/shard_map/transpose | solution.py:586
  194.3 1.4 copy-done.1
  195.8 3.9 %convolution_convert_fusion = bf16[2048,640]{1,0:T(8,128)(2,1)} fusion(bf16[2048,576]{0,1:T(8,128)(2,1)S(1)} %bitcast.36, bf16[640,576]{1,0:T(8,128)(2,1)S(1)} %bitcast.49), kind=kOutput, calls=%fused_computation.2 | convolution fusion | flops 1511260160 | bytes 5718016 | tf_op jit(solution)/shard_map/rs,ds->rd/dot_general | solution.py:594
  200.4 1.0 copy-done
  201.4 3.7 %fusion = bf16[640,576]{0,1:T(8,128)(2,1)S(1)} fusion(bf16[2048,576]{0,1:T(8,128)(2,1)} %bitcast.37, bf16[2048,640]{1,0:T(8,128)(2,1)S(1)} %copy-done), kind=kOutput, calls=%fused_computation.7 | convolution fusion | flops 1510318080 | bytes 5718016 | tf_op jit(solution)/shard_map/rd,rs->ds/dot_general | solution.py:589
  205.1 1.2 copy.52
  206.4 3.7 %all-to-all-start.1 = ((bf16[8,80,576]{2,1,0:T(8,128)(2,1)}), bf16[8,80,576]{2,1,0:T(8,128)(2,1)S(1)}, u32[]{:S(2)}, u32[]{:S(2)}) async-start(bf16[8,80,576]{2,1,0:T(8,128)(2,1)} %bitcast.16), calls=%async_computation.2 | async-start | bytes 1638400 | tf_op jit(solution)/shard_map/all_to_all | solution.py:590
  210.1 46.1 %psum.15 = f32[16,640]{1,0:T(8,128)S(1)} all-reduce(f32[16,640]{1,0:T(8,128)S(1)} %copy-done.4), channel_id=1, replica_groups=mesh['dp'=8,'mp'=4] {'dp','mp'}, use_global_device_ids=true, to_apply=%region_6.7 | all-reduce | flops 10240 | bytes 81920 | tf_op jit(solution)/shard_map/psum | solution.py:583
  257.6 13.7 %psum.14 = f32[2,192]{1,0:T(2,128)} all-reduce(f32[2,192]{1,0:T(2,128)S(1)} %pad_maximum_fusion.1), channel_id=1, replica_groups=mesh['dp'=8,'mp'=4] {'dp'}, use_global_device_ids=true, to_apply=%region_3.4 | all-reduce | flops 384 | bytes 3072 | tf_op jit(solution)/shard_map/psum | solution.py:588
  271.6 0.7 copy.53
  272.4 2.0 add_convert_fusion
  274.4 2.7 reduce-scatter.8.cloned.1.call-done
  277.1 1.0 bitcast_convert_fusion
  278.2 0.8 slice_bitcast_fusion
  279.0 0.7 maximum_bitcast_fusion.1
  (44 shorter events, 10.6 us)
Async XLA Ops:
  7.2 192.8 %reduce-scatter.6.cloned.1.call-start = ((), (), s32[]{:S(2)}) async-start(), calls=%async_computation.6 | async-start | bytes 8110080 | tf_op jit(solution)/shard_map/reduce_scatter | solution.py:581
  118.9 1.2 copy-start.3
  121.4 24.5 %all-to-all-start = ((bf16[4,512,192]{1,2,0:T(8,128)(2,1)}), bf16[4,512,192]{1,2,0:T(8,128)(2,1)S(1)}, u32[]{:S(2)}, u32[]{:S(2)}) async-start(bf16[4,512,192]{1,2,0:T(8,128)(2,1)} %copy.47), calls=%async_computation | async-start | bytes 1572864 | tf_op jit(solution)/shard_map/all_to_all | solution.py:579
  124.9 147.4 %reduce-scatter.4.cloned.1.call-start = ((), (), s32[]{:S(2)}) async-start(), calls=%async_computation.5 | async-start | bytes 3276800 | tf_op jit(solution)/shard_map/reduce_scatter | solution.py:595
  189.6 6.1 %copy-start.5 = (bf16[8,80,576]{2,1,0:T(8,128)(2,1)S(1)}, bf16[8,80,576]{2,1,0:T(8,128)(2,1)}, u32[]{:S(2)}) copy-start(bf16[8,80,576]{2,1,0:T(8,128)(2,1)} %get-tuple-element.44) | copy-start | bytes 2211844
  194.3 1.4 copy-start.1
  199.7 1.7 copy-start
  199.7 77.4 %reduce-scatter.8.cloned.1.call-start = ((), (), s32[]{:S(2)}) async-start(), calls=%async_computation.7 | async-start | bytes 1126400 | tf_op jit(solution)/shard_map/reduce_scatter | solution.py:582
  205.1 4.9 %copy-start.4 = (f32[16,640]{1,0:T(8,128)S(1)}, f32[16,640]{1,0:T(8,128)}, u32[]{:S(2)}) copy-start(f32[16,640]{1,0:T(8,128)} %get-tuple-element.47) | copy-start | bytes 122884
  206.4 66.0 %copy-start.2 = (f32[512,640]{1,0:T(8,128)S(1)}, f32[512,640]{1,0:T(8,128)}, u32[]{:S(2)}) copy-start(f32[512,640]{1,0:T(8,128)} %get-tuple-element.45) | copy-start | bytes 3932164
  206.4 65.0 %all-to-all-start.1 = ((bf16[8,80,576]{2,1,0:T(8,128)(2,1)}), bf16[8,80,576]{2,1,0:T(8,128)(2,1)S(1)}, u32[]{:S(2)}, u32[]{:S(2)}) async-start(bf16[8,80,576]{2,1,0:T(8,128)(2,1)} %bitcast.16), calls=%async_computation.2 | async-start | bytes 1638400 | tf_op jit(solution)/shard_map/all_to_all | solution.py:590
Sparse Core Ops, SparseCore 0:
  119.1 63.5 reduce-scatter.5
  199.8 50.2 reduce-scatter.3
  252.4 24.6 reduce-scatter.7
where the time goes:
time: 287 us; the launch traced here: 286 us
  Pallas kernels  133 us (46%)
  blocking collectives  59.8 us (21%)
  local copies, waits for them, and re-layouts  30.6 us (11%)
  waiting for transfers between devices  24.1 us (8%)
  between operations  13.9 us (5%)
  other arithmetic  9.91 us (3%)
  matrix products  7.62 us (3%)
  starting transfers between devices  7.54 us (3%)
    pallas_call x1, Pallas kernels, front(): pl.pallas_call(functools.partial(front_kernel, slots, sub), in_specs=[vme...  69.5 us
    psum x1, blocking collectives, body(): small = lax.psum(small, ('dp', 'mp'))  46.1 us
    pallas_call x1, Pallas kernels, attend_back(): pl.pallas_call(functools.partial(attend_back_kernel, sub), grid=(slots, r...  35.7 us
    pallas_call x1, Pallas kernels, middle(): pl.pallas_call(functools.partial(middle_kernel, groups, hidden_cols, bloc...  27.6 us
    all_to_all x1, waiting for transfers between devices, body(): back = lax.all_to_all(back, 'mp', 0, 0, tiled=True)  20.9 us
    psum x1, blocking collectives, body(): lax.psum(jnp.stack([qkv_bias_grad[0], qkv_bias_grad[2]]), 'dp')  13.7 us
  transfers between devices with their start and end apart: 5, of which 2 were waited for; matrix products, arithmetic and copies ran while one was open for 10% of the time, Pallas kernels for 12%

commit v1 on v0

--- a/solution.py
+++ b/solution.py
@@ -89,15 +89,20 @@
     rows = x_ref.shape[0]
     share = rows // 4
 
-    mine = pltpu.make_async_copy(wq_ref, wfull_ref.at[dp], here.at[0])
+    piece = wq_ref.shape[0]
+
+    def rows_of(d):
+        return wfull_ref.at[pl.ds(pl.multiple_of(d * piece, piece), piece)]
+
+    mine = pltpu.make_async_copy(wq_ref, rows_of(dp), here.at[0])
     mine.start()
     firsts = [
-        remote(wq_ref, wfull_ref.at[dp], q_send.at[i], q_recv.at[i], (plane[i], mp))
+        remote(wq_ref, rows_of(dp), q_send.at[i], q_recv.at[i], (plane[i], mp))
         for i in range(CHIPS)
     ]
     for copy in firsts:
         copy.start()
-    shared = [remote(wq_ref, wfull_ref.at[dp], q_send.at[3], q_recv.at[3], sibling)]
+    shared = [remote(wq_ref, rows_of(dp), q_send.at[3], q_recv.at[3], sibling)]
     shared[0].start()
     own = pltpu.make_async_copy(pack_ref, all_ref.at[mp, dp], here.at[1])
     own.start()
@@ -116,7 +121,7 @@
     for i in range(CHIPS):
         firsts[i].wait_recv()
         passed = remote(
-            wfull_ref.at[plane[i]], wfull_ref.at[plane[i]], q_send.at[4 + i], q_recv.at[4 + i], sibling
+            rows_of(plane[i]), rows_of(plane[i]), q_send.at[4 + i], q_recv.at[4 + i], sibling
         )
         passed.start()
         shared.append(passed)
@@ -158,8 +163,7 @@
         part = pl.ds(pl.multiple_of(step * block, block), block)
         x = x_ref[part, :]
         made = off_ref[...] + jnp.zeros((block, off_ref.shape[1]), F32)
-        full = jnp.concatenate([wfull_ref[d] for d in range(wfull_ref.shape[0])], 0)
-        made = made + jnp.dot(x, full, preferred_element_type=F32)
+        made = made + jnp.dot(x, wfull_ref[...], preferred_element_type=F32)
         spread_rows(made.astype(BF16), seg_ref[part, :], slots, qs_ref, ka_ref, va_ref, kk_ref, part)
         return carry
 
@@ -255,7 +259,7 @@
         out_specs=[vmem] * 9,
         out_shape=[
             jax.ShapeDtypeStruct((4, 8, piece, lanes), BF16),
-            jax.ShapeDtypeStruct((8,) + wq.shape, BF16),
+            jax.ShapeDtypeStruct((8 * piece, wq.shape[1]), BF16),
             jax.ShapeDtypeStruct((4,) + up_bias.shape, F32),
             shape(AUG), shape(AUG), shape(VAUG), shape(HD),
             jax.ShapeDtypeStruct((slots, rows, HD), F32),
@@ -411,14 +415,30 @@
 
 
 def middle_kernel(
-    groups, hidden_cols, block, at_ref,
+    groups, hidden_cols, block, linked,
     x_ref, y_ref, got_ref, w_ref, ub_ref, vec_ref,
-    out_ref, s1_ref, back_ref, grad_ref, small_ref,
-    ow, act, pre_low, slope, hid_low, two_low, one_low,
+    out_ref, s1_ref, back_ref, grad_ref, small_ref, *scratch,
 ):
+    x_own, y_own, ow, act, pre_low, slope, hid_low, two_low, one_low, here = scratch[:10]
     share = out_ref.shape[0]
     width = got_ref.shape[2]
     gap = HALF - hidden_cols
+    dp = lax.axis_index("dp")
+    mp = lax.axis_index("mp")
+    rows = pl.ds(pl.multiple_of(mp * share, share), share)
+    loads = [
+        pltpu.make_async_copy(x_ref.at[rows], x_own, here.at[0]),
+        pltpu.make_async_copy(y_ref.at[rows], y_own, here.at[1]),
+    ]
+    for copy in loads:
+        copy.start()
+    if linked:
+        back_own, grads, arrived, b_send, b_recv, g_send, g_recv = scratch[10:]
+        core = lax.rem(dp, 2)
+        sibling = (dp ^ 1, mp)
+        plane_barrier([sibling] + [(dp, mp ^ s) for s in range(1, 4)])
+    else:
+        back_own, grads = back_ref, grad_ref
     out_bias, gain_one, shift_one = vec_ref[0:1, :], vec_ref[1:2, :], vec_ref[2:3, :]
     down_bias, gain_two, shift_two = vec_ref[3:4, :], vec_ref[4:5, :], vec_ref[5:6, :]
     for g in range(groups):
@@ -426,10 +446,22 @@
         ow[g, :, gap:] = w_ref[g, :, HALF + hidden_cols : HALF + hidden_cols + width - gap]
     small_ref[...] = jnp.zeros_like(small_ref)
     real = lane_marks(1, HALF, hidden_cols)
+    alive = [
+        lane_marks(1, width, HD * (HEADS // groups + (g < HEADS % groups))) for g in range(groups)
+    ]
+    for copy in loads:
+        copy.wait()
+
+    def send_back(step, s):
+        part = pl.ds(pl.multiple_of(step * block, block), block)
+        at = step * 3 + s - 1
+        return remote(
+            back_own.at[mp ^ s, part], back_ref.at[mp, part], b_send.at[at], b_recv.at[at], (dp, mp ^ s)
+        )
 
     def some_rows(step, carry):
         part = pl.ds(pl.multiple_of(step * block, block), block)
-        summed = x_ref[part, :].astype(F32) + out_bias
+        summed = x_own[part, :].astype(F32) + out_bias
         for g in range(groups):
             summed += lax.dot_general(got_ref[g, part, :], ow[g], NT, preferred_element_type=F32)
         normed_one, factor_one = norm_forward(summed)
@@ -449,7 +481,7 @@
             )
         normed_two, factor_two = norm_forward(feed)
         out_ref[part, :] = (normed_two * gain_two + shift_two).astype(BF16)
-        upstream = y_ref[part, :].astype(F32)
+        upstream = y_own[part, :].astype(F32)
         two_grad = norm_backward(upstream, normed_two, factor_two, gain_two)
         sum_two = two_grad.astype(BF16)
         two_low[part, :] = sum_two
@@ -469,7 +501,11 @@
         s1_ref[part, :] = one_grad
         one_low[part, :] = sum_one
         for g in range(groups):
-            back_ref[g, part, :] = jnp.dot(sum_one, ow[g], preferred_element_type=F32).astype(BF16)
+            made = jnp.dot(sum_one, ow[g], preferred_element_type=F32)
+            back_own[g, part, :] = jnp.where(alive[g], made, 0.0).astype(BF16)
+        if linked:
+            for s in range(1, 4):
+                send_back(step, s).start()
         for at, term in enumerate((
             sum_one.astype(F32), hidden_grad * normed_one, hidden_grad,
             sum_two.astype(F32), upstream * normed_two, upstream,
@@ -478,55 +514,413 @@
         return carry
 
     lax.fori_loop(0, share // block, some_rows, 0)
+    if linked:
+        keep = pltpu.make_async_copy(back_own.at[mp], back_ref.at[mp], here.at[2])
+        keep.start()
     hid_flip, two_flip, one_flip = hid_low[...].T, two_low[...].T, one_low[...].T
+    shared = []
     for g in range(groups):
-        grad_up = jnp.dot(hid_flip, pre_low[g], preferred_element_type=F32).astype(BF16)
-        grad_down = jnp.dot(two_flip, act[g], preferred_element_type=F32).astype(BF16)
+        made = jnp.dot(hid_flip, pre_low[g], preferred_element_type=F32).astype(BF16)
         grad_out = jnp.dot(one_flip, got_ref[g], preferred_element_type=F32).astype(BF16)
-        grad_ref[g, :, :HALF] = grad_up
-        grad_ref[g, :, HALF : 2 * HALF] = grad_down
-        grad_ref[g, :, hidden_cols:HALF] = grad_out[:, :gap]
         rest = width - gap
-        grad_ref[g, :, HALF + hidden_cols : HALF + hidden_cols + rest] = grad_out[:, gap:]
-        spare = grad_ref.shape[2] - HALF - hidden_cols - rest
-        grad_ref[g, :, HALF + hidden_cols + rest :] = jnp.zeros((grad_ref.shape[1], spare), BF16)
-
-
-def middle(frames, cotangent, got, weights, up_bias, vectors, mp_index, hidden_cols):
+        left = jnp.concatenate([made[:, :hidden_cols], grad_out[:, :gap]], 1)
+        made = jnp.dot(two_flip, act[g], preferred_element_type=F32).astype(BF16)
+        spare = w_ref.shape[2] - HALF - hidden_cols - rest
+        right = jnp.concatenate(
+            [made[:, :hidden_cols], grad_out[:, gap:], jnp.zeros((made.shape[0], spare), BF16)], 1
+        )
+        if linked:
+            piece = grads.shape[4 - 1]
+            for d in range(8):
+                at = slice(d * piece, (d + 1) * piece)
+                grads[g, d // 2, d % 2, :, :HALF] = left[at]
+                grads[g, d // 2, d % 2, :, HALF:] = right[at]
+            copy = remote(grads.at[g, :, 1 - core], arrived.at[g], g_send.at[g], g_recv.at[g], sibling)
+            copy.start()
+            shared.append(copy)
+        else:
+            grads[g, :, :HALF] = left
+            grads[g, :, HALF:] = right
+    if linked:
+        for g in range(groups):
+            shared[g].wait_recv()
+            for c in range(4):
+                grad_ref[g, c] = grads[g, c, core] + arrived[g, c]
+        for step in range(share // block):
+            for s in range(1, 4):
+                send_back(step, s).wait()
+        for copy in shared:
+            copy.wait_send()
+        keep.wait()
+
+
+def middle(frames, cotangent, got, weights, up_bias, vectors, hidden_cols, linked):
     groups, share, width = got.shape
     depth = frames.shape[1]
+    lanes = weights.shape[2]
     block = min(256, share)
-    whole = lambda a: pl.BlockSpec(a.shape, lambda i, at: (0,) * a.ndim)
-    pick = pl.BlockSpec((share, depth), lambda i, at: (at[0], 0))
-    same = lambda s: pl.BlockSpec(s.shape, lambda i, at: (0,) * len(s.shape))
-    out_shape = [
-        jax.ShapeDtypeStruct((share, depth), BF16),
-        jax.ShapeDtypeStruct((share, depth), F32),
-        jax.ShapeDtypeStruct((groups, share, width), BF16),
-        jax.ShapeDtypeStruct(weights.shape, BF16),
-        jax.ShapeDtypeStruct((16, HALF), F32),
+    vmem = pl.BlockSpec(memory_space=pltpu.VMEM)
+    rest = pl.BlockSpec(memory_space=pl.ANY)
+    dma = pltpu.SemaphoreType.DMA
+    scratch = [
+        pltpu.VMEM((share, depth), BF16),
+        pltpu.VMEM((share, depth), BF16),
+        pltpu.VMEM((groups, depth, width), BF16),
+        pltpu.VMEM((groups, share, HALF), BF16),
+        pltpu.VMEM((groups, share, HALF), BF16),
+        pltpu.VMEM((groups, block, HALF), F32),
+        pltpu.VMEM((share, depth), BF16),
+        pltpu.VMEM((share, depth), BF16),
+        pltpu.VMEM((share, depth), BF16),
+        dma((3,)),
     ]
+    grads = jax.ShapeDtypeStruct(weights.shape, BF16)
+    if linked:
+        piece = depth // 8
+        grads = jax.ShapeDtypeStruct((groups, 4, piece, lanes), BF16)
+        sends = 3 * (share // block)
+        scratch += [
+            pltpu.VMEM((groups, share, width), BF16),
+            pltpu.VMEM((groups, 4, 2, piece, lanes), BF16),
+            pltpu.VMEM((groups, 4, piece, lanes), BF16),
+            dma((sends,)), dma((sends,)), dma((groups,)), dma((groups,)),
+        ]
+    extra = dict(collective_id=2, has_side_effects=True) if linked else {}
     return pl.pallas_call(
-        functools.partial(middle_kernel, groups, hidden_cols, block),
-        grid_spec=pltpu.PrefetchScalarGridSpec(
-            num_scalar_prefetch=1,
-            grid=(1,),
-            in_specs=[pick, pick, whole(got), whole(weights), whole(up_bias), whole(vectors)],
-            out_specs=[same(s) for s in out_shape],
-            scratch_shapes=[
-                pltpu.VMEM((groups, depth, width), BF16),
-                pltpu.VMEM((groups, share, HALF), BF16),
-                pltpu.VMEM((groups, share, HALF), BF16),
-                pltpu.VMEM((groups, block, HALF), F32),
-                pltpu.VMEM((share, depth), BF16),
-                pltpu.VMEM((share, depth), BF16),
-                pltpu.VMEM((share, depth), BF16),
-            ],
+        functools.partial(middle_kernel, groups, hidden_cols, block, linked),
+        in_specs=[rest, rest, vmem, vmem, vmem, vmem],
+        out_specs=[vmem] * 5,
+        out_shape=[
+            jax.ShapeDtypeStruct((share, depth), BF16),
+            jax.ShapeDtypeStruct((share, depth), F32),
+            jax.ShapeDtypeStruct((groups, share, width), BF16),
+            grads,
+            jax.ShapeDtypeStruct((16, HALF), F32),
+        ],
+        scratch_shapes=scratch,
+        compiler_params=pltpu.CompilerParams(vmem_limit_bytes=VMEM_LIMIT, **extra),
+        name="middle",
+    )(frames, cotangent, got, weights, up_bias, vectors)
+
+
+PAIRS = (
+    (0, 3), (1, 3), (2, 3), (3, 3), (3, 2), (3, 1), (3, 0), (0, 2), (1, 2), (2, 2), (2, 1), (2, 0),
+    (0, 1), (1, 1), (1, 0), (0, 0),
+)
+ENDS = {6: 3, 11: 2, 14: 1, 15: 0}
+
+
+def pick(table, step):
+    made = jnp.int32(table[0])
+    for at in range(1, len(table)):
+        made = jnp.where(step >= at, jnp.int32(table[at]), made)
+    return made
+
+
+def back_kernel(
+    slots, sub,
+    qs_ref, ka_ref, va_ref, kk_ref, mixed_ref, up_ref, sums_ref, x_ref, wq_ref, one_ref, small_ref,
+    fg_ref, gq_ref, gb_ref, gw_ref, gs_ref,
+    upper, up_flip, q_flip, dq_acc, dk_acc, dv_acc, low, part_out, chain, fresh, far_in, near_in, third,
+    tall_in, gq_own, gq_in, gb_own, gb_in, tiny, tiny_in,
+    c_send, c_recv, f_send, f_recv, n_send, n_recv, t_send, t_recv, q_send, q_recv, b_send, b_recv,
+    s_send, s_recv,
+):
+    dp = lax.axis_index("dp")
+    mp = lax.axis_index("mp")
+    chip = dp // 2
+    rows, depth = x_ref.shape
+    share = rows // 4
+    width = slots * HD
+    others = [(dp ^ d, mp) for d in range(1, 8)]
+    tall = [(dp, mp ^ s) for s in range(1, 4)]
+    plane_barrier(others + tall)
+    x_peer, y_peer = (dp ^ 2, mp), (dp ^ 4, mp)
+
+    def rows_of(name):
+        return pl.ds(pl.multiple_of((mp ^ name) * share, share), share)
+
+    def far(s):
+        return remote(
+            sums_ref.at[mp ^ s, chip ^ 3], far_in.at[s], f_send.at[s], f_recv.at[s],
+            y_peer if s % 2 == 0 else x_peer,
+        )
+
+    def near(s, kind):
+        toward_x = (s % 2 == 0) == (kind == 1)
+        source = third.at[s] if kind == 1 else sums_ref.at[mp ^ s, chip ^ (1 if toward_x else 2)]
+        return remote(
+            source, near_in.at[s, kind], n_send.at[s, kind], n_recv.at[s, kind],
+            x_peer if toward_x else y_peer,
+        )
+
+    def lift(s):
+        return remote(
+            fresh.at[s], tall_in.at[s], t_send.at[s], t_recv.at[s], (dp, mp ^ s)
+        )
+
+    def begin_grads(s):
+        far(s).start()
+        near(s, 0).start()
+
+    def join_far(s):
+        far(s).wait_recv()
+        third[s] = sums_ref[mp ^ s, chip ^ (1 if s % 2 == 0 else 2)] + far_in[s]
+        near(s, 1).start()
+
+    def join_near(s):
+        near(s, 0).wait_recv()
+        near(s, 1).wait_recv()
+        total = sums_ref[mp ^ s, chip].astype(F32) + near_in[s, 0].astype(F32)
+        fresh[s] = (total + near_in[s, 1].astype(F32)).astype(BF16)
+        if s > 0:
+            lift(s).start()
+
+    partners = [(dp ^ 1, mp), (dp ^ 2, mp), (dp ^ 4, mp), (dp, mp ^ 1), (dp, mp ^ 2)]
+
+    def swap(at):
+        return remote(tiny.at[at], tiny_in.at[at], s_send.at[at], s_recv.at[at], partners[at])
+
+    def small_step(at):
+        if at == 0:
+            tiny[0] = small_ref[...]
+        else:
+            swap(at - 1).wait_recv()
+            made = tiny[at - 1] + tiny_in[at - 1]
+            if at == len(partners):
+                gs_ref[...] = made
+                return
+            tiny[at] = made
+        swap(at).start()
+
+    def chain_copy(name, leftward):
+        block = mp ^ name
+        target = mp - 1 if leftward else mp + 1
+        slot = jnp.where(block == target, 4, block) if leftward else block
+        return remote(
+            part_out.at[name], chain.at[slot], c_send.at[name], c_recv.at[slot], (dp, target)
+        )
+
+    def chain_arrival(slot):
+        return remote(part_out.at[0], chain.at[slot], c_send.at[0], c_recv.at[slot], (dp, mp ^ 1))
+
+    def relay(name):
+        block = mp ^ name
+        inner = (mp == 1) | (mp == 2)
+        waits = inner
+
+        @pl.when(waits)
+        def _():
+            chain_arrival(block).wait_recv()
+            part_out[name] = (
+                part_out[name].astype(F32) + chain[block].astype(F32)
+            ).astype(BF16)
+
+        @pl.when(block < mp)
+        def _():
+            chain_copy(name, True).start()
+
+        @pl.when(block > mp)
+        def _():
+            chain_copy(name, False).start()
+
+    def finish(name):
+        at = rows_of(name)
+        for slot in range(slots):
+            col = slot * HD
+            low[at, col : col + HD] = (dq_acc[slot, at, :] * SCALE).astype(BF16)
+            low[at, width + col : width + col + HD] = (dk_acc[slot, :, at] * SCALE).T.astype(BF16)
+            low[at, 2 * width + col : 2 * width + col + HD] = dv_acc[slot, :, at].T.astype(BF16)
+        part_out[name] = lax.dot_general(
+            low[at, :], wq_ref[...], NT, preferred_element_type=F32
+        ).astype(BF16)
+
+    dq_acc[...] = jnp.zeros_like(dq_acc)
+    dk_acc[...] = jnp.zeros_like(dk_acc)
+    dv_acc[...] = jnp.zeros_like(dv_acc)
+    begin_grads(3)
+    begin_grads(2)
+    small_step(0)
+
+    def prepare(step, carry):
+        at = pl.ds(pl.multiple_of(step * share, share), share)
+        for slot in range(slots):
+            up = up_ref[step, :, slot * HD : (slot + 1) * HD]
+            one, two, three = thirds(
+                jnp.sum(up.astype(F32) * mixed_ref[slot, at, :], -1, keepdims=True)
+            )
+            blank = jnp.zeros((share, VAUG - HD - 3), BF16)
+            upper[slot, at, :] = jnp.concatenate([up, one, two, three, blank], 1)
+            up_flip[slot, :, at] = up.T
+            q_flip[slot, :, at] = qs_ref[slot, at, :HD].T
+        return carry
+
+    lax.fori_loop(0, 4, prepare, 0)
+    actions = {
+        1: [(small_step, 1)],
+        2: [(begin_grads, 1), (small_step, 2)],
+        3: [(join_far, 3), (small_step, 3)],
+        4: [(begin_grads, 0), (small_step, 4)],
+        5: [(join_far, 2)],
+        6: [(small_step, 5)],
+        7: [(join_far, 1), (join_near, 3)],
+        9: [(join_far, 0), (join_near, 2)],
+        12: [(join_near, 1)],
+        14: [(join_near, 0)],
+    }
+
+    def pair(step, carry):
+        query = mp ^ pick([p[0] for p in PAIRS], step)
+        key = mp ^ pick([p[1] for p in PAIRS], step)
+        keys = pl.ds(pl.multiple_of(key * share, share), share)
+        for when, todo in actions.items():
+
+            @pl.when(step == when)
+            def _():
+                for act, s in todo:
+                    act(s)
+
+        for at in range(0, share, sub):
+            part = pl.ds(pl.multiple_of(query * share + at, sub), sub)
+            for slot in range(slots):
+                x = lax.dot_general(
+                    qs_ref[slot, part, :], ka_ref[slot, keys, :], NT, preferred_element_type=F32
+                )
+                p = jnp.exp2(x)
+                dp_ = lax.dot_general(
+                    upper[slot, part, :], va_ref[slot, keys, :], NT, preferred_element_type=F32
+                )
+                ds = (p * dp_).astype(BF16)
+                dv_acc[slot, :, keys] += jnp.dot(
+                    up_flip[slot, :, part], p.astype(BF16), preferred_element_type=F32
+                )
+                dk_acc[slot, :, keys] += jnp.dot(
+                    q_flip[slot, :, part], ds, preferred_element_type=F32
+                )
+                dq_acc[slot, part, :] += jnp.dot(
+                    ds, kk_ref[slot, keys, :], preferred_element_type=F32
+                )
+        for when, name in ENDS.items():
+
+            @pl.when(step == when)
+            def _():
+                finish(name)
+                if name > 0:
+
+                    @pl.when((mp == 0) | (mp == 3))
+                    def _():
+                        relay(name)
+
+        return carry
+
+    lax.fori_loop(0, len(PAIRS), pair, 0)
+    for name in (2, 3, 1):
+
+        @pl.when((mp == 1) | (mp == 2))
+        def _():
+            relay(name)
+
+    gq_parts = low[...]
+    ones = jnp.ones((16, rows), BF16)
+    gb_own[...] = jnp.dot(ones, gq_parts, preferred_element_type=F32)[0:8, :]
+    gb_in[dp] = gb_own[...]
+    piece = depth // 8
+    made = lax.dot_general(x_ref[...], gq_parts, TN, preferred_element_type=F32).astype(BF16)
+    for d in range(8):
+        gq_own[d] = made[d * piece : (d + 1) * piece]
+    q_copies = []
+    for d in range(1, 8):
+        to = dp ^ d
+        q_copies.append(
+            remote(gq_own.at[to], gq_in.at[d - 1], q_send.at[d - 1], q_recv.at[d - 1], others[d - 1])
+        )
+        q_copies.append(
+            remote(gb_own, gb_in.at[dp], b_send.at[d - 1], b_recv.at[d - 1], others[d - 1])
+        )
+    for copy in q_copies:
+        copy.start()
+    for s in range(1, 4):
+        lift(s).wait_recv()
+    total = fresh[0].astype(F32)
+    for s in range(1, 4):
+        total = total + tall_in[s].astype(F32)
+    gw_ref[...] = total
+    for copy in q_copies:
+        copy.wait_recv()
+    total = gq_own[dp].astype(F32)
+    for d in range(7):
+        total = total + gq_in[d].astype(F32)
+    gq_ref[...] = total
+    total = gb_in[0]
+    for d in range(1, 8):
+        total = total + gb_in[d]
+    gb_ref[...] = total
+
+    wide = one_ref[...] + part_out[0].astype(F32)
+
+    @pl.when(mp > 0)
+    def _():
+        chain_arrival(mp).wait_recv()
+
+    @pl.when(mp < 3)
+    def _():
+        chain_arrival(4).wait_recv()
+
+    left = jnp.where(mp > 0, chain[mp].astype(F32), 0.0)
+    right = jnp.where(mp < 3, chain[4].astype(F32), 0.0)
+    fg_ref[...] = (wide + left + right).astype(BF16)
+    for name in (1, 2, 3):
+        remote(
+            part_out.at[name], chain.at[0], c_send.at[name], c_recv.at[0], (dp, mp ^ 1)
+        ).wait_send()
+    for s in range(4):
+        far(s).wait_send()
+        near(s, 0).wait_send()
+        near(s, 1).wait_send()
+        if s > 0:
+            lift(s).wait_send()
+    for at in range(len(partners)):
+        swap(at).wait_send()
+    for copy in q_copies:
+        copy.wait_send()
+
+
+def back_pass(qs, ka, va, kk, mixed, up, sums, frames, wq, one_grad, small):
+    slots, rows, _ = qs.shape
+    depth = frames.shape[1]
+    share = rows // 4
+    piece, lanes = sums.shape[2:]
+    cols = wq.shape[1]
+    vmem = pl.BlockSpec(memory_space=pltpu.VMEM)
+    dma = pltpu.SemaphoreType.DMA
+    V = pltpu.VMEM
+    return pl.pallas_call(
+        functools.partial(back_kernel, slots, min(256, share)),
+        in_specs=[vmem] * 11,
+        out_specs=[vmem] * 5,
+        out_shape=[
+            jax.ShapeDtypeStruct((share, depth), BF16),
+            jax.ShapeDtypeStruct((piece, cols), F32),
+            jax.ShapeDtypeStruct((8, cols), F32),
+            jax.ShapeDtypeStruct((piece, lanes), F32),
+            jax.ShapeDtypeStruct(small.shape, F32),
+        ],
+        scratch_shapes=[
+            V((slots, rows, VAUG), BF16), V((slots, HD, rows), BF16), V((slots, HD, rows), BF16),
+            V((slots, rows, HD), F32), V((slots, HD, rows), F32), V((slots, HD, rows), F32),
+            V((rows, cols), BF16), V((4, share, depth), BF16), V((5, share, depth), BF16),
+            V((4, piece, lanes), BF16), V((4, piece, lanes), BF16), V((4, 2, piece, lanes), BF16),
+            V((4, piece, lanes), BF16), V((4, piece, lanes), BF16),
+            V((8, piece, cols), BF16), V((7, piece, cols), BF16),
+            V((8, cols), F32), V((8, 8, cols), F32), V((5,) + small.shape, F32), V((5,) + small.shape, F32),
+            dma((4,)), dma((5,)), dma((4,)), dma((4,)), dma((4, 2)), dma((4, 2)), dma((4,)), dma((4,)),
+            dma((7,)), dma((7,)), dma((7,)), dma((7,)), dma((5,)), dma((5,)),
+        ],
+        compiler_params=pltpu.CompilerParams(
+            collective_id=3, has_side_effects=True, vmem_limit_bytes=60 << 20
         ),
-        out_shape=out_shape,
-        compiler_params=pltpu.CompilerParams(vmem_limit_bytes=VMEM_LIMIT),
-        name="middle",
-    )(mp_index.reshape(1), frames, cotangent, got, weights, up_bias, vectors)
+        name="back_pass",
+    )(qs, ka, va, kk, mixed, up, sums, frames, wq, one_grad, small)
 
 
 def body(
@@ -554,12 +948,12 @@
     )
     ub_pad = jnp.pad(up_bias, (0, gap))[None]
     offsets = jnp.concatenate([qkv_bias[0], jnp.zeros_like(qkv_bias[0]), qkv_bias[1]])[None]
-    if (dp_size, mp_size) == (8, 4):
+    linked = (dp_size, mp_size) == (8, 4)
+    if linked:
         weights, qkv_full, ub_full, qs, ka, va, kk, mixed, got = front(
             frames, wq, packed, ub_pad, offsets, seg_ids, slots
         )
         weights = weights.reshape(mp_size, depth, -1)
-        qkv_full = qkv_full.reshape(depth, -1)
     else:
         qkv_full = lax.all_gather(wq, "dp", axis=0, tiled=True)
         weights = lax.all_gather(packed, "mp", axis=0, tiled=False)
@@ -574,26 +968,33 @@
         [out_bias, gain_one, shift_one, down_bias, gain_two, shift_two, out_bias, out_bias]
     )
     output_frames, sum_one_grad, back, partial, small = middle(
-        frames, cotangent, got, weights, ub_full, vectors, mp_index, hidden_cols
+        frames, cotangent, got, weights, ub_full, vectors, hidden_cols, linked
     )
-    back = lax.all_to_all(back, "mp", 0, 0, tiled=True)
-    back = back.reshape(rows, slots, HD).transpose(1, 0, 2) * live.astype(BF16)[:, None, None]
-    partial = lax.psum_scatter(partial, "dp", scatter_dimension=1, tiled=True)
-    partial = lax.psum_scatter(partial, "mp", scatter_dimension=0, tiled=True)[0].astype(F32)
-    small = lax.psum(small, ("dp", "mp"))
-
-    dq, dk, dv = attend_back(qs, ka, va, kk, mixed, back)
-    grads_low = jnp.stack([dq, dk, dv]).transpose(2, 0, 1, 3).reshape(rows, 3 * width)
-    qkv_bias_grad = jnp.sum(grads_low.astype(F32), 0).reshape(3, width)
-    qkv_bias_grad = lax.psum(jnp.stack([qkv_bias_grad[0], qkv_bias_grad[2]]), "dp")
-    grad_qkv = jnp.einsum("rd,rs->ds", frames, grads_low, preferred_element_type=F32)
-    arrived = lax.all_to_all(
-        grad_qkv.astype(BF16).reshape(dp_size, piece, 3 * width), "dp", 0, 0, tiled=True
-    )
-    grad_qkv = arrived.astype(F32).sum(0).reshape(piece, 3, width).transpose(1, 0, 2)
-    input_part = jnp.einsum("rs,ds->rd", grads_low, qkv_full, preferred_element_type=F32)
-    input_sum = lax.psum_scatter(input_part.astype(BF16), "mp", scatter_dimension=0, tiled=True)
-    frames_grad = (input_sum.astype(F32) + sum_one_grad).astype(BF16)
+    if linked:
+        frames_grad, grad_qkv, bias_sums, partial, small = back_pass(
+            qs, ka, va, kk, mixed, back, partial, frames, qkv_full, sum_one_grad, small
+        )
+        bias_sums = bias_sums[0]
+    else:
+        back = lax.all_to_all(back, "mp", 0, 0, tiled=True)
+        back = back.reshape(rows, slots, HD).transpose(1, 0, 2)
+        partial = lax.psum_scatter(partial, "dp", scatter_dimension=1, tiled=True)
+        partial = lax.psum_scatter(partial, "mp", scatter_dimension=0, tiled=True)[0].astype(F32)
+        small = lax.psum(small, ("dp", "mp"))
+        dq, dk, dv = attend_back(qs, ka, va, kk, mixed, back)
+        grads_low = jnp.stack([dq, dk, dv]).transpose(2, 0, 1, 3).reshape(rows, 3 * width)
+        bias_sums = lax.psum(jnp.sum(grads_low.astype(F32), 0), "dp")
+        grad_qkv = jnp.einsum("rd,rs->ds", frames, grads_low, preferred_element_type=F32)
+        arrived = lax.all_to_all(
+            grad_qkv.astype(BF16).reshape(dp_size, piece, 3 * width), "dp", 0, 0, tiled=True
+        )
+        grad_qkv = arrived.astype(F32).sum(0)
+        input_part = jnp.einsum("rs,ds->rd", grads_low, qkv_full, preferred_element_type=F32)
+        input_sum = lax.psum_scatter(input_part.astype(BF16), "mp", scatter_dimension=0, tiled=True)
+        frames_grad = (input_sum.astype(F32) + sum_one_grad).astype(BF16)
+    grad_qkv = grad_qkv.reshape(piece, 3, width).transpose(1, 0, 2)
+    bias_sums = bias_sums.reshape(3, width)
+    qkv_bias_grad = jnp.stack([bias_sums[0], bias_sums[2]])
     out_grad = jnp.concatenate(
         [partial[:, hidden_cols:HALF], partial[:, HALF + hidden_cols : HALF + hidden_cols + width - gap]], 1
     )

time: 287 us -> 229 us (0.80)
  Pallas kernels: 133 us -> 204 us
  blocking collectives: 59.8 us -> 0 us
  waiting for transfers between devices: 24.1 us -> 0 us
  between operations: 13.9 us -> 0.85 us
  local copies, waits for them, and re-layouts: 30.6 us -> 21.5 us
  other arithmetic: 9.91 us -> 1.4 us
  matrix products: 7.62 us -> 0 us
  starting transfers between devices: 7.54 us -> 0 us
    pallas_call x1, Pallas kernels: 35.7 us -> 95.8 us  [back_pass(): pl.pallas_call(functools.partial(back_kernel, slots, min(256, share)), in...]
    psum x2 -> x0, blocking collectives: 59.8 us -> none  [the longest x1 46.1 us: body(): small = lax.psum(small, ('dp', 'mp'))]
    all_to_all x2 -> x0, waiting for transfers between devices: 20.9 us -> none  [the longest x1 20.9 us: body(): back = lax.all_to_all(back, 'mp', 0, 0, tiled=True)]
    pallas_call x1, Pallas kernels: 27.6 us -> 38.7 us  [middle(): pl.pallas_call(functools.partial(middle_kernel, groups, hidden_cols, bloc...]
    dot_general x2 -> x0, matrix products: 7.62 us -> none  [the longest x1 3.9 us: body(): jnp.einsum('rs,ds->rd', grads_low, qkv_full, preferred_element_type=F32)]
    all_to_all x2 -> x0, starting transfers between devices: 7.2 us -> none  [the longest x1 3.68 us: body(): lax.all_to_all(grad_qkv.astype(BF16).reshape(dp_size, piece, 3 * width),...]
    reduce_sum x2 -> x0, other arithmetic: 4.76 us -> none  [the longest x1 4.65 us: body(): qkv_bias_grad = jnp.sum(grads_low.astype(F32), 0).reshape(3, width)]
    transpose x1 -> x0, local copies, waits for them, and re-layouts: 4.68 us -> none  [body(): jnp.stack([dq, dk, dv]).transpose(2, 0, 1, 3).reshape(rows, 3 * width)]
  transfers between devices with their start and end apart: 5 -> 0, of which waited for: 2 -> 0; matrix products, arithmetic and copies ran while one was open for 10% -> 0% of each run, Pallas kernels for 12% -> 0%
where the time goes in v1:
time: 229 us; the launch traced here: 228 us
  Pallas kernels  204 us (89%)
  local copies, waits for them, and re-layouts  21.5 us (9%)
    pallas_call x1, Pallas kernels, back_pass(): pl.pallas_call(functools.partial(back_kernel, slots, min(256, share)), in...  95.8 us
    pallas_call x1, Pallas kernels, front(): pl.pallas_call(functools.partial(front_kernel, slots, sub), in_specs=[vme...  69.8 us
    pallas_call x1, Pallas kernels, middle(): pl.pallas_call(functools.partial(middle_kernel, groups, hidden_cols, bloc...  38.7 us

profile of v1, /device:TPU:0, one launch (start us, length us, event | category | flops | bytes accessed | tf_op | source)
XLA Modules:
  0.0 228.0 jit_solution(14639000731919253544)
XLA Ops:
  0.7 0.8 slice.77
  1.5 0.9 slice.78
  2.3 1.7 concatenate.9.pack_ref
  4.1 0.8 fusion.1
  4.8 0.1 pad_maximum_fusion
  4.9 0.6 broadcast_in_dim.15.off_ref
  5.5 2.0 copy.32.seg_ref
  7.5 1.0 copy.31
  8.5 0.8 reshape.43.wq_ref
  9.3 0.7 pad.4
  10.0 0.6 broadcast_in_dim.13.bias_ref
  10.6 69.8 %front.1 = (bf16[4,8,80,1408]{3,2,1,0:T(8,128)(2,1)}, bf16[640,576]{1,0:T(8,128)(2,1)}, f32[4,1,640]{2,1,0:T(1,128)}, bf16[3,2048,256]{2,1,0:T(8,128)(2,1)}, bf1...) custom-call(bf16[2048,640]{1,0:T(8,128)(2,1)} %x_ref.5, ...), custom_call_target="tpu_custom_call" | custom-call | tf_op jit(solution)/shard_map/front/pallas_call | solution.py:256
  80.4 0.0 copy-done.2
  80.4 0.0 copy-done.3
  80.4 0.0 copy-done.4
  80.5 0.0 copy-done.5
  80.5 0.0 copy-done.6
  80.5 0.6 stack.32.vec_ref
  81.2 38.7 %middle.1 = (bf16[512,640]{1,0:T(8,128)(2,1)}, f32[512,640]{1,0:T(8,128)}, bf16[4,512,192]{2,1,0:T(8,128)(2,1)}, bf16[4,4,80,1408]{3,2,1,0:T(8,128)(2,1)}, f32[16,640]{1,0:T(8,128)}) custom-call(bf16[2048,640]{1,0:T(8,128)(2,1)} %x_ref.5, bf16[2048,640]{1,0:T(8,128)(2,1)} %y_ref.1, bf16[4,512,192]{2,1,0:T(8,128)(2,1)} %get-tuple-element.33.got_ref, ...), custom_call_target="tpu_custom_call" | custom-call | tf_op jit(solution)/shard_map/middle/pallas_call | solution.py:589
  119.9 95.8 %back_pass.1 = (bf16[512,640]{1,0:T(8,128)(2,1)}, f32[80,576]{1,0:T(8,128)}, f32[8,576]{1,0:T(8,128)}, f32[80,1408]{1,0:T(8,128)}, f32[16,640]{1,0:T(8,128)}) custom-call(bf16[3,2048,256]{2,1,0:T(8,128)(2,1)} %get-tuple-element.37.qs_ref, bf16[3,2048,256]{2,1,0:T(8,128)(2,1)} %get-tuple-element.38.ka_ref, bf16[3,2048,128]{2,1,0:T(8,128)(2,1)} %get-tuple-element.39.va_ref, ...), custom_call_target="tpu_custom_call" | custom-call | tf_op jit(solution)/shard_map/back_pass/pallas_call | solution.py:897
  215.7 0.9 slice.65
  216.6 1.0 slice.66
  217.6 0.7 maximum_bitcast_fusion
  218.3 0.7 fusion
  219.0 0.6 pad_maximum_fusion.1
  219.6 1.1 reshape.46
  220.7 0.7 copy.33
  221.4 1.8 slice_bitcast_fusion
  223.2 1.7 slice_reduce_fusion
  225.0 1.3 dynamic-slice_reduce_fusion
  226.3 0.8 copy.36
  227.2 0.8 copy.37
  (19 shorter events, 0.1 us)
Async XLA Ops:
  0.6 79.8 %copy-start.2 = (f32[640]{0:T(1024)S(1)}, f32[640]{0:T(1024)}, u32[]{:S(2)}) copy-start(f32[640]{0:T(1024)} %param.20) | copy-start | bytes 7684
  0.7 79.8 %copy-start.3 = (f32[640]{0:T(1024)S(1)}, f32[640]{0:T(1024)}, u32[]{:S(2)}) copy-start(f32[640]{0:T(1024)} %param.21) | copy-start | bytes 7684
  0.7 79.8 %copy-start.4 = (f32[640]{0:T(1024)S(1)}, f32[640]{0:T(1024)}, u32[]{:S(2)}) copy-start(f32[640]{0:T(1024)} %param.22) | copy-start | bytes 7684
  0.7 79.8 %copy-start.5 = (f32[640]{0:T(1024)S(1)}, f32[640]{0:T(1024)}, u32[]{:S(2)}) copy-start(f32[640]{0:T(1024)} %param.26) | copy-start | bytes 7684
  0.7 79.8 %copy-start.6 = (f32[640]{0:T(1024)S(1)}, f32[640]{0:T(1024)}, u32[]{:S(2)}) copy-start(f32[640]{0:T(1024)} %param.27) | copy-start | bytes 7684
  0.7 79.8 %copy-start.7 = (f32[640]{0:T(1024)S(1)}, f32[640]{0:T(1024)}, u32[]{:S(2)}) copy-start(f32[640]{0:T(1024)} %param.28) | copy-start | bytes 7684
  119.9 106.4 %copy-start = (bf16[512,640]{1,0:T(8,128)(2,1)S(1)}, bf16[512,640]{1,0:T(8,128)(2,1)}, u32[]{:S(2)}) copy-start(bf16[512,640]{1,0:T(8,128)(2,1)} %get-tuple-element.92) | copy-start | bytes 1966084
  215.7 11.5 %copy-start.1 = (bf16[512,640]{1,0:T(8,128)(2,1)S(1)}, bf16[512,640]{1,0:T(8,128)(2,1)}, u32[]{:S(2)}) copy-start(bf16[512,640]{1,0:T(8,128)(2,1)} %get-tuple-element.93) | copy-start | bytes 1966084

commit v2 on v1

--- a/solution.py
+++ b/solution.py
@@ -39,12 +39,11 @@
     return lax.broadcasted_iota(jnp.int32, (rows, width), 1) < count
 
 
-def spread_rows(made, seg, slots, qs_ref, ka_ref, va_ref, kk_ref, rows):
+def spread_rows(made, picked, slots, qs_ref, ka_ref, va_ref, kk_ref, rows):
     count = made.shape[0]
     width = slots * HD
-    marks = seg == lax.broadcasted_iota(jnp.int32, (count, MAX_SEGS), 1)
-    chosen = jnp.where(marks, 1.0, 0.0).astype(BF16)
-    barred = jnp.where(marks, 0.0, MASKED).astype(BF16)
+    chosen = picked.astype(BF16)
+    barred = ((picked - 1.0) * -MASKED).astype(BF16)
     tail = AUG - 3 * HD - MAX_SEGS
     q_tail = jnp.zeros((count, tail), BF16)
     minus = jnp.where(lane_marks(count, tail, 3), -1.0, 0.0).astype(BF16)
@@ -74,17 +73,48 @@
     )
 
 
+def pack_rows(wide):
+    half = wide.shape[0] // 2
+    third = wide[:, 2 * HD :]
+    return jnp.concatenate(
+        [wide[:, : 2 * HD], jnp.concatenate([third[:half], third[half:]], 1)], 0
+    )
+
+
+def unpack_rows(packed):
+    rows = packed.shape[0] * 2 // 3
+    rest = packed[rows:]
+    return jnp.concatenate(
+        [packed[:rows], jnp.concatenate([rest[:, :HD], rest[:, HD:]], 0)], 1
+    )
+
+
 def front_kernel(
     slots, sub,
-    x_ref, wq_ref, pack_ref, bias_ref, off_ref, seg_ref,
+    x_ref, qkv_ref, up_ref, down_ref, out_ref, vec_ref, seg_ref,
     all_ref, wfull_ref, ball_ref, qs_ref, ka_ref, va_ref, kk_ref, mixed_ref, got_ref,
-    stage, q_send, q_recv, z_send, z_recv, w_send, w_recv, b_send, b_recv, a_send, a_recv, here,
+    stage, wq_ref, pack_ref, bias_ref,
+    q_send, q_recv, z_send, z_recv, w_send, w_recv, b_send, b_recv, a_send, a_recv, here,
 ):
     dp = lax.axis_index("dp")
     mp = lax.axis_index("mp")
     plane = [dp ^ 2, dp ^ 4, dp ^ 6]
     sibling = (dp ^ 1, mp)
     tall = [(dp, mp ^ s) for s in range(1, 4)]
+    inner = (mp == 1) | (mp == 2)
+    width = slots * HD
+    for i in range(3):
+        wq_ref[:, i * width : (i + 1) * width] = qkv_ref[i]
+    hidden_cols = up_ref.shape[1]
+    gap = HALF - hidden_cols
+    rest = width - gap
+    pack_ref[:, :hidden_cols] = up_ref[...]
+    pack_ref[:, hidden_cols:HALF] = out_ref[:, :gap]
+    pack_ref[:, HALF : HALF + hidden_cols] = down_ref[...]
+    pack_ref[:, HALF + hidden_cols : HALF + hidden_cols + rest] = out_ref[:, gap:]
+    spare = pack_ref.shape[1] - HALF - hidden_cols - rest
+    pack_ref[:, HALF + hidden_cols + rest :] = jnp.zeros((pack_ref.shape[0], spare), BF16)
+    bias_ref[...] = vec_ref[6:7, :]
     plane_barrier([sibling] + [(d, mp) for d in plane] + tall)
     rows = x_ref.shape[0]
     share = rows // 4
@@ -106,13 +136,27 @@
     shared[0].start()
     own = pltpu.make_async_copy(pack_ref, all_ref.at[mp, dp], here.at[1])
     own.start()
-    lifts = [
-        remote(pack_ref, all_ref.at[mp, dp], z_send.at[s], z_recv.at[s], tall[s]) for s in range(3)
+    def lift(at, s, landing, peer):
+        ref = all_ref.at[mp ^ s, dp]
+        return remote(pack_ref if s == 0 else ref, ref, z_send.at[at], z_recv.at[landing], peer)
+
+    near, middle = tall[0], tall[2]
+    lifts = [lift(0, 0, 1, near)]
+    inner_lifts = [
+        lift(1, 0, 3, middle), lift(2, 1, 2, middle), lift(3, 3, 2, near), lift(4, 2, 3, near),
     ]
+
+    def arrive(s):
+        lift(0, s, s, near).wait_recv()
+
     own_bias = pltpu.make_async_copy(bias_ref, ball_ref.at[mp], here.at[2])
     own_bias.start()
-    for copy in lifts:
-        copy.start()
+    lifts[0].start()
+
+    @pl.when(inner)
+    def _():
+        inner_lifts[0].start()
+
     biases = [
         remote(bias_ref, ball_ref.at[mp], b_send.at[s], b_recv.at[s], tall[s]) for s in range(3)
     ]
@@ -137,8 +181,12 @@
         return remote(ref, ref, w_send.at[s, kind], w_recv.at[s, kind], peer.get(kind, sibling))
 
     def start_weights(s):
-        if s > 0:
-            lifts[s - 1].wait_recv()
+        if s == 3:
+
+            @pl.when(~inner)
+            def _():
+                arrive(3)
+
         for kind in (0, 1, 2):
             weights(s, kind).start()
 
@@ -156,23 +204,42 @@
     mine.wait()
     for copy in shared:
         copy.wait_recv()
+    arrive(1)
+
+    @pl.when(inner)
+    def _():
+        inner_lifts[1].start()
+        arrive(3)
+        inner_lifts[2].start()
+
 
     block = 256
 
     def project_rows(step, carry):
         part = pl.ds(pl.multiple_of(step * block, block), block)
         x = x_ref[part, :]
-        made = off_ref[...] + jnp.zeros((block, off_ref.shape[1]), F32)
-        made = made + jnp.dot(x, wfull_ref[...], preferred_element_type=F32)
-        spread_rows(made.astype(BF16), seg_ref[part, :], slots, qs_ref, ka_ref, va_ref, kk_ref, part)
+        offsets = jnp.concatenate(
+            [vec_ref[7:8, :width], jnp.zeros((1, width), F32), vec_ref[8:9, :width]], 1
+        )
+        made = jnp.dot(x, wfull_ref[...], preferred_element_type=F32) + offsets
+        marks = seg_ref[:, part] == lax.broadcasted_iota(jnp.int32, (MAX_SEGS, block), 0)
+        picked = jnp.where(marks, 1.0, 0.0).T
+        spread_rows(made.astype(BF16), picked, slots, qs_ref, ka_ref, va_ref, kk_ref, part)
         return carry
 
     lax.fori_loop(0, rows // block, project_rows, 0)
+    arrive(2)
+
+    @pl.when(inner)
+    def _():
+        inner_lifts[3].start()
+
+    pass_weights(0)
+    start_weights(1)
 
     live_count = HEADS // 4 + (mp < HEADS % 4).astype(jnp.int32)
     per_share = share // sub
     actions = {
-        0: [(start_weights, 1), (pass_weights, 0)],
         1: [(start_weights, 2), (last_weights, 0)],
         2: [(pass_weights, 1)],
         3: [(start_weights, 3), (last_weights, 1)],
@@ -182,12 +249,9 @@
     }
 
     def send_rows(step, stage_index):
-        group = mp ^ stage_index
-        offset = pl.multiple_of(lax.rem(step, per_share) * sub, sub)
-        source = pl.ds(pl.multiple_of(group * share, share) + offset, sub)
         return remote(
-            stage.at[source], got_ref.at[mp, pl.ds(offset, sub)], a_send.at[step], a_recv.at[step],
-            (dp, group),
+            stage.at[step], got_ref.at[mp, lax.rem(step, per_share)], a_send.at[step], a_recv.at[step],
+            (dp, mp ^ stage_index),
         )
 
     def attend_rows(step, carry):
@@ -202,6 +266,7 @@
                 for act, s in todo:
                     act(s)
 
+        kept = []
         for slot in range(slots):
             x = lax.dot_general(
                 qs_ref[slot, part, :], ka_ref[slot], NT, preferred_element_type=F32
@@ -216,7 +281,8 @@
             qs_ref[slot, part, base : base + 3] = jnp.concatenate([one, two, three], 1)
             mixed_ref[slot, part, :] = mixed
             alive = (slot < live_count).astype(F32)
-            stage[part, slot * HD : (slot + 1) * HD] = (mixed * alive).astype(BF16)
+            kept.append((mixed * alive).astype(BF16))
+        stage[step] = pack_rows(jnp.concatenate(kept, 1))
 
         @pl.when(step < 3 * per_share)
         def _():
@@ -225,8 +291,9 @@
         return carry
 
     lax.fori_loop(0, rows // sub, attend_rows, 0)
-    start = pl.ds(pl.multiple_of(mp * share, share), share)
-    keep = pltpu.make_async_copy(stage.at[start], got_ref.at[mp], here.at[3])
+    keep = pltpu.make_async_copy(
+        stage.at[pl.ds(3 * per_share, per_share)], got_ref.at[mp], here.at[3]
+    )
     keep.start()
     last_weights(3)
     for s in range(4):
@@ -237,6 +304,12 @@
             weights(s, kind).wait_send()
     for copy in firsts + shared + lifts:
         copy.wait_send()
+
+    @pl.when(inner)
+    def _():
+        for copy in inner_lifts:
+            copy.wait_send()
+
     for copy in biases:
         copy.wait()
     for step in range(3 * per_share):
@@ -245,9 +318,11 @@
     keep.wait()
 
 
-def front(frames, wq, packed, up_bias, offsets, seg_ids, slots):
-    rows, _ = frames.shape
-    piece, lanes = packed.shape
+def front(frames, qkv_weight, up_weight, down_flip, out_flip, vectors, seg_ids, slots):
+    rows, depth = frames.shape
+    piece, hidden_cols = up_weight.shape
+    width = slots * HD
+    lanes = -(-(2 * hidden_cols + width) // 128) * 128
     sub = 256
     shape = lambda n: jax.ShapeDtypeStruct((slots, rows, n), BF16)
     vmem = pl.BlockSpec(memory_space=pltpu.VMEM)
@@ -255,32 +330,35 @@
     steps = rows // sub
     return pl.pallas_call(
         functools.partial(front_kernel, slots, sub),
-        in_specs=[vmem] * 6,
+        in_specs=[vmem] * 7,
         out_specs=[vmem] * 9,
         out_shape=[
             jax.ShapeDtypeStruct((4, 8, piece, lanes), BF16),
-            jax.ShapeDtypeStruct((8 * piece, wq.shape[1]), BF16),
-            jax.ShapeDtypeStruct((4,) + up_bias.shape, F32),
+            jax.ShapeDtypeStruct((8 * piece, 3 * width), BF16),
+            jax.ShapeDtypeStruct((4, 1, HALF), F32),
             shape(AUG), shape(AUG), shape(VAUG), shape(HD),
             jax.ShapeDtypeStruct((slots, rows, HD), F32),
-            jax.ShapeDtypeStruct((4, rows // 4, slots * HD), BF16),
+            jax.ShapeDtypeStruct((4, steps // 4, sub * 3 // 2, 2 * HD), BF16),
         ],
         scratch_shapes=[
-            pltpu.VMEM((rows, slots * HD), BF16),
-            dma((7,)), dma((7,)), dma((3,)), dma((3,)), dma((4, 7)), dma((4, 7)), dma((3,)), dma((3,)),
+            pltpu.VMEM((steps, sub * 3 // 2, 2 * HD), BF16),
+            pltpu.VMEM((piece, 3 * width), BF16), pltpu.VMEM((piece, lanes), BF16),
+            pltpu.VMEM((1, HALF), F32),
+            dma((7,)), dma((7,)), dma((5,)), dma((4,)), dma((4, 7)), dma((4, 7)), dma((3,)), dma((3,)),
             dma((steps,)), dma((steps,)), dma((4,)),
         ],
         compiler_params=pltpu.CompilerParams(
-            collective_id=1, has_side_effects=True, vmem_limit_bytes=VMEM_LIMIT
+            collective_id=1, has_side_effects=True, vmem_limit_bytes=16 << 20
         ),
         name="front",
-    )(frames, wq, packed, up_bias, offsets, seg_ids.reshape(rows, 1))
+    )(frames, qkv_weight, up_weight, down_flip, out_flip, vectors, seg_ids.reshape(1, rows))
 
 
 def project_kernel(slots, x_ref, w_ref, b_ref, seg_ref, qs_ref, ka_ref, va_ref, kk_ref):
     made = jnp.dot(x_ref[...], w_ref[...], preferred_element_type=F32) + b_ref[...]
+    marks = seg_ref[...] == lax.broadcasted_iota(jnp.int32, (x_ref.shape[0], MAX_SEGS), 1)
     spread_rows(
-        made.astype(BF16), seg_ref[...], slots, qs_ref, ka_ref, va_ref, kk_ref, slice(None)
+        made.astype(BF16), jnp.where(marks, 1.0, 0.0), slots, qs_ref, ka_ref, va_ref, kk_ref, slice(None)
     )
 
 
@@ -421,7 +499,7 @@
 ):
     x_own, y_own, ow, act, pre_low, slope, hid_low, two_low, one_low, here = scratch[:10]
     share = out_ref.shape[0]
-    width = got_ref.shape[2]
+    width = ow.shape[2]
     gap = HALF - hidden_cols
     dp = lax.axis_index("dp")
     mp = lax.axis_index("mp")
@@ -433,12 +511,12 @@
     for copy in loads:
         copy.start()
     if linked:
-        back_own, grads, arrived, b_send, b_recv, g_send, g_recv = scratch[10:]
+        back_own, got, grads, arrived, b_send, b_recv, g_send, g_recv = scratch[10:]
         core = lax.rem(dp, 2)
         sibling = (dp ^ 1, mp)
         plane_barrier([sibling] + [(dp, mp ^ s) for s in range(1, 4)])
     else:
-        back_own, grads = back_ref, grad_ref
+        back_own, got, grads = back_ref, got_ref, grad_ref
     out_bias, gain_one, shift_one = vec_ref[0:1, :], vec_ref[1:2, :], vec_ref[2:3, :]
     down_bias, gain_two, shift_two = vec_ref[3:4, :], vec_ref[4:5, :], vec_ref[5:6, :]
     for g in range(groups):
@@ -453,17 +531,18 @@
         copy.wait()
 
     def send_back(step, s):
-        part = pl.ds(pl.multiple_of(step * block, block), block)
         at = step * 3 + s - 1
         return remote(
-            back_own.at[mp ^ s, part], back_ref.at[mp, part], b_send.at[at], b_recv.at[at], (dp, mp ^ s)
+            back_own.at[mp ^ s, step], back_ref.at[mp, step], b_send.at[at], b_recv.at[at], (dp, mp ^ s)
         )
 
     def some_rows(step, carry):
         part = pl.ds(pl.multiple_of(step * block, block), block)
         summed = x_own[part, :].astype(F32) + out_bias
         for g in range(groups):
-            summed += lax.dot_general(got_ref[g, part, :], ow[g], NT, preferred_element_type=F32)
+            if linked:
+                got[g, part, :] = unpack_rows(got_ref[g, step])
+            summed += lax.dot_general(got[g, part, :], ow[g], NT, preferred_element_type=F32)
         normed_one, factor_one = norm_forward(summed)
         hidden = normed_one * gain_one + shift_one
         hidden_low = hidden.astype(BF16)
@@ -502,7 +581,11 @@
         one_low[part, :] = sum_one
         for g in range(groups):
             made = jnp.dot(sum_one, ow[g], preferred_element_type=F32)
-            back_own[g, part, :] = jnp.where(alive[g], made, 0.0).astype(BF16)
+            made = jnp.where(alive[g], made, 0.0).astype(BF16)
+            if linked:
+                back_own[g, step] = pack_rows(made)
+            else:
+                back_own[g, part, :] = made
         if linked:
             for s in range(1, 4):
                 send_back(step, s).start()
@@ -521,7 +604,7 @@
     shared = []
     for g in range(groups):
         made = jnp.dot(hid_flip, pre_low[g], preferred_element_type=F32).astype(BF16)
-        grad_out = jnp.dot(one_flip, got_ref[g], preferred_element_type=F32).astype(BF16)
+        grad_out = jnp.dot(one_flip, got[g], preferred_element_type=F32).astype(BF16)
         rest = width - gap
         left = jnp.concatenate([made[:, :hidden_cols], grad_out[:, :gap]], 1)
         made = jnp.dot(two_flip, act[g], preferred_element_type=F32).astype(BF16)
@@ -530,12 +613,21 @@
             [made[:, :hidden_cols], grad_out[:, gap:], jnp.zeros((made.shape[0], spare), BF16)], 1
         )
         if linked:
-            piece = grads.shape[4 - 1]
+            piece = grad_ref.shape[2]
             for d in range(8):
                 at = slice(d * piece, (d + 1) * piece)
-                grads[g, d // 2, d % 2, :, :HALF] = left[at]
-                grads[g, d // 2, d % 2, :, HALF:] = right[at]
-            copy = remote(grads.at[g, :, 1 - core], arrived.at[g], g_send.at[g], g_recv.at[g], sibling)
+
+                @pl.when(core == d % 2)
+                def _():
+                    grad_ref[g, d // 2, :, :HALF] = left[at]
+                    grad_ref[g, d // 2, :, HALF:] = right[at]
+
+                @pl.when(core != d % 2)
+                def _():
+                    grads[g, d // 2, :, :HALF] = left[at]
+                    grads[g, d // 2, :, HALF:] = right[at]
+
+            copy = remote(grads.at[g], arrived.at[g], g_send.at[g], g_recv.at[g], sibling)
             copy.start()
             shared.append(copy)
         else:
@@ -545,7 +637,7 @@
         for g in range(groups):
             shared[g].wait_recv()
             for c in range(4):
-                grad_ref[g, c] = grads[g, c, core] + arrived[g, c]
+                grad_ref[g, c] += arrived[g, c]
         for step in range(share // block):
             for s in range(1, 4):
                 send_back(step, s).wait()
@@ -555,9 +647,10 @@
 
 
 def middle(frames, cotangent, got, weights, up_bias, vectors, hidden_cols, linked):
-    groups, share, width = got.shape
-    depth = frames.shape[1]
+    groups = got.shape[0]
+    share, depth = frames.shape[0] // groups, frames.shape[1]
     lanes = weights.shape[2]
+    width = 3 * HD
     block = min(256, share)
     vmem = pl.BlockSpec(memory_space=pltpu.VMEM)
     rest = pl.BlockSpec(memory_space=pl.ANY)
@@ -580,8 +673,9 @@
         grads = jax.ShapeDtypeStruct((groups, 4, piece, lanes), BF16)
         sends = 3 * (share // block)
         scratch += [
+            pltpu.VMEM(got.shape, BF16),
             pltpu.VMEM((groups, share, width), BF16),
-            pltpu.VMEM((groups, 4, 2, piece, lanes), BF16),
+            pltpu.VMEM((groups, 4, piece, lanes), BF16),
             pltpu.VMEM((groups, 4, piece, lanes), BF16),
             dma((sends,)), dma((sends,)), dma((groups,)), dma((groups,)),
         ]
@@ -593,12 +687,14 @@
         out_shape=[
             jax.ShapeDtypeStruct((share, depth), BF16),
             jax.ShapeDtypeStruct((share, depth), F32),
-            jax.ShapeDtypeStruct((groups, share, width), BF16),
+            jax.ShapeDtypeStruct(got.shape, BF16),
             grads,
             jax.ShapeDtypeStruct((16, HALF), F32),
         ],
         scratch_shapes=scratch,
-        compiler_params=pltpu.CompilerParams(vmem_limit_bytes=VMEM_LIMIT, **extra),
+        compiler_params=pltpu.CompilerParams(
+            vmem_limit_bytes=33 << 20 if linked else VMEM_LIMIT, **extra
+        ),
         name="middle",
     )(frames, cotangent, got, weights, up_bias, vectors)
 
@@ -620,11 +716,11 @@
 def back_kernel(
     slots, sub,
     qs_ref, ka_ref, va_ref, kk_ref, mixed_ref, up_ref, sums_ref, x_ref, wq_ref, one_ref, small_ref,
-    fg_ref, gq_ref, gb_ref, gw_ref, gs_ref,
+    fg_ref, gq_ref, gb_ref, gup_ref, gdown_ref, gout_ref, gub_ref, s0, s1, s2, s3, s4, s5,
     upper, up_flip, q_flip, dq_acc, dk_acc, dv_acc, low, part_out, chain, fresh, far_in, near_in, third,
     tall_in, gq_own, gq_in, gb_own, gb_in, tiny, tiny_in,
     c_send, c_recv, f_send, f_recv, n_send, n_recv, t_send, t_recv, q_send, q_recv, b_send, b_recv,
-    s_send, s_recv,
+    s_send, s_recv, small_sum,
 ):
     dp = lax.axis_index("dp")
     mp = lax.axis_index("mp")
@@ -688,7 +784,11 @@
             swap(at - 1).wait_recv()
             made = tiny[at - 1] + tiny_in[at - 1]
             if at == len(partners):
-                gs_ref[...] = made
+                small_sum[...] = made
+                for row, ref in enumerate((s0, s1, s2, s3, s4, s5)):
+                    ref[...] = made[row : row + 1, :].reshape(ref.shape)
+                cols = gub_ref.shape[-1]
+                gub_ref[...] = small_sum[pl.ds(8 + mp, 1), :cols].reshape(gub_ref.shape)
                 return
             tiny[at] = made
         swap(at).start()
@@ -744,8 +844,9 @@
 
     def prepare(step, carry):
         at = pl.ds(pl.multiple_of(step * share, share), share)
+        wide = jnp.concatenate([unpack_rows(up_ref[step, i]) for i in range(up_ref.shape[1])], 0)
         for slot in range(slots):
-            up = up_ref[step, :, slot * HD : (slot + 1) * HD]
+            up = wide[:, slot * HD : (slot + 1) * HD]
             one, two, three = thirds(
                 jnp.sum(up.astype(F32) * mixed_ref[slot, at, :], -1, keepdims=True)
             )
@@ -759,14 +860,13 @@
     actions = {
         1: [(small_step, 1)],
         2: [(begin_grads, 1), (small_step, 2)],
-        3: [(join_far, 3), (small_step, 3)],
-        4: [(begin_grads, 0), (small_step, 4)],
-        5: [(join_far, 2)],
-        6: [(small_step, 5)],
-        7: [(join_far, 1), (join_near, 3)],
-        9: [(join_far, 0), (join_near, 2)],
-        12: [(join_near, 1)],
-        14: [(join_near, 0)],
+        3: [(join_far, 3), (begin_grads, 0), (small_step, 3)],
+        4: [(join_far, 2), (small_step, 4)],
+        5: [(join_near, 3), (small_step, 5)],
+        7: [(join_near, 2), (join_far, 1)],
+        9: [(join_far, 0)],
+        11: [(join_near, 1)],
+        13: [(join_near, 0)],
     }
 
     def pair(step, carry):
@@ -805,7 +905,9 @@
             @pl.when(step == when)
             def _():
                 finish(name)
-                if name > 0:
+                if name == 2:
+                    relay(name)
+                elif name > 0:
 
                     @pl.when((mp == 0) | (mp == 3))
                     def _():
@@ -814,12 +916,6 @@
         return carry
 
     lax.fori_loop(0, len(PAIRS), pair, 0)
-    for name in (2, 3, 1):
-
-        @pl.when((mp == 1) | (mp == 2))
-        def _():
-            relay(name)
-
     gq_parts = low[...]
     ones = jnp.ones((16, rows), BF16)
     gb_own[...] = jnp.dot(ones, gq_parts, preferred_element_type=F32)[0:8, :]
@@ -839,22 +935,35 @@
         )
     for copy in q_copies:
         copy.start()
+    for name in (3, 1):
+
+        @pl.when((mp == 1) | (mp == 2))
+        def _():
+            relay(name)
+
     for s in range(1, 4):
         lift(s).wait_recv()
     total = fresh[0].astype(F32)
     for s in range(1, 4):
         total = total + tall_in[s].astype(F32)
-    gw_ref[...] = total
+    cols = gup_ref.shape[1]
+    gap = HALF - cols
+    gup_ref[...] = total[:, :cols]
+    gdown_ref[...] = total[:, HALF : HALF + cols]
+    gout_ref[:, :gap] = total[:, cols:HALF]
+    gout_ref[:, gap:] = total[:, HALF + cols : HALF + cols + width - gap]
     for copy in q_copies:
         copy.wait_recv()
     total = gq_own[dp].astype(F32)
     for d in range(7):
         total = total + gq_in[d].astype(F32)
-    gq_ref[...] = total
+    for i in range(3):
+        gq_ref[i] = total[:, i * width : (i + 1) * width]
     total = gb_in[0]
     for d in range(1, 8):
         total = total + gb_in[d]
-    gb_ref[...] = total
+    gb_ref[0:1, :] = total[0:1, :width]
+    gb_ref[1:2, :] = total[0:1, 2 * width :]
 
     wide = one_ref[...] + part_out[0].astype(F32)
 
@@ -885,7 +994,7 @@
         copy.wait_send()
 
 
-def back_pass(qs, ka, va, kk, mixed, up, sums, frames, wq, one_grad, small):
+def back_pass(qs, ka, va, kk, mixed, up, sums, frames, wq, one_grad, small, hidden_cols):
     slots, rows, _ = qs.shape
     depth = frames.shape[1]
     share = rows // 4
@@ -895,16 +1004,19 @@
     dma = pltpu.SemaphoreType.DMA
     V = pltpu.VMEM
     return pl.pallas_call(
-        functools.partial(back_kernel, slots, min(256, share)),
+        functools.partial(back_kernel, slots, min(512, share)),
         in_specs=[vmem] * 11,
-        out_specs=[vmem] * 5,
+        out_specs=[vmem] * 13,
         out_shape=[
             jax.ShapeDtypeStruct((share, depth), BF16),
-            jax.ShapeDtypeStruct((piece, cols), F32),
-            jax.ShapeDtypeStruct((8, cols), F32),
-            jax.ShapeDtypeStruct((piece, lanes), F32),
-            jax.ShapeDtypeStruct(small.shape, F32),
-        ],
+            jax.ShapeDtypeStruct((3, piece, cols // 3), F32),
+            jax.ShapeDtypeStruct((2, cols // 3), F32),
+            jax.ShapeDtypeStruct((piece, hidden_cols), F32),
+            jax.ShapeDtypeStruct((piece, hidden_cols), F32),
+            jax.ShapeDtypeStruct((piece, cols // 3), F32),
+            jax.ShapeDtypeStruct((hidden_cols,), F32),
+        ]
+        + [jax.ShapeDtypeStruct((depth,), F32)] * 6,
         scratch_shapes=[
             V((slots, rows, VAUG), BF16), V((slots, HD, rows), BF16), V((slots, HD, rows), BF16),
             V((slots, rows, HD), F32), V((slots, HD, rows), F32), V((slots, HD, rows), F32),
@@ -914,10 +1026,10 @@
             V((8, piece, cols), BF16), V((7, piece, cols), BF16),
             V((8, cols), F32), V((8, 8, cols), F32), V((5,) + small.shape, F32), V((5,) + small.shape, F32),
             dma((4,)), dma((5,)), dma((4,)), dma((4,)), dma((4, 2)), dma((4, 2)), dma((4,)), dma((4,)),
-            dma((7,)), dma((7,)), dma((7,)), dma((7,)), dma((5,)), dma((5,)),
+            dma((7,)), dma((7,)), dma((7,)), dma((7,)), dma((5,)), dma((5,)), V(small.shape, F32),
         ],
         compiler_params=pltpu.CompilerParams(
-            collective_id=3, has_side_effects=True, vmem_limit_bytes=60 << 20
+            collective_id=3, has_side_effects=True, vmem_limit_bytes=31 << 20
         ),
         name="back_pass",
     )(qs, ka, va, kk, mixed, up, sums, frames, wq, one_grad, small)
@@ -941,20 +1053,28 @@
     live_count = HEADS // mp_size + (mp_index < HEADS % mp_size).astype(jnp.int32)
     live = (jnp.arange(slots) < live_count).astype(F32)
 
-    wq = jnp.transpose(qkv_weight, (1, 0, 2)).reshape(piece, 3 * width)
     out_flip = out_weight.T
-    packed = jnp.concatenate(
-        [up_weight, out_flip[:, :gap], down_weight.T, out_flip[:, gap:], jnp.zeros((piece, spare), BF16)], 1
+    down_flip = down_weight.T
+    wide = lambda v: jnp.pad(v, (0, HALF - v.shape[0]))
+    vectors = jnp.stack(
+        [
+            out_bias, gain_one, shift_one, down_bias, gain_two, shift_two, wide(up_bias),
+            wide(qkv_bias[0]), wide(qkv_bias[1]),
+        ]
     )
-    ub_pad = jnp.pad(up_bias, (0, gap))[None]
-    offsets = jnp.concatenate([qkv_bias[0], jnp.zeros_like(qkv_bias[0]), qkv_bias[1]])[None]
-    linked = (dp_size, mp_size) == (8, 4)
+    linked = (dp_size, mp_size, slots, rows) == (8, 4, 3, 2048)
     if linked:
         weights, qkv_full, ub_full, qs, ka, va, kk, mixed, got = front(
-            frames, wq, packed, ub_pad, offsets, seg_ids, slots
+            frames, qkv_weight, up_weight, down_flip, out_flip, vectors, seg_ids, slots
         )
         weights = weights.reshape(mp_size, depth, -1)
     else:
+        wq = jnp.transpose(qkv_weight, (1, 0, 2)).reshape(piece, 3 * width)
+        packed = jnp.concatenate(
+            [up_weight, out_flip[:, :gap], down_flip, out_flip[:, gap:], jnp.zeros((piece, spare), BF16)], 1
+        )
+        ub_pad = jnp.pad(up_bias, (0, gap))[None]
+        offsets = jnp.concatenate([qkv_bias[0], jnp.zeros_like(qkv_bias[0]), qkv_bias[1]])[None]
         qkv_full = lax.all_gather(wq, "dp", axis=0, tiled=True)
         weights = lax.all_gather(packed, "mp", axis=0, tiled=False)
         weights = lax.all_gather(weights, "dp", axis=1, tiled=True)
@@ -964,18 +1084,18 @@
         mixed_low = (mixed * live[:, None, None]).astype(BF16)
         sent = mixed_low.reshape(slots, mp_size, share, HD).transpose(1, 2, 0, 3)
         got = lax.all_to_all(sent.reshape(mp_size, share, width), "mp", 0, 0, tiled=True)
-    vectors = jnp.stack(
-        [out_bias, gain_one, shift_one, down_bias, gain_two, shift_two, out_bias, out_bias]
-    )
     output_frames, sum_one_grad, back, partial, small = middle(
         frames, cotangent, got, weights, ub_full, vectors, hidden_cols, linked
     )
     if linked:
-        frames_grad, grad_qkv, bias_sums, partial, small = back_pass(
-            qs, ka, va, kk, mixed, back, partial, frames, qkv_full, sum_one_grad, small
-        )
-        bias_sums = bias_sums[0]
-    else:
+        made = back_pass(
+            qs, ka, va, kk, mixed, back, partial, frames, qkv_full, sum_one_grad, small, hidden_cols
+        )
+        return (
+            output_frames, made[0], made[1], made[2], made[5].T, made[7], made[8], made[9], made[3],
+            made[6], made[4].T, made[10], made[11], made[12],
+        )
+    if not linked:
         back = lax.all_to_all(back, "mp", 0, 0, tiled=True)
         back = back.reshape(rows, slots, HD).transpose(1, 0, 2)
         partial = lax.psum_scatter(partial, "dp", scatter_dimension=1, tiled=True)

time: 229 us -> 211 us (0.921)
  Pallas kernels: 204 us -> 171 us
  local copies, waits for them, and re-layouts: 21.5 us -> 38.4 us
    unnamed x19 -> x54, local copies, waits for them, and re-layouts: 2.45 us -> 32.8 us
    pallas_call x1, Pallas kernels: 69.8 us -> 57.2 us  [front(): pl.pallas_call(functools.partial(front_kernel, slots, sub), in_specs=[vme...]
    pallas_call x1, Pallas kernels: 95.8 us -> 85.1 us  [back_pass(): pl.pallas_call(functools.partial(back_kernel, slots, min(512, share)), in...]
    pallas_call x1, Pallas kernels: 38.7 us -> 28.3 us  [middle(): pl.pallas_call(functools.partial(middle_kernel, groups, hidden_cols, bloc...]
    slice x8 -> x1, local copies, waits for them, and re-layouts: 8.05 us -> 0.76 us  [body(): qkv_bias[1]]
    reshape x3 -> x0, local copies, waits for them, and re-layouts: 3.91 us -> none  [the longest x1 2.05 us: front(): seg_ids.reshape(rows, 1)]
    another operation x7 -> x10, local copies, waits for them, and re-layouts: 0.67 us -> 4.2 us  [body(): jnp.stack([out_bias, gain_one, shift_one, down_bias, gain_two, shift_two,...]
    transpose x2 -> x0, local copies, waits for them, and re-layouts: 2.79 us -> none  [the longest x1 1.8 us: body(): partial[:, HALF:HALF + hidden_cols]]
where the time goes in v2:
time: 211 us; the launch traced here: 210 us
  Pallas kernels  171 us (81%)
  local copies, waits for them, and re-layouts  38.4 us (18%)
    pallas_call x1, Pallas kernels, back_pass(): pl.pallas_call(functools.partial(back_kernel, slots, min(512, share)), in...  85.1 us
    pallas_call x1, Pallas kernels, front(): pl.pallas_call(functools.partial(front_kernel, slots, sub), in_specs=[vme...  57.2 us
    unnamed x54, local copies, waits for them, and re-layouts  32.8 us
    pallas_call x1, Pallas kernels, middle(): pl.pallas_call(functools.partial(middle_kernel, groups, hidden_cols, bloc...  28.3 us

profile of v2, /device:TPU:0, one launch (start us, length us, event | category | flops | bytes accessed | tf_op | source)
XLA Modules:
  0.0 209.8 jit_solution(14894911430407566500)
XLA Ops:
  0.6 0.8 fusion
  1.4 0.7 stack.30
  2.1 0.7 stack.31
  2.8 0.7 stack.32
  3.5 0.7 stack.33
  4.2 0.7 stack.34
  4.8 0.7 stack.35
  5.6 0.7 pad.11
  6.3 1.7 copy-done
  8.1 0.9 copy-done.15
  9.0 0.9 copy-done.16
  9.9 0.9 copy-done.17
  10.8 0.8 copy-done.18
  11.5 0.7 copy-done.19
  12.2 57.2 %front.1 = (bf16[4,8,80,1408]{3,2,1,0:T(8,128)(2,1)S(1)}, bf16[640,576]{1,0:T(8,128)(2,1)S(1)}, f32[4,1,640]{2,1,0:T(1,128)S(1)}, bf16[3,2048,256]{2,1,0:T(8,128...) custom-call(bf16[2048,640]{1,0:T(8,128)(2,1)S(1)} %copy-done, ...), custom_call_target="tpu_custom_call" | custom-call | tf_op jit(solution)/shard_map/front/pallas_call | solution.py:331
  69.5 1.7 copy-done.4
  71.2 1.7 copy-done.6
  72.9 1.7 copy-done.8
  74.6 1.1 copy-done.11
  75.7 1.7 copy-done.10
  77.5 28.3 %middle.1 = (bf16[512,640]{1,0:T(8,128)(2,1)S(1)}, f32[512,640]{1,0:T(8,128)S(1)}, bf16[4,2,384,128]{3,2,1,0:T(8,128)(2,1)S(1)}, bf16[4,4,80,1408]{3,2,1,0:T(8,128)(2,1)S(1)}, f32[16,640]{1,0:T(8,128)S(1)}) custom-call(bf16[2048,640]{1,0:T(8,128)(2,1)S(1)} %copy-done.1, bf16[2048,640]{1,0:T(8,128)(2,1)S(1)} %copy-done.10, ...), custom_call_target="tpu_custom_call" | custom-call | tf_op jit(solution)/shard_map/middle/pallas_call | solution.py:683
  105.8 1.8 copy-done.2
  107.6 0.8 copy-done.13
  108.4 2.0 copy-done.3
  110.4 1.9 copy-done.5
  112.3 1.9 copy-done.9
  114.2 1.4 copy-done.12
  115.6 85.1 %back_pass.1 = (bf16[512,640]{1,0:T(8,128)(2,1)S(1)}, f32[3,80,192]{2,1,0:T(8,128)S(1)}, f32[2,192]{1,0:T(2,128)S(1)}, f32[80,560]{1,0:T(8,128)S(1)}, f32[80,560...) custom-call(bf16[3,2048,256]{2,1,0:T(8,128)(2,1)S(1)} %copy-done.5, ...), custom_call_target="tpu_custom_call" | custom-call | tf_op jit(solution)/shard_map/back_pass/pallas_call | solution.py:1006
  200.7 0.8 copy.43
  201.6 0.8 copy.44
  202.4 0.7 copy.45
  207.4 0.7 copy.53
  (39 shorter events, 6.2 us)
Async XLA Ops:
  6.3 1.7 copy-start
  8.1 0.9 copy-start.15
  9.0 0.9 copy-start.16
  9.9 0.9 copy-start.17
  10.8 0.8 copy-start.18
  11.5 0.7 copy-start.19
  12.2 63.5 %copy-start.1 = (bf16[2048,640]{1,0:T(8,128)(2,1)S(1)}, bf16[2048,640]{1,0:T(8,128)(2,1)}, u32[]{:S(2)}) copy-start(bf16[2048,640]{1,0:T(8,128)(2,1)} %x_ref.5) | copy-start | bytes 7864324
  69.5 1.7 copy-start.4
  71.2 1.7 copy-start.6
  72.9 1.7 copy-start.8
  74.6 1.1 copy-start.11
  75.7 1.7 copy-start.10
  77.5 30.9 %copy-start.7 = (bf16[3,2048,256]{2,1,0:T(8,128)(2,1)S(1)}, bf16[3,2048,256]{2,1,0:T(8,128)(2,1)}, u32[]{:S(2)}) copy-start(bf16[3,2048,256]{2,1,0:T(8,128)(2,1)} %copy-done.6) | copy-start | bytes 9437188
  105.8 1.8 copy-start.2
  107.6 0.8 copy-start.13
  108.4 2.0 copy-start.3
  110.4 1.9 copy-start.5
  112.3 1.9 copy-start.9
  114.2 1.4 copy-start.12
  115.6 85.1 %copy-start.14 = (bf16[512,640]{1,0:T(8,128)(2,1)S(1)}, bf16[512,640]{1,0:T(8,128)(2,1)}, u32[]{:S(2)}) copy-start(bf16[512,640]{1,0:T(8,128)(2,1)} %copy-done.13) | copy-start | bytes 1966084

commit v3 on v2

--- a/solution.py
+++ b/solution.py
@@ -57,7 +57,7 @@
         qs_ref[slot, rows, :] = jnp.concatenate([q, q, q, chosen, q_tail], 1)
         ka_ref[slot, rows, :] = jnp.concatenate([one, two, three, barred, minus], 1)
         va_ref[slot, rows, :] = jnp.concatenate([v, v_tail], 1)
-        kk_ref[slot, rows, :] = k
+    kk_ref[rows, :] = made[:, width : 2 * width]
 
 
 def plane_barrier(peers):
@@ -91,10 +91,10 @@
 
 def front_kernel(
     slots, sub,
-    x_ref, qkv_ref, up_ref, down_ref, out_ref, vec_ref, seg_ref,
+    x_hbm, qkv_hbm, up_hbm, down_hbm, out_hbm, ub_ref, qb_ref, seg_ref,
     all_ref, wfull_ref, ball_ref, qs_ref, ka_ref, va_ref, kk_ref, mixed_ref, got_ref,
-    stage, wq_ref, pack_ref, bias_ref,
-    q_send, q_recv, z_send, z_recv, w_send, w_recv, b_send, b_recv, a_send, a_recv, here,
+    x_ref, qkv_ref, up_ref, down_ref, out_ref, stage, wq_ref, pack_ref, bias_ref,
+    q_send, q_recv, z_send, z_recv, w_send, w_recv, b_send, b_recv, a_send, a_recv, here, loaded,
 ):
     dp = lax.axis_index("dp")
     mp = lax.axis_index("mp")
@@ -103,6 +103,14 @@
     tall = [(dp, mp ^ s) for s in range(1, 4)]
     inner = (mp == 1) | (mp == 2)
     width = slots * HD
+    pairs = ((qkv_hbm, qkv_ref), (up_hbm, up_ref), (down_hbm, down_ref), (out_hbm, out_ref), (x_hbm, x_ref))
+    loads = [pltpu.make_async_copy(a, b, loaded.at[i]) for i, (a, b) in enumerate(pairs)]
+    for copy in loads:
+        copy.start()
+    bias_ref[...] = jnp.zeros_like(bias_ref)
+    bias_ref[:, : up_hbm.shape[1]] = ub_ref[...].reshape(1, up_hbm.shape[1])
+    for copy in loads[:4]:
+        copy.wait()
     for i in range(3):
         wq_ref[:, i * width : (i + 1) * width] = qkv_ref[i]
     hidden_cols = up_ref.shape[1]
@@ -114,7 +122,6 @@
     pack_ref[:, HALF + hidden_cols : HALF + hidden_cols + rest] = out_ref[:, gap:]
     spare = pack_ref.shape[1] - HALF - hidden_cols - rest
     pack_ref[:, HALF + hidden_cols + rest :] = jnp.zeros((pack_ref.shape[0], spare), BF16)
-    bias_ref[...] = vec_ref[6:7, :]
     plane_barrier([sibling] + [(d, mp) for d in plane] + tall)
     rows = x_ref.shape[0]
     share = rows // 4
@@ -213,13 +220,14 @@
         inner_lifts[2].start()
 
 
+    loads[4].wait()
     block = 256
 
     def project_rows(step, carry):
         part = pl.ds(pl.multiple_of(step * block, block), block)
         x = x_ref[part, :]
         offsets = jnp.concatenate(
-            [vec_ref[7:8, :width], jnp.zeros((1, width), F32), vec_ref[8:9, :width]], 1
+            [qb_ref[0:1, :], jnp.zeros((1, width), F32), qb_ref[1:2, :]], 1
         )
         made = jnp.dot(x, wfull_ref[...], preferred_element_type=F32) + offsets
         marks = seg_ref[:, part] == lax.broadcasted_iota(jnp.int32, (MAX_SEGS, block), 0)
@@ -279,7 +287,7 @@
             one, two, three = thirds(top + jnp.log2(total))
             base = 3 * HD + MAX_SEGS
             qs_ref[slot, part, base : base + 3] = jnp.concatenate([one, two, three], 1)
-            mixed_ref[slot, part, :] = mixed
+            mixed_ref[part, slot * HD : (slot + 1) * HD] = mixed
             alive = (slot < live_count).astype(F32)
             kept.append((mixed * alive).astype(BF16))
         stage[step] = pack_rows(jnp.concatenate(kept, 1))
@@ -318,7 +326,7 @@
     keep.wait()
 
 
-def front(frames, qkv_weight, up_weight, down_flip, out_flip, vectors, seg_ids, slots):
+def front(frames, qkv_weight, up_weight, down_flip, out_flip, up_bias, qkv_bias, seg_ids, slots):
     rows, depth = frames.shape
     piece, hidden_cols = up_weight.shape
     width = slots * HD
@@ -326,32 +334,38 @@
     sub = 256
     shape = lambda n: jax.ShapeDtypeStruct((slots, rows, n), BF16)
     vmem = pl.BlockSpec(memory_space=pltpu.VMEM)
+    hbm = pl.BlockSpec(memory_space=pltpu.MemorySpace.HBM)
     dma = pltpu.SemaphoreType.DMA
     steps = rows // sub
+    operands = (frames, qkv_weight, up_weight, down_flip, out_flip)
     return pl.pallas_call(
         functools.partial(front_kernel, slots, sub),
-        in_specs=[vmem] * 7,
+        in_specs=[hbm] * 5 + [vmem] * 3,
         out_specs=[vmem] * 9,
         out_shape=[
             jax.ShapeDtypeStruct((4, 8, piece, lanes), BF16),
             jax.ShapeDtypeStruct((8 * piece, 3 * width), BF16),
             jax.ShapeDtypeStruct((4, 1, HALF), F32),
-            shape(AUG), shape(AUG), shape(VAUG), shape(HD),
-            jax.ShapeDtypeStruct((slots, rows, HD), F32),
+            shape(AUG), shape(AUG), shape(VAUG),
+            jax.ShapeDtypeStruct((rows, width), BF16),
+            jax.ShapeDtypeStruct((rows, width), F32),
             jax.ShapeDtypeStruct((4, steps // 4, sub * 3 // 2, 2 * HD), BF16),
         ],
         scratch_shapes=[
+            pltpu.VMEM(frames.shape, BF16), pltpu.VMEM(qkv_weight.shape, BF16),
+            pltpu.VMEM(up_weight.shape, BF16), pltpu.VMEM(down_flip.shape, BF16),
+            pltpu.VMEM(out_flip.shape, BF16),
             pltpu.VMEM((steps, sub * 3 // 2, 2 * HD), BF16),
             pltpu.VMEM((piece, 3 * width), BF16), pltpu.VMEM((piece, lanes), BF16),
             pltpu.VMEM((1, HALF), F32),
             dma((7,)), dma((7,)), dma((5,)), dma((4,)), dma((4, 7)), dma((4, 7)), dma((3,)), dma((3,)),
-            dma((steps,)), dma((steps,)), dma((4,)),
+            dma((steps,)), dma((steps,)), dma((4,)), dma((len(operands),)),
         ],
         compiler_params=pltpu.CompilerParams(
-            collective_id=1, has_side_effects=True, vmem_limit_bytes=16 << 20
+            collective_id=1, has_side_effects=True, vmem_limit_bytes=20 << 20
         ),
         name="front",
-    )(frames, qkv_weight, up_weight, down_flip, out_flip, vectors, seg_ids.reshape(1, rows))
+    )(*operands, up_bias, qkv_bias, seg_ids.reshape(1, rows))
 
 
 def project_kernel(slots, x_ref, w_ref, b_ref, seg_ref, qs_ref, ka_ref, va_ref, kk_ref):
@@ -376,8 +390,12 @@
             pl.BlockSpec((1, offsets.shape[1]), lambda i: (0, 0)),
             pl.BlockSpec((block, 1), lambda i: (i, 0)),
         ],
-        out_specs=[spread(AUG), spread(AUG), spread(VAUG), spread(HD)],
-        out_shape=[shape(AUG), shape(AUG), shape(VAUG), shape(HD)],
+        out_specs=[
+            spread(AUG), spread(AUG), spread(VAUG), pl.BlockSpec((block, slots * HD), lambda i: (i, 0)),
+        ],
+        out_shape=[
+            shape(AUG), shape(AUG), shape(VAUG), jax.ShapeDtypeStruct((rows, slots * HD), BF16),
+        ],
         compiler_params=pltpu.CompilerParams(vmem_limit_bytes=VMEM_LIMIT),
         name="project",
     )(frames, weight, offsets, seg_ids.reshape(rows, 1))
@@ -494,7 +512,7 @@
 
 def middle_kernel(
     groups, hidden_cols, block, linked,
-    x_ref, y_ref, got_ref, w_ref, ub_ref, vec_ref,
+    x_ref, y_ref, got_ref, w_ref, ub_ref, v0, v1, v2, v3, v4, v5,
     out_ref, s1_ref, back_ref, grad_ref, small_ref, *scratch,
 ):
     x_own, y_own, ow, act, pre_low, slope, hid_low, two_low, one_low, here = scratch[:10]
@@ -517,8 +535,9 @@
         plane_barrier([sibling] + [(dp, mp ^ s) for s in range(1, 4)])
     else:
         back_own, got, grads = back_ref, got_ref, grad_ref
-    out_bias, gain_one, shift_one = vec_ref[0:1, :], vec_ref[1:2, :], vec_ref[2:3, :]
-    down_bias, gain_two, shift_two = vec_ref[3:4, :], vec_ref[4:5, :], vec_ref[5:6, :]
+    out_bias, gain_one, shift_one, down_bias, gain_two, shift_two = (
+        v[...].reshape(1, v.shape[0]) for v in (v0, v1, v2, v3, v4, v5)
+    )
     for g in range(groups):
         ow[g, :, :gap] = w_ref[g, :, hidden_cols:HALF]
         ow[g, :, gap:] = w_ref[g, :, HALF + hidden_cols : HALF + hidden_cols + width - gap]
@@ -600,22 +619,35 @@
     if linked:
         keep = pltpu.make_async_copy(back_own.at[mp], back_ref.at[mp], here.at[2])
         keep.start()
-    hid_flip, two_flip, one_flip = hid_low[...].T, two_low[...].T, one_low[...].T
+    depth = hid_low.shape[1]
+    rest = width - gap
+    spare = w_ref.shape[2] - HALF - hidden_cols - rest
+    span = depth // 2
     shared = []
     for g in range(groups):
-        made = jnp.dot(hid_flip, pre_low[g], preferred_element_type=F32).astype(BF16)
-        grad_out = jnp.dot(one_flip, got[g], preferred_element_type=F32).astype(BF16)
-        rest = width - gap
-        left = jnp.concatenate([made[:, :hidden_cols], grad_out[:, :gap]], 1)
-        made = jnp.dot(two_flip, act[g], preferred_element_type=F32).astype(BF16)
-        spare = w_ref.shape[2] - HALF - hidden_cols - rest
-        right = jnp.concatenate(
-            [made[:, :hidden_cols], grad_out[:, gap:], jnp.zeros((made.shape[0], spare), BF16)], 1
-        )
-        if linked:
+        for part in range(2):
+            cols = slice(part * span, (part + 1) * span)
+            made = lax.dot_general(
+                hid_low[:, cols], pre_low[g], TN, preferred_element_type=F32
+            ).astype(BF16)
+            grad_out = lax.dot_general(
+                one_low[:, cols], got[g], TN, preferred_element_type=F32
+            ).astype(BF16)
+            left = jnp.concatenate([made[:, :hidden_cols], grad_out[:, :gap]], 1)
+            made = lax.dot_general(
+                two_low[:, cols], act[g], TN, preferred_element_type=F32
+            ).astype(BF16)
+            right = jnp.concatenate(
+                [made[:, :hidden_cols], grad_out[:, gap:], jnp.zeros((span, spare), BF16)], 1
+            )
+            if not linked:
+                grads[g, cols, :HALF] = left
+                grads[g, cols, HALF:] = right
+                continue
             piece = grad_ref.shape[2]
-            for d in range(8):
-                at = slice(d * piece, (d + 1) * piece)
+            for i in range(span // piece):
+                d = part * (span // piece) + i
+                at = slice(i * piece, (i + 1) * piece)
 
                 @pl.when(core == d % 2)
                 def _():
@@ -627,12 +659,10 @@
                     grads[g, d // 2, :, :HALF] = left[at]
                     grads[g, d // 2, :, HALF:] = right[at]
 
+        if linked:
             copy = remote(grads.at[g], arrived.at[g], g_send.at[g], g_recv.at[g], sibling)
             copy.start()
             shared.append(copy)
-        else:
-            grads[g, :, :HALF] = left
-            grads[g, :, HALF:] = right
     if linked:
         for g in range(groups):
             shared[g].wait_recv()
@@ -653,7 +683,7 @@
     width = 3 * HD
     block = min(256, share)
     vmem = pl.BlockSpec(memory_space=pltpu.VMEM)
-    rest = pl.BlockSpec(memory_space=pl.ANY)
+    rest = pl.BlockSpec(memory_space=pltpu.MemorySpace.HBM)
     dma = pltpu.SemaphoreType.DMA
     scratch = [
         pltpu.VMEM((share, depth), BF16),
@@ -682,7 +712,7 @@
     extra = dict(collective_id=2, has_side_effects=True) if linked else {}
     return pl.pallas_call(
         functools.partial(middle_kernel, groups, hidden_cols, block, linked),
-        in_specs=[rest, rest, vmem, vmem, vmem, vmem],
+        in_specs=[rest, rest] + [vmem] * 9,
         out_specs=[vmem] * 5,
         out_shape=[
             jax.ShapeDtypeStruct((share, depth), BF16),
@@ -696,7 +726,7 @@
             vmem_limit_bytes=33 << 20 if linked else VMEM_LIMIT, **extra
         ),
         name="middle",
-    )(frames, cotangent, got, weights, up_bias, vectors)
+    )(frames, cotangent, got, weights, up_bias, *vectors)
 
 
 PAIRS = (
@@ -715,17 +745,17 @@
 
 def back_kernel(
     slots, sub,
-    qs_ref, ka_ref, va_ref, kk_ref, mixed_ref, up_ref, sums_ref, x_ref, wq_ref, one_ref, small_ref,
+    qs_ref, ka_ref, va_ref, kk_ref, mixed_ref, up_ref, sums_ref, x_hbm, wq_ref, one_ref, small_ref,
     fg_ref, gq_ref, gb_ref, gup_ref, gdown_ref, gout_ref, gub_ref, s0, s1, s2, s3, s4, s5,
     upper, up_flip, q_flip, dq_acc, dk_acc, dv_acc, low, part_out, chain, fresh, far_in, near_in, third,
     tall_in, gq_own, gq_in, gb_own, gb_in, tiny, tiny_in,
     c_send, c_recv, f_send, f_recv, n_send, n_recv, t_send, t_recv, q_send, q_recv, b_send, b_recv,
-    s_send, s_recv, small_sum,
+    s_send, s_recv, small_sum, x_ref, loaded, gq_acc,
 ):
     dp = lax.axis_index("dp")
     mp = lax.axis_index("mp")
     chip = dp // 2
-    rows, depth = x_ref.shape
+    rows, depth = x_hbm.shape
     share = rows // 4
     width = slots * HD
     others = [(dp ^ d, mp) for d in range(1, 8)]
@@ -735,6 +765,11 @@
 
     def rows_of(name):
         return pl.ds(pl.multiple_of((mp ^ name) * share, share), share)
+
+    def load_rows(name):
+        return pltpu.make_async_copy(x_hbm.at[rows_of(name)], x_ref, loaded.at[0])
+
+    load_rows(3).start()
 
     def far(s):
         return remote(
@@ -828,16 +863,26 @@
         at = rows_of(name)
         for slot in range(slots):
             col = slot * HD
-            low[at, col : col + HD] = (dq_acc[slot, at, :] * SCALE).astype(BF16)
-            low[at, width + col : width + col + HD] = (dk_acc[slot, :, at] * SCALE).T.astype(BF16)
-            low[at, 2 * width + col : 2 * width + col + HD] = dv_acc[slot, :, at].T.astype(BF16)
+            low[:, col : col + HD] = (dq_acc[slot, at, :] * SCALE).astype(BF16)
+            low[:, width + col : width + col + HD] = (dk_acc[slot, :, at] * SCALE).T.astype(BF16)
+            low[:, 2 * width + col : 2 * width + col + HD] = dv_acc[slot, :, at].T.astype(BF16)
         part_out[name] = lax.dot_general(
-            low[at, :], wq_ref[...], NT, preferred_element_type=F32
+            low[...], wq_ref[...], NT, preferred_element_type=F32
         ).astype(BF16)
+
+    def add_rows(name):
+        ones = jnp.ones((16, share), BF16)
+        gb_own[...] += jnp.dot(ones, low[...], preferred_element_type=F32)[0:8, :]
+        load_rows(name).wait()
+        gq_acc[...] += lax.dot_general(x_ref[...], low[...], TN, preferred_element_type=F32)
+        if name > 0:
+            load_rows(name - 1).start()
 
     dq_acc[...] = jnp.zeros_like(dq_acc)
     dk_acc[...] = jnp.zeros_like(dk_acc)
     dv_acc[...] = jnp.zeros_like(dv_acc)
+    gq_acc[...] = jnp.zeros_like(gq_acc)
+    gb_own[...] = jnp.zeros_like(gb_own)
     begin_grads(3)
     begin_grads(2)
     small_step(0)
@@ -848,7 +893,9 @@
         for slot in range(slots):
             up = wide[:, slot * HD : (slot + 1) * HD]
             one, two, three = thirds(
-                jnp.sum(up.astype(F32) * mixed_ref[slot, at, :], -1, keepdims=True)
+                jnp.sum(
+                    up.astype(F32) * mixed_ref[at, slot * HD : (slot + 1) * HD], -1, keepdims=True
+                )
             )
             blank = jnp.zeros((share, VAUG - HD - 3), BF16)
             upper[slot, at, :] = jnp.concatenate([up, one, two, three, blank], 1)
@@ -898,7 +945,7 @@
                     q_flip[slot, :, part], ds, preferred_element_type=F32
                 )
                 dq_acc[slot, part, :] += jnp.dot(
-                    ds, kk_ref[slot, keys, :], preferred_element_type=F32
+                    ds, kk_ref[keys, slot * HD : (slot + 1) * HD], preferred_element_type=F32
                 )
         for when, name in ENDS.items():
 
@@ -913,17 +960,15 @@
                     def _():
                         relay(name)
 
+                add_rows(name)
+
         return carry
 
     lax.fori_loop(0, len(PAIRS), pair, 0)
-    gq_parts = low[...]
-    ones = jnp.ones((16, rows), BF16)
-    gb_own[...] = jnp.dot(ones, gq_parts, preferred_element_type=F32)[0:8, :]
     gb_in[dp] = gb_own[...]
     piece = depth // 8
-    made = lax.dot_general(x_ref[...], gq_parts, TN, preferred_element_type=F32).astype(BF16)
     for d in range(8):
-        gq_own[d] = made[d * piece : (d + 1) * piece]
+        gq_own[d] = gq_acc[d * piece : (d + 1) * piece, :].astype(BF16)
     q_copies = []
     for d in range(1, 8):
         to = dp ^ d
@@ -1001,11 +1046,12 @@
     piece, lanes = sums.shape[2:]
     cols = wq.shape[1]
     vmem = pl.BlockSpec(memory_space=pltpu.VMEM)
+    hbm = pl.BlockSpec(memory_space=pltpu.MemorySpace.HBM)
     dma = pltpu.SemaphoreType.DMA
     V = pltpu.VMEM
     return pl.pallas_call(
         functools.partial(back_kernel, slots, min(512, share)),
-        in_specs=[vmem] * 11,
+        in_specs=[vmem] * 7 + [hbm] + [vmem] * 3,
         out_specs=[vmem] * 13,
         out_shape=[
             jax.ShapeDtypeStruct((share, depth), BF16),
@@ -1020,19 +1066,44 @@
         scratch_shapes=[
             V((slots, rows, VAUG), BF16), V((slots, HD, rows), BF16), V((slots, HD, rows), BF16),
             V((slots, rows, HD), F32), V((slots, HD, rows), F32), V((slots, HD, rows), F32),
-            V((rows, cols), BF16), V((4, share, depth), BF16), V((5, share, depth), BF16),
+            V((share, cols), BF16), V((4, share, depth), BF16), V((5, share, depth), BF16),
             V((4, piece, lanes), BF16), V((4, piece, lanes), BF16), V((4, 2, piece, lanes), BF16),
             V((4, piece, lanes), BF16), V((4, piece, lanes), BF16),
             V((8, piece, cols), BF16), V((7, piece, cols), BF16),
             V((8, cols), F32), V((8, 8, cols), F32), V((5,) + small.shape, F32), V((5,) + small.shape, F32),
             dma((4,)), dma((5,)), dma((4,)), dma((4,)), dma((4, 2)), dma((4, 2)), dma((4,)), dma((4,)),
             dma((7,)), dma((7,)), dma((7,)), dma((7,)), dma((5,)), dma((5,)), V(small.shape, F32),
+            V((share, depth), BF16), dma((1,)), V((depth, cols), F32),
         ],
         compiler_params=pltpu.CompilerParams(
-            collective_id=3, has_side_effects=True, vmem_limit_bytes=31 << 20
+            collective_id=3, has_side_effects=True, vmem_limit_bytes=36 << 20
         ),
         name="back_pass",
     )(qs, ka, va, kk, mixed, up, sums, frames, wq, one_grad, small)
+
+
+def deliver_kernel(count, *refs):
+    sources, results, sem = refs[:count], refs[count : 2 * count], refs[2 * count]
+    copies = [
+        pltpu.make_async_copy(a, b, sem.at[i]) for i, (a, b) in enumerate(zip(sources, results))
+    ]
+    for copy in copies:
+        copy.start()
+    for copy in copies:
+        copy.wait()
+
+
+def deliver(arrays):
+    count = len(arrays)
+    return pl.pallas_call(
+        functools.partial(deliver_kernel, count),
+        in_specs=[pl.BlockSpec(memory_space=pltpu.VMEM)] * count,
+        out_specs=[pl.BlockSpec(memory_space=pltpu.MemorySpace.HBM)] * count,
+        out_shape=[jax.ShapeDtypeStruct(a.shape, a.dtype) for a in arrays],
+        scratch_shapes=[pltpu.SemaphoreType.DMA((count,))],
+        compiler_params=pltpu.CompilerParams(vmem_limit_bytes=4 << 20),
+        name="deliver",
+    )(*arrays)
 
 
 def body(
@@ -1053,19 +1124,15 @@
     live_count = HEADS // mp_size + (mp_index < HEADS % mp_size).astype(jnp.int32)
     live = (jnp.arange(slots) < live_count).astype(F32)
 
+    in_hbm = lambda a: pltpu.with_memory_space_constraint(a, pltpu.MemorySpace.HBM)
     out_flip = out_weight.T
     down_flip = down_weight.T
-    wide = lambda v: jnp.pad(v, (0, HALF - v.shape[0]))
-    vectors = jnp.stack(
-        [
-            out_bias, gain_one, shift_one, down_bias, gain_two, shift_two, wide(up_bias),
-            wide(qkv_bias[0]), wide(qkv_bias[1]),
-        ]
-    )
+    vectors = (out_bias, gain_one, shift_one, down_bias, gain_two, shift_two)
     linked = (dp_size, mp_size, slots, rows) == (8, 4, 3, 2048)
     if linked:
         weights, qkv_full, ub_full, qs, ka, va, kk, mixed, got = front(
-            frames, qkv_weight, up_weight, down_flip, out_flip, vectors, seg_ids, slots
+            *map(in_hbm, (frames, qkv_weight, up_weight, down_flip, out_flip)), up_bias, qkv_bias,
+            seg_ids, slots,
         )
         weights = weights.reshape(mp_size, depth, -1)
     else:
@@ -1085,12 +1152,13 @@
         sent = mixed_low.reshape(slots, mp_size, share, HD).transpose(1, 2, 0, 3)
         got = lax.all_to_all(sent.reshape(mp_size, share, width), "mp", 0, 0, tiled=True)
     output_frames, sum_one_grad, back, partial, small = middle(
-        frames, cotangent, got, weights, ub_full, vectors, hidden_cols, linked
+        in_hbm(frames), in_hbm(cotangent), got, weights, ub_full, vectors, hidden_cols, linked
     )
     if linked:
         made = back_pass(
-            qs, ka, va, kk, mixed, back, partial, frames, qkv_full, sum_one_grad, small, hidden_cols
-        )
+            qs, ka, va, kk, mixed, back, partial, in_hbm(frames), qkv_full, sum_one_grad, small, hidden_cols
+        )
+        output_frames, *made = deliver([output_frames, *made])
         return (
             output_frames, made[0], made[1], made[2], made[5].T, made[7], made[8], made[9], made[3],
             made[6], made[4].T, made[10], made[11], made[12],
@@ -1101,6 +1169,7 @@
         partial = lax.psum_scatter(partial, "dp", scatter_dimension=1, tiled=True)
         partial = lax.psum_scatter(partial, "mp", scatter_dimension=0, tiled=True)[0].astype(F32)
         small = lax.psum(small, ("dp", "mp"))
+        kk = kk.reshape(rows, slots, HD).transpose(1, 0, 2)
         dq, dk, dv = attend_back(qs, ka, va, kk, mixed, back)
         grads_low = jnp.stack([dq, dk, dv]).transpose(2, 0, 1, 3).reshape(rows, 3 * width)
         bias_sums = lax.psum(jnp.sum(grads_low.astype(F32), 0), "dp")

time: 211 us -> 182 us (0.86)
  local copies, waits for them, and re-layouts: 38.4 us -> 3.85 us
  Pallas kernels: 171 us -> 177 us
    unnamed x54 -> x20, local copies, waits for them, and re-layouts: 32.8 us -> 3.85 us
    another operation x10 -> x0, local copies, waits for them, and re-layouts: 4.2 us -> none  [body(): jnp.stack([out_bias, gain_one, shift_one, down_bias, gain_two, shift_two,...]
    pallas_call x1 -> x2, Pallas kernels: 57.2 us -> 60.1 us  [the longest x1 58.6 us: front(): pl.pallas_call(functools.partial(front_kernel, slots, sub), in_specs=[hbm...]
where the time goes in v3:
time: 182 us
  Pallas kernels  177 us (97%)
  local copies, waits for them, and re-layouts  3.85 us (2%)
    pallas_call x1, Pallas kernels, back_pass(): pl.pallas_call(functools.partial(back_kernel, slots, min(512, share)), in...  87.1 us
    pallas_call x1, Pallas kernels, front(): pl.pallas_call(functools.partial(front_kernel, slots, sub), in_specs=[hbm...  58.6 us
    pallas_call x1, Pallas kernels, middle(): pl.pallas_call(functools.partial(middle_kernel, groups, hidden_cols, bloc...  29.6 us
    unnamed x20, local copies, waits for them, and re-layouts  3.85 us

profile of v3, /device:TPU:0, one launch (start us, length us, event | category | flops | bytes accessed | tf_op | source)
XLA Modules:
  0.0 181.6 jit_solution(4653202646858574860)
XLA Ops:
  0.7 0.0 copy-start.3
  0.7 0.0 copy-start.1
  0.7 0.7 copy-done.1
  1.4 0.0 copy-start.2
  1.4 0.7 copy-done.2
  2.1 0.0 copy-start.9
  2.1 0.7 copy-done.9
  2.7 0.0 copy-start.4
  2.7 0.0 copy-start.5
  2.7 0.0 copy-start.6
  2.7 0.0 copy-start.7
  2.7 0.0 copy-start.8
  2.8 58.6 %front.1 = (bf16[4,8,80,1408]{3,2,1,0:T(8,128)(2,1)S(1)}, bf16[640,576]{1,0:T(8,128)(2,1)S(1)}, f32[4,1,640]{2,1,0:T(1,128)S(1)}, bf16[3,2048,256]{2,1,0:T(8,128...) custom-call(bf16[2048,640]{1,0:T(8,128)(2,1)} %x_hbm.3, ...), custom_call_target="tpu_custom_call" | custom-call | tf_op jit(solution)/shard_map/front/pallas_call | solution.py:341
  61.4 0.0 copy-done.3
  61.4 0.0 copy-done.4
  61.4 0.0 copy-done.5
  61.4 0.0 copy-done.6
  61.4 0.0 copy-done.7
  61.4 0.0 copy-done.8
  61.5 29.6 %middle.1 = (bf16[512,640]{1,0:T(8,128)(2,1)S(1)}, f32[512,640]{1,0:T(8,128)S(1)}, bf16[4,2,384,128]{3,2,1,0:T(8,128)(2,1)S(1)}, bf16[4,4,80,1408]{3,2,1,0:T(8,128)(2,1)S(1)}, f32[16,640]{1,0:T(8,128)S(1)}) custom-call(bf16[2048,640]{1,0:T(8,128)(2,1)} %x_hbm.3, bf16[2048,640]{1,0:T(8,128)(2,1)} %y_ref.1, ...), custom_call_target="tpu_custom_call" | custom-call | tf_op jit(solution)/shard_map/middle/pallas_call | solution.py:713
  91.1 0.0 copy-start
  91.1 1.8 copy-done
  92.9 87.1 %back_pass.1 = (bf16[512,640]{1,0:T(8,128)(2,1)S(1)}, f32[3,80,192]{2,1,0:T(8,128)S(1)}, f32[2,192]{1,0:T(2,128)S(1)}, f32[80,560]{1,0:T(8,128)S(1)}, f32[80,560...) custom-call(bf16[3,2048,256]{2,1,0:T(8,128)(2,1)S(1)} %get-tuple-ele, ...), custom_call_target="tpu_custom_call" | custom-call | tf_op jit(solution)/shard_map/back_pass/pallas_call | solution.py:1052
  180.0 1.4 deliver.1
Async XLA Ops:
  0.7 60.7 %copy-start.3 = (f32[640]{0:T(1024)S(1)}, f32[640]{0:T(1024)}, u32[]{:S(2)}) copy-start(f32[640]{0:T(1024)} %v0.1) | copy-start | bytes 7684
  0.7 0.7 copy-start.1
  1.4 0.7 copy-start.2
  2.1 0.7 copy-start.9
  2.7 58.7 %copy-start.4 = (f32[640]{0:T(1024)S(1)}, f32[640]{0:T(1024)}, u32[]{:S(2)}) copy-start(f32[640]{0:T(1024)} %v1.1) | copy-start | bytes 7684
  2.7 58.7 %copy-start.5 = (f32[640]{0:T(1024)S(1)}, f32[640]{0:T(1024)}, u32[]{:S(2)}) copy-start(f32[640]{0:T(1024)} %v2.1) | copy-start | bytes 7684
  2.7 58.7 %copy-start.6 = (f32[640]{0:T(1024)S(1)}, f32[640]{0:T(1024)}, u32[]{:S(2)}) copy-start(f32[640]{0:T(1024)} %v3.1) | copy-start | bytes 7684
  2.7 58.7 %copy-start.7 = (f32[640]{0:T(1024)S(1)}, f32[640]{0:T(1024)}, u32[]{:S(2)}) copy-start(f32[640]{0:T(1024)} %v4.1) | copy-start | bytes 7684
  2.7 58.7 %copy-start.8 = (f32[640]{0:T(1024)S(1)}, f32[640]{0:T(1024)}, u32[]{:S(2)}) copy-start(f32[640]{0:T(1024)} %v5.1) | copy-start | bytes 7684
  91.1 1.8 copy-start

commit v4 on v3

--- a/solution.py
+++ b/solution.py
@@ -219,6 +219,7 @@
         arrive(3)
         inner_lifts[2].start()
 
+    start_weights(1)
 
     loads[4].wait()
     block = 256
@@ -243,17 +244,17 @@
         inner_lifts[3].start()
 
     pass_weights(0)
-    start_weights(1)
+    start_weights(2)
 
     live_count = HEADS // 4 + (mp < HEADS % 4).astype(jnp.int32)
     per_share = share // sub
     actions = {
-        1: [(start_weights, 2), (last_weights, 0)],
-        2: [(pass_weights, 1)],
-        3: [(start_weights, 3), (last_weights, 1)],
-        4: [(pass_weights, 2)],
-        5: [(last_weights, 2)],
-        6: [(pass_weights, 3)],
+        1: [(pass_weights, 1)],
+        2: [(start_weights, 3)],
+        4: [(last_weights, 0)],
+        5: [(pass_weights, 2)],
+        6: [(last_weights, 1)],
+        7: [(pass_weights, 3)],
     }
 
     def send_rows(step, stage_index):
@@ -303,6 +304,7 @@
         stage.at[pl.ds(3 * per_share, per_share)], got_ref.at[mp], here.at[3]
     )
     keep.start()
+    last_weights(2)
     last_weights(3)
     for s in range(4):
         weights(s, 2).wait_recv()
@@ -515,7 +517,7 @@
     x_ref, y_ref, got_ref, w_ref, ub_ref, v0, v1, v2, v3, v4, v5,
     out_ref, s1_ref, back_ref, grad_ref, small_ref, *scratch,
 ):
-    x_own, y_own, ow, act, pre_low, slope, hid_low, two_low, one_low, here = scratch[:10]
+    x_own, y_own, ow, act, pre_low, slope, hid_flip, two_flip, one_flip, here = scratch[:10]
     share = out_ref.shape[0]
     width = ow.shape[2]
     gap = HALF - hidden_cols
@@ -565,7 +567,7 @@
         normed_one, factor_one = norm_forward(summed)
         hidden = normed_one * gain_one + shift_one
         hidden_low = hidden.astype(BF16)
-        hid_low[part, :] = hidden_low
+        hid_flip[:, part] = hidden_low.T
         feed = hidden + down_bias
         for g in range(groups):
             pre = jnp.dot(hidden_low, w_ref[g, :, :HALF], preferred_element_type=F32) + ub_ref[g]
@@ -582,7 +584,7 @@
         upstream = y_own[part, :].astype(F32)
         two_grad = norm_backward(upstream, normed_two, factor_two, gain_two)
         sum_two = two_grad.astype(BF16)
-        two_low[part, :] = sum_two
+        two_flip[:, part] = sum_two.T
         hidden_grad = two_grad
         for g in range(groups):
             act_grad = jnp.dot(
@@ -597,7 +599,7 @@
         one_grad = norm_backward(hidden_grad, normed_one, factor_one, gain_one)
         sum_one = one_grad.astype(BF16)
         s1_ref[part, :] = one_grad
-        one_low[part, :] = sum_one
+        one_flip[:, part] = sum_one.T
         for g in range(groups):
             made = jnp.dot(sum_one, ow[g], preferred_element_type=F32)
             made = jnp.where(alive[g], made, 0.0).astype(BF16)
@@ -619,7 +621,7 @@
     if linked:
         keep = pltpu.make_async_copy(back_own.at[mp], back_ref.at[mp], here.at[2])
         keep.start()
-    depth = hid_low.shape[1]
+    depth = hid_flip.shape[0]
     rest = width - gap
     spare = w_ref.shape[2] - HALF - hidden_cols - rest
     span = depth // 2
@@ -627,16 +629,10 @@
     for g in range(groups):
         for part in range(2):
             cols = slice(part * span, (part + 1) * span)
-            made = lax.dot_general(
-                hid_low[:, cols], pre_low[g], TN, preferred_element_type=F32
-            ).astype(BF16)
-            grad_out = lax.dot_general(
-                one_low[:, cols], got[g], TN, preferred_element_type=F32
-            ).astype(BF16)
+            made = jnp.dot(hid_flip[cols], pre_low[g], preferred_element_type=F32).astype(BF16)
+            grad_out = jnp.dot(one_flip[cols], got[g], preferred_element_type=F32).astype(BF16)
             left = jnp.concatenate([made[:, :hidden_cols], grad_out[:, :gap]], 1)
-            made = lax.dot_general(
-                two_low[:, cols], act[g], TN, preferred_element_type=F32
-            ).astype(BF16)
+            made = jnp.dot(two_flip[cols], act[g], preferred_element_type=F32).astype(BF16)
             right = jnp.concatenate(
                 [made[:, :hidden_cols], grad_out[:, gap:], jnp.zeros((span, spare), BF16)], 1
             )
@@ -692,9 +688,9 @@
         pltpu.VMEM((groups, share, HALF), BF16),
         pltpu.VMEM((groups, share, HALF), BF16),
         pltpu.VMEM((groups, block, HALF), F32),
-        pltpu.VMEM((share, depth), BF16),
-        pltpu.VMEM((share, depth), BF16),
-        pltpu.VMEM((share, depth), BF16),
+        pltpu.VMEM((depth, share), BF16),
+        pltpu.VMEM((depth, share), BF16),
+        pltpu.VMEM((depth, share), BF16),
         dma((3,)),
     ]
     grads = jax.ShapeDtypeStruct(weights.shape, BF16)
@@ -883,8 +879,10 @@
     dv_acc[...] = jnp.zeros_like(dv_acc)
     gq_acc[...] = jnp.zeros_like(gq_acc)
     gb_own[...] = jnp.zeros_like(gb_own)
-    begin_grads(3)
-    begin_grads(2)
+    far(3).start()
+    far(2).start()
+    near(3, 0).start()
+    near(2, 0).start()
     small_step(0)
 
     def prepare(step, carry):
@@ -906,13 +904,14 @@
     lax.fori_loop(0, 4, prepare, 0)
     actions = {
         1: [(small_step, 1)],
-        2: [(begin_grads, 1), (small_step, 2)],
-        3: [(join_far, 3), (begin_grads, 0), (small_step, 3)],
-        4: [(join_far, 2), (small_step, 4)],
+        2: [(join_far, 3), (join_far, 2), (small_step, 2)],
+        3: [(begin_grads, 1), (small_step, 3)],
+        4: [(begin_grads, 0), (small_step, 4)],
         5: [(join_near, 3), (small_step, 5)],
-        7: [(join_near, 2), (join_far, 1)],
+        6: [(join_near, 2)],
+        8: [(join_far, 1)],
         9: [(join_far, 0)],
-        11: [(join_near, 1)],
+        12: [(join_near, 1)],
         13: [(join_near, 0)],
     }
 
@@ -1076,7 +1075,7 @@
             V((share, depth), BF16), dma((1,)), V((depth, cols), F32),
         ],
         compiler_params=pltpu.CompilerParams(
-            collective_id=3, has_side_effects=True, vmem_limit_bytes=36 << 20
+            collective_id=3, has_side_effects=True, vmem_limit_bytes=34 << 20
         ),
         name="back_pass",
     )(qs, ka, va, kk, mixed, up, sums, frames, wq, one_grad, small)

time: 182 us -> 169 us (0.929)
  Pallas kernels: 177 us -> 166 us
    pallas_call x1, Pallas kernels: 58.6 us -> 50.9 us  [front(): pl.pallas_call(functools.partial(front_kernel, slots, sub), in_specs=[hbm...]
    pallas_call x1, Pallas kernels: 87.1 us -> 84.2 us  [back_pass(): pl.pallas_call(functools.partial(back_kernel, slots, min(512, share)), in...]
    unnamed x20 -> x18, local copies, waits for them, and re-layouts: 3.85 us -> 2.09 us
where the time goes in v4:
time: 169 us
  Pallas kernels  166 us (98%)
  local copies, waits for them, and re-layouts  2.09 us (1%)
    pallas_call x1, Pallas kernels, back_pass(): pl.pallas_call(functools.partial(back_kernel, slots, min(512, share)), in...  84.2 us
    pallas_call x1, Pallas kernels, front(): pl.pallas_call(functools.partial(front_kernel, slots, sub), in_specs=[hbm...  50.9 us
    pallas_call x1, Pallas kernels, middle(): pl.pallas_call(functools.partial(middle_kernel, groups, hidden_cols, bloc...  29.2 us

profile of v4, /device:TPU:0, one launch (start us, length us, event | category | flops | bytes accessed | tf_op | source)
XLA Modules:
  0.0 168.7 jit_solution(12394276110519959638)
XLA Ops:
  0.7 0.0 copy-start.2
  0.7 0.0 copy-start
  0.7 0.7 copy-done
  1.4 0.0 copy-start.1
  1.4 0.7 copy-done.1
  2.1 0.0 copy-start.8
  2.1 0.7 copy-done.8
  2.7 0.0 copy-start.3
  2.7 0.0 copy-start.4
  2.7 0.0 copy-start.5
  2.7 0.0 copy-start.6
  2.7 0.0 copy-start.7
  2.8 50.9 %front.1 = (bf16[4,8,80,1408]{3,2,1,0:T(8,128)(2,1)S(1)}, bf16[640,576]{1,0:T(8,128)(2,1)S(1)}, f32[4,1,640]{2,1,0:T(1,128)S(1)}, bf16[3,2048,256]{2,1,0:T(8,128...) custom-call(bf16[2048,640]{1,0:T(8,128)(2,1)} %x_hbm.3, ...), custom_call_target="tpu_custom_call" | custom-call | tf_op jit(solution)/shard_map/front/pallas_call | solution.py:343
  53.7 0.0 copy-done.2
  53.7 0.0 copy-done.3
  53.7 0.0 copy-done.4
  53.7 0.0 copy-done.5
  53.7 0.0 copy-done.6
  53.7 0.0 copy-done.7
  53.7 29.2 %middle.1 = (bf16[512,640]{1,0:T(8,128)(2,1)S(1)}, f32[512,640]{1,0:T(8,128)S(1)}, bf16[4,2,384,128]{3,2,1,0:T(8,128)(2,1)S(1)}, bf16[4,4,80,1408]{3,2,1,0:T(8,128)(2,1)S(1)}, f32[16,640]{1,0:T(8,128)S(1)}) custom-call(bf16[2048,640]{1,0:T(8,128)(2,1)} %x_hbm.3, bf16[2048,640]{1,0:T(8,128)(2,1)} %y_ref.1, ...), custom_call_target="tpu_custom_call" | custom-call | tf_op jit(solution)/shard_map/middle/pallas_call | solution.py:709
  82.9 84.2 %back_pass.1 = (bf16[512,640]{1,0:T(8,128)(2,1)S(1)}, f32[3,80,192]{2,1,0:T(8,128)S(1)}, f32[2,192]{1,0:T(2,128)S(1)}, f32[80,560]{1,0:T(8,128)S(1)}, f32[80,560...) custom-call(bf16[3,2048,256]{2,1,0:T(8,128)(2,1)S(1)} %get-tuple-ele, ...), custom_call_target="tpu_custom_call" | custom-call | tf_op jit(solution)/shard_map/back_pass/pallas_call | solution.py:1051
  167.1 1.4 deliver.1
Async XLA Ops:
  0.7 53.0 %copy-start.2 = (f32[640]{0:T(1024)S(1)}, f32[640]{0:T(1024)}, u32[]{:S(2)}) copy-start(f32[640]{0:T(1024)} %v0.1) | copy-start | bytes 7684
  0.7 0.7 copy-start
  1.4 0.7 copy-start.1
  2.1 0.7 copy-start.8
  2.7 51.0 %copy-start.3 = (f32[640]{0:T(1024)S(1)}, f32[640]{0:T(1024)}, u32[]{:S(2)}) copy-start(f32[640]{0:T(1024)} %v1.1) | copy-start | bytes 7684
  2.7 51.0 %copy-start.4 = (f32[640]{0:T(1024)S(1)}, f32[640]{0:T(1024)}, u32[]{:S(2)}) copy-start(f32[640]{0:T(1024)} %v2.1) | copy-start | bytes 7684
  2.7 51.0 %copy-start.5 = (f32[640]{0:T(1024)S(1)}, f32[640]{0:T(1024)}, u32[]{:S(2)}) copy-start(f32[640]{0:T(1024)} %v3.1) | copy-start | bytes 7684
  2.7 51.0 %copy-start.6 = (f32[640]{0:T(1024)S(1)}, f32[640]{0:T(1024)}, u32[]{:S(2)}) copy-start(f32[640]{0:T(1024)} %v4.1) | copy-start | bytes 7684
  2.7 51.0 %copy-start.7 = (f32[640]{0:T(1024)S(1)}, f32[640]{0:T(1024)}, u32[]{:S(2)}) copy-start(f32[640]{0:T(1024)} %v5.1) | copy-start | bytes 7684

commit v5 on v4

--- a/solution.py
+++ b/solution.py
@@ -222,7 +222,7 @@
     start_weights(1)
 
     loads[4].wait()
-    block = 256
+    block = 512
 
     def project_rows(step, carry):
         part = pl.ds(pl.multiple_of(step * block, block), block)
@@ -250,7 +250,7 @@
     per_share = share // sub
     actions = {
         1: [(pass_weights, 1)],
-        2: [(start_weights, 3)],
+        3: [(start_weights, 3)],
         4: [(last_weights, 0)],
         5: [(pass_weights, 2)],
         6: [(last_weights, 1)],
@@ -276,10 +276,12 @@
                     act(s)
 
         kept = []
+        scores = [
+            lax.dot_general(qs_ref[slot, part, :], ka_ref[slot], NT, preferred_element_type=F32)
+            for slot in range(slots)
+        ]
         for slot in range(slots):
-            x = lax.dot_general(
-                qs_ref[slot, part, :], ka_ref[slot], NT, preferred_element_type=F32
-            )
+            x = scores[slot]
             top = jnp.max(x, -1, keepdims=True)
             p = jnp.exp2(x - top).astype(BF16)
             made = jnp.dot(p, va_ref[slot], preferred_element_type=F32)
@@ -569,15 +571,20 @@
         hidden_low = hidden.astype(BF16)
         hid_flip[:, part] = hidden_low.T
         feed = hidden + down_bias
+        dots = [
+            jnp.dot(hidden_low, w_ref[g, :, :HALF], preferred_element_type=F32)
+            for g in range(groups)
+        ]
         for g in range(groups):
-            pre = jnp.dot(hidden_low, w_ref[g, :, :HALF], preferred_element_type=F32) + ub_ref[g]
+            pre = dots[g] + ub_ref[g]
             half = 0.5 + 0.5 * lax.erf(pre * math.sqrt(0.5))
             bell = jnp.exp(pre * pre * -0.5) * (pre * (1.0 / math.sqrt(2.0 * math.pi)))
             slope[g] = jnp.where(real, half + bell, 0.0)
             made = jnp.where(real, pre * half, 0.0).astype(BF16)
             act[g, part, :] = made
+        for g in range(groups):
             feed += lax.dot_general(
-                made, w_ref[g, :, HALF : 2 * HALF], NT, preferred_element_type=F32
+                act[g, part, :], w_ref[g, :, HALF : 2 * HALF], NT, preferred_element_type=F32
             )
         normed_two, factor_two = norm_forward(feed)
         out_ref[part, :] = (normed_two * gain_two + shift_two).astype(BF16)
@@ -586,16 +593,18 @@
         sum_two = two_grad.astype(BF16)
         two_flip[:, part] = sum_two.T
         hidden_grad = two_grad
+        dots = [
+            jnp.dot(sum_two, w_ref[g, :, HALF : 2 * HALF], preferred_element_type=F32)
+            for g in range(groups)
+        ]
         for g in range(groups):
-            act_grad = jnp.dot(
-                sum_two, w_ref[g, :, HALF : 2 * HALF], preferred_element_type=F32
+            low = (slope[g] * dots[g]).astype(BF16)
+            pre_low[g, part, :] = low
+            small_ref[8 + g : 9 + g, :] += jnp.sum(low.astype(F32), 0, keepdims=True)
+        for g in range(groups):
+            hidden_grad += lax.dot_general(
+                pre_low[g, part, :], w_ref[g, :, :HALF], NT, preferred_element_type=F32
             )
-            low = (slope[g] * act_grad).astype(BF16)
-            pre_low[g, part, :] = low
-            hidden_grad += lax.dot_general(
-                low, w_ref[g, :, :HALF], NT, preferred_element_type=F32
-            )
-            small_ref[8 + g : 9 + g, :] += jnp.sum(low.astype(F32), 0, keepdims=True)
         one_grad = norm_backward(hidden_grad, normed_one, factor_one, gain_one)
         sum_one = one_grad.astype(BF16)
         s1_ref[part, :] = one_grad
@@ -725,11 +734,11 @@
     )(frames, cotangent, got, weights, up_bias, *vectors)
 
 
-PAIRS = (
-    (0, 3), (1, 3), (2, 3), (3, 3), (3, 2), (3, 1), (3, 0), (0, 2), (1, 2), (2, 2), (2, 1), (2, 0),
-    (0, 1), (1, 1), (1, 0), (0, 0),
+STEPS = (
+    (3, 3, 0), (3, 0, 0), (3, 1, 0), (3, 2, 0), (3, 0, 1), (3, 1, 1), (3, 2, 1),
+    (2, 2, 0), (2, 0, 0), (2, 1, 0), (2, 0, 1), (2, 1, 1), (1, 1, 0), (1, 0, 0), (1, 0, 1), (0, 0, 0),
 )
-ENDS = {6: 3, 11: 2, 14: 1, 15: 0}
+ENDS = {3: (3, 0), 6: (3, 1), 9: (2, 0), 11: (2, 1), 13: (1, 0), 14: (1, 1)}
 
 
 def pick(table, step):
@@ -740,11 +749,11 @@
 
 
 def back_kernel(
-    slots, sub,
+    slots,
     qs_ref, ka_ref, va_ref, kk_ref, mixed_ref, up_ref, sums_ref, x_hbm, wq_ref, one_ref, small_ref,
     fg_ref, gq_ref, gb_ref, gup_ref, gdown_ref, gout_ref, gub_ref, s0, s1, s2, s3, s4, s5,
     upper, up_flip, q_flip, dq_acc, dk_acc, dv_acc, low, part_out, chain, fresh, far_in, near_in, third,
-    tall_in, gq_own, gq_in, gb_own, gb_in, tiny, tiny_in,
+    fresh_in, gq_own, gq_in, gb_own, gb_in, tiny, tiny_in,
     c_send, c_recv, f_send, f_recv, n_send, n_recv, t_send, t_recv, q_send, q_recv, b_send, b_recv,
     s_send, s_recv, small_sum, x_ref, loaded, gq_acc,
 ):
@@ -762,10 +771,16 @@
     def rows_of(name):
         return pl.ds(pl.multiple_of((mp ^ name) * share, share), share)
 
-    def load_rows(name):
-        return pltpu.make_async_copy(x_hbm.at[rows_of(name)], x_ref, loaded.at[0])
-
-    load_rows(3).start()
+    half_rows = share // 2
+
+    def half_of(name, half):
+        start = (mp ^ name) * share + half * half_rows
+        return pl.ds(pl.multiple_of(start, half_rows), half_rows)
+
+    def load_rows(name, half):
+        return pltpu.make_async_copy(x_hbm.at[half_of(name, half)], x_ref, loaded.at[0])
+
+    load_rows(3, 0).start()
 
     def far(s):
         return remote(
@@ -781,13 +796,10 @@
             x_peer if toward_x else y_peer,
         )
 
-    def lift(s):
-        return remote(
-            fresh.at[s], tall_in.at[s], t_send.at[s], t_recv.at[s], (dp, mp ^ s)
-        )
-
-    def begin_grads(s):
+    def begin_far(s):
         far(s).start()
+
+    def begin_near(s):
         near(s, 0).start()
 
     def join_far(s):
@@ -800,8 +812,6 @@
         near(s, 1).wait_recv()
         total = sums_ref[mp ^ s, chip].astype(F32) + near_in[s, 0].astype(F32)
         fresh[s] = (total + near_in[s, 1].astype(F32)).astype(BF16)
-        if s > 0:
-            lift(s).start()
 
     partners = [(dp ^ 1, mp), (dp ^ 2, mp), (dp ^ 4, mp), (dp, mp ^ 1), (dp, mp ^ 2)]
 
@@ -824,55 +834,62 @@
             tiny[at] = made
         swap(at).start()
 
-    def chain_copy(name, leftward):
+    def chain_copy(name, half, slot, target):
+        at = pl.ds(half * half_rows, half_rows)
+        return remote(
+            part_out.at[name, at], chain.at[slot, at], c_send.at[name, half], c_recv.at[slot, half],
+            (dp, target),
+        )
+
+    def fresh_copy(name, slot, target):
+        return remote(
+            fresh.at[name], fresh_in.at[slot], t_send.at[name], t_recv.at[slot], (dp, target)
+        )
+
+    inner = (mp == 1) | (mp == 2)
+
+    def relay(name, half):
         block = mp ^ name
-        target = mp - 1 if leftward else mp + 1
-        slot = jnp.where(block == target, 4, block) if leftward else block
-        return remote(
-            part_out.at[name], chain.at[slot], c_send.at[name], c_recv.at[slot], (dp, target)
-        )
-
-    def chain_arrival(slot):
-        return remote(part_out.at[0], chain.at[slot], c_send.at[0], c_recv.at[slot], (dp, mp ^ 1))
-
-    def relay(name):
-        block = mp ^ name
-        inner = (mp == 1) | (mp == 2)
-        waits = inner
-
-        @pl.when(waits)
+        at = pl.ds(half * half_rows, half_rows)
+
+        @pl.when(inner)
         def _():
-            chain_arrival(block).wait_recv()
-            part_out[name] = (
-                part_out[name].astype(F32) + chain[block].astype(F32)
+            chain_copy(name, half, block, mp ^ 1).wait_recv()
+            part_out[name, at] = (
+                part_out[name, at].astype(F32) + chain[block, at].astype(F32)
             ).astype(BF16)
-
-        @pl.when(block < mp)
-        def _():
-            chain_copy(name, True).start()
-
-        @pl.when(block > mp)
-        def _():
-            chain_copy(name, False).start()
-
-    def finish(name):
-        at = rows_of(name)
+            if half == 1:
+                fresh_copy(name, block, mp ^ 1).wait_recv()
+                fresh[name] = (fresh[name].astype(F32) + fresh_in[block].astype(F32)).astype(BF16)
+
+        for leftward in (True, False):
+
+            @pl.when((block < mp) == leftward)
+            def _():
+                target = mp - 1 if leftward else mp + 1
+                slot = jnp.where(block == target, 4, block) if leftward else block
+                chain_copy(name, half, slot, target).start()
+                if half == 1:
+                    fresh_copy(name, slot, target).start()
+
+    def finish(name, half):
+        at = half_of(name, half)
         for slot in range(slots):
             col = slot * HD
             low[:, col : col + HD] = (dq_acc[slot, at, :] * SCALE).astype(BF16)
             low[:, width + col : width + col + HD] = (dk_acc[slot, :, at] * SCALE).T.astype(BF16)
             low[:, 2 * width + col : 2 * width + col + HD] = dv_acc[slot, :, at].T.astype(BF16)
-        part_out[name] = lax.dot_general(
+        part_out[name, half * half_rows : (half + 1) * half_rows] = lax.dot_general(
             low[...], wq_ref[...], NT, preferred_element_type=F32
         ).astype(BF16)
 
-    def add_rows(name):
-        ones = jnp.ones((16, share), BF16)
+    def add_rows(name, half):
+        ones = jnp.ones((16, half_rows), BF16)
         gb_own[...] += jnp.dot(ones, low[...], preferred_element_type=F32)[0:8, :]
-        load_rows(name).wait()
+        load_rows(name, half).wait()
         gq_acc[...] += lax.dot_general(x_ref[...], low[...], TN, preferred_element_type=F32)
-        if name > 0:
-            load_rows(name - 1).start()
+        if (name, half) != (0, 1):
+            load_rows(name - half, 1 - half).start()
 
     dq_acc[...] = jnp.zeros_like(dq_acc)
     dk_acc[...] = jnp.zeros_like(dk_acc)
@@ -881,8 +898,6 @@
     gb_own[...] = jnp.zeros_like(gb_own)
     far(3).start()
     far(2).start()
-    near(3, 0).start()
-    near(2, 0).start()
     small_step(0)
 
     def prepare(step, carry):
@@ -905,20 +920,45 @@
     actions = {
         1: [(small_step, 1)],
         2: [(join_far, 3), (join_far, 2), (small_step, 2)],
-        3: [(begin_grads, 1), (small_step, 3)],
-        4: [(begin_grads, 0), (small_step, 4)],
-        5: [(join_near, 3), (small_step, 5)],
-        6: [(join_near, 2)],
-        8: [(join_far, 1)],
-        9: [(join_far, 0)],
-        12: [(join_near, 1)],
-        13: [(join_near, 0)],
+        3: [(small_step, 3)],
+        4: [(begin_near, 3), (begin_near, 2), (small_step, 4)],
+        5: [(small_step, 5)],
+        6: [(join_near, 3), (join_near, 2)],
+        7: [(begin_far, 1), (begin_far, 0)],
+        9: [(join_far, 1), (join_far, 0)],
+        11: [(begin_near, 1), (begin_near, 0)],
+        13: [(join_near, 1), (join_near, 0)],
     }
 
-    def pair(step, carry):
-        query = mp ^ pick([p[0] for p in PAIRS], step)
-        key = mp ^ pick([p[1] for p in PAIRS], step)
-        keys = pl.ds(pl.multiple_of(key * share, share), share)
+    def tiles(pairs):
+        todo = [(slot, part, keys) for part, keys in pairs for slot in range(slots)]
+        scores = [
+            lax.dot_general(
+                qs_ref[slot, part, :], ka_ref[slot, keys, :], NT, preferred_element_type=F32
+            )
+            for slot, part, keys in todo
+        ]
+        slopes = [
+            lax.dot_general(
+                upper[slot, part, :], va_ref[slot, keys, :], NT, preferred_element_type=F32
+            )
+            for slot, part, keys in todo
+        ]
+        probs = [jnp.exp2(x) for x in scores]
+        lows = [(p * d).astype(BF16) for p, d in zip(probs, slopes)]
+        for (slot, part, keys), p, ds in zip(todo, probs, lows):
+            dv_acc[slot, :, keys] += jnp.dot(
+                up_flip[slot, :, part], p.astype(BF16), preferred_element_type=F32
+            )
+            dk_acc[slot, :, keys] += jnp.dot(
+                q_flip[slot, :, part], ds, preferred_element_type=F32
+            )
+            dq_acc[slot, part, :] += jnp.dot(
+                ds, kk_ref[keys, slot * HD : (slot + 1) * HD], preferred_element_type=F32
+            )
+
+    def some_work(step, carry):
+        name, other, half = (pick([s[i] for s in STEPS], step) for i in range(3))
         for when, todo in actions.items():
 
             @pl.when(step == when)
@@ -926,44 +966,40 @@
                 for act, s in todo:
                     act(s)
 
-        for at in range(0, share, sub):
-            part = pl.ds(pl.multiple_of(query * share + at, sub), sub)
-            for slot in range(slots):
-                x = lax.dot_general(
-                    qs_ref[slot, part, :], ka_ref[slot, keys, :], NT, preferred_element_type=F32
-                )
-                p = jnp.exp2(x)
-                dp_ = lax.dot_general(
-                    upper[slot, part, :], va_ref[slot, keys, :], NT, preferred_element_type=F32
-                )
-                ds = (p * dp_).astype(BF16)
-                dv_acc[slot, :, keys] += jnp.dot(
-                    up_flip[slot, :, part], p.astype(BF16), preferred_element_type=F32
-                )
-                dk_acc[slot, :, keys] += jnp.dot(
-                    q_flip[slot, :, part], ds, preferred_element_type=F32
-                )
-                dq_acc[slot, part, :] += jnp.dot(
-                    ds, kk_ref[keys, slot * HD : (slot + 1) * HD], preferred_element_type=F32
-                )
-        for when, name in ENDS.items():
+        @pl.when(name == other)
+        def _():
+            tiles([(rows_of(name), rows_of(name))])
+
+        @pl.when(name != other)
+        def _():
+            tiles([(half_of(name, half), rows_of(other)), (rows_of(other), half_of(name, half))])
+
+        for when, (n, h) in ENDS.items():
 
             @pl.when(step == when)
             def _():
-                finish(name)
-                if name == 2:
-                    relay(name)
-                elif name > 0:
-
-                    @pl.when((mp == 0) | (mp == 3))
+                finish(n, h)
+                if n == 3:
+
+                    @pl.when(~inner)
                     def _():
-                        relay(name)
-
-                add_rows(name)
+                        relay(n, h)
+
+                else:
+                    relay(n, h)
+                add_rows(n, h)
+
+        @pl.when((step == 14) & inner)
+        def _():
+            relay(3, 0)
 
         return carry
 
-    lax.fori_loop(0, len(PAIRS), pair, 0)
+    lax.fori_loop(0, len(STEPS), some_work, 0)
+    for half in range(2):
+        finish(0, half)
+        add_rows(0, half)
+
     gb_in[dp] = gb_own[...]
     piece = depth // 8
     for d in range(8):
@@ -979,17 +1015,31 @@
         )
     for copy in q_copies:
         copy.start()
-    for name in (3, 1):
-
-        @pl.when((mp == 1) | (mp == 2))
+    @pl.when(inner)
+    def _():
+        relay(3, 1)
+
+    for half in range(2):
+
+        @pl.when(mp > 0)
         def _():
-            relay(name)
-
-    for s in range(1, 4):
-        lift(s).wait_recv()
+            chain_copy(0, half, mp, mp ^ 1).wait_recv()
+
+        @pl.when(mp < 3)
+        def _():
+            chain_copy(0, half, 4, mp ^ 1).wait_recv()
+
+    @pl.when(mp > 0)
+    def _():
+        fresh_copy(0, mp, mp ^ 1).wait_recv()
+
+    @pl.when(mp < 3)
+    def _():
+        fresh_copy(0, 4, mp ^ 1).wait_recv()
+
     total = fresh[0].astype(F32)
-    for s in range(1, 4):
-        total = total + tall_in[s].astype(F32)
+    total = total + jnp.where(mp > 0, fresh_in[mp].astype(F32), 0.0)
+    total = total + jnp.where(mp < 3, fresh_in[4].astype(F32), 0.0)
     cols = gup_ref.shape[1]
     gap = HALF - cols
     gup_ref[...] = total[:, :cols]
@@ -1010,28 +1060,17 @@
     gb_ref[1:2, :] = total[0:1, 2 * width :]
 
     wide = one_ref[...] + part_out[0].astype(F32)
-
-    @pl.when(mp > 0)
-    def _():
-        chain_arrival(mp).wait_recv()
-
-    @pl.when(mp < 3)
-    def _():
-        chain_arrival(4).wait_recv()
-
     left = jnp.where(mp > 0, chain[mp].astype(F32), 0.0)
     right = jnp.where(mp < 3, chain[4].astype(F32), 0.0)
     fg_ref[...] = (wide + left + right).astype(BF16)
     for name in (1, 2, 3):
-        remote(
-            part_out.at[name], chain.at[0], c_send.at[name], c_recv.at[0], (dp, mp ^ 1)
-        ).wait_send()
+        for half in range(2):
+            chain_copy(name, half, 0, mp ^ 1).wait_send()
+        fresh_copy(name, 0, mp ^ 1).wait_send()
     for s in range(4):
         far(s).wait_send()
         near(s, 0).wait_send()
         near(s, 1).wait_send()
-        if s > 0:
-            lift(s).wait_send()
     for at in range(len(partners)):
         swap(at).wait_send()
     for copy in q_copies:
@@ -1049,7 +1088,7 @@
     dma = pltpu.SemaphoreType.DMA
     V = pltpu.VMEM
     return pl.pallas_call(
-        functools.partial(back_kernel, slots, min(512, share)),
+        functools.partial(back_kernel, slots),
         in_specs=[vmem] * 7 + [hbm] + [vmem] * 3,
         out_specs=[vmem] * 13,
         out_shape=[
@@ -1065,14 +1104,14 @@
         scratch_shapes=[
             V((slots, rows, VAUG), BF16), V((slots, HD, rows), BF16), V((slots, HD, rows), BF16),
             V((slots, rows, HD), F32), V((slots, HD, rows), F32), V((slots, HD, rows), F32),
-            V((share, cols), BF16), V((4, share, depth), BF16), V((5, share, depth), BF16),
+            V((share // 2, cols), BF16), V((4, share, depth), BF16), V((5, share, depth), BF16),
             V((4, piece, lanes), BF16), V((4, piece, lanes), BF16), V((4, 2, piece, lanes), BF16),
-            V((4, piece, lanes), BF16), V((4, piece, lanes), BF16),
+            V((4, piece, lanes), BF16), V((5, piece, lanes), BF16),
             V((8, piece, cols), BF16), V((7, piece, cols), BF16),
             V((8, cols), F32), V((8, 8, cols), F32), V((5,) + small.shape, F32), V((5,) + small.shape, F32),
-            dma((4,)), dma((5,)), dma((4,)), dma((4,)), dma((4, 2)), dma((4, 2)), dma((4,)), dma((4,)),
+            dma((4, 2)), dma((5, 2)), dma((4,)), dma((4,)), dma((4, 2)), dma((4, 2)), dma((4,)), dma((5,)),
             dma((7,)), dma((7,)), dma((7,)), dma((7,)), dma((5,)), dma((5,)), V(small.shape, F32),
-            V((share, depth), BF16), dma((1,)), V((depth, cols), F32),
+            V((share // 2, depth), BF16), dma((1,)), V((depth, cols), F32),
         ],
         compiler_params=pltpu.CompilerParams(
             collective_id=3, has_side_effects=True, vmem_limit_bytes=34 << 20

time: 169 us -> 165 us (0.976); the launches traced: 169 us -> 162 us
  Pallas kernels: 166 us -> 159 us
    pallas_call x1, Pallas kernels: 84.2 us -> 81.1 us  [back_pass(): pl.pallas_call(functools.partial(back_kernel, slots), in_specs=[vmem] * 7...]
    pallas_call x1, Pallas kernels: 50.9 us -> 47.9 us  [front(): pl.pallas_call(functools.partial(front_kernel, slots, sub), in_specs=[hbm...]
where the time goes in v5:
time: 165 us; the launch traced here: 162 us
  Pallas kernels  159 us (96%)
  local copies, waits for them, and re-layouts  2.09 us (1%)
    pallas_call x1, Pallas kernels, back_pass(): pl.pallas_call(functools.partial(back_kernel, slots), in_specs=[vmem] * 7...  81.1 us
    pallas_call x1, Pallas kernels, front(): pl.pallas_call(functools.partial(front_kernel, slots, sub), in_specs=[hbm...  47.9 us
    pallas_call x1, Pallas kernels, middle(): pl.pallas_call(functools.partial(middle_kernel, groups, hidden_cols, bloc...  29 us

profile of v5, /device:TPU:0, one launch (start us, length us, event | category | flops | bytes accessed | tf_op | source)
XLA Modules:
  0.0 162.5 jit_solution(7533633434523722002)
XLA Ops:
  0.7 0.0 copy-start.2
  0.7 0.0 copy-start
  0.7 0.7 copy-done
  1.4 0.0 copy-start.1
  1.4 0.7 copy-done.1
  2.1 0.0 copy-start.8
  2.1 0.7 copy-done.8
  2.7 0.0 copy-start.3
  2.7 0.0 copy-start.4
  2.7 0.0 copy-start.5
  2.7 0.0 copy-start.6
  2.7 0.0 copy-start.7
  2.8 47.9 %front.1 = (bf16[4,8,80,1408]{3,2,1,0:T(8,128)(2,1)S(1)}, bf16[640,576]{1,0:T(8,128)(2,1)S(1)}, f32[4,1,640]{2,1,0:T(1,128)S(1)}, bf16[3,2048,256]{2,1,0:T(8,128...) custom-call(bf16[2048,640]{1,0:T(8,128)(2,1)} %x_hbm.3, ...), custom_call_target="tpu_custom_call" | custom-call | tf_op jit(solution)/shard_map/front/pallas_call | solution.py:345
  50.7 0.0 copy-done.2
  50.7 0.0 copy-done.3
  50.7 0.0 copy-done.4
  50.7 0.0 copy-done.5
  50.7 0.0 copy-done.6
  50.7 0.0 copy-done.7
  50.7 29.0 %middle.1 = (bf16[512,640]{1,0:T(8,128)(2,1)S(1)}, f32[512,640]{1,0:T(8,128)S(1)}, bf16[4,2,384,128]{3,2,1,0:T(8,128)(2,1)S(1)}, bf16[4,4,80,1408]{3,2,1,0:T(8,128)(2,1)S(1)}, f32[16,640]{1,0:T(8,128)S(1)}) custom-call(bf16[2048,640]{1,0:T(8,128)(2,1)} %x_hbm.3, bf16[2048,640]{1,0:T(8,128)(2,1)} %y_ref.1, ...), custom_call_target="tpu_custom_call" | custom-call | tf_op jit(solution)/shard_map/middle/pallas_call | solution.py:718
  79.7 81.1 %back_pass.1 = (bf16[512,640]{1,0:T(8,128)(2,1)S(1)}, f32[3,80,192]{2,1,0:T(8,128)S(1)}, f32[2,192]{1,0:T(2,128)S(1)}, f32[80,560]{1,0:T(8,128)S(1)}, f32[80,560...) custom-call(bf16[3,2048,256]{2,1,0:T(8,128)(2,1)S(1)} %get-tuple-ele, ...), custom_call_target="tpu_custom_call" | custom-call | tf_op jit(solution)/shard_map/back_pass/pallas_call | solution.py:1090
  160.8 1.4 deliver.1
Async XLA Ops:
  0.7 50.0 %copy-start.2 = (f32[640]{0:T(1024)S(1)}, f32[640]{0:T(1024)}, u32[]{:S(2)}) copy-start(f32[640]{0:T(1024)} %v0.1) | copy-start | bytes 7684
  0.7 0.7 copy-start
  1.4 0.7 copy-start.1
  2.1 0.7 copy-start.8
  2.7 47.9 %copy-start.3 = (f32[640]{0:T(1024)S(1)}, f32[640]{0:T(1024)}, u32[]{:S(2)}) copy-start(f32[640]{0:T(1024)} %v1.1) | copy-start | bytes 7684
  2.7 47.9 %copy-start.4 = (f32[640]{0:T(1024)S(1)}, f32[640]{0:T(1024)}, u32[]{:S(2)}) copy-start(f32[640]{0:T(1024)} %v2.1) | copy-start | bytes 7684
  2.7 48.0 %copy-start.5 = (f32[640]{0:T(1024)S(1)}, f32[640]{0:T(1024)}, u32[]{:S(2)}) copy-start(f32[640]{0:T(1024)} %v3.1) | copy-start | bytes 7684
  2.7 48.0 %copy-start.6 = (f32[640]{0:T(1024)S(1)}, f32[640]{0:T(1024)}, u32[]{:S(2)}) copy-start(f32[640]{0:T(1024)} %v4.1) | copy-start | bytes 7684
  2.7 48.0 %copy-start.7 = (f32[640]{0:T(1024)S(1)}, f32[640]{0:T(1024)}, u32[]{:S(2)}) copy-start(f32[640]{0:T(1024)} %v5.1) | copy-start | bytes 7684

commit v6 on v5

--- a/solution.py
+++ b/solution.py
@@ -848,6 +848,14 @@
 
     inner = (mp == 1) | (mp == 2)
 
+    def down_the_chain(block, copy):
+        for leftward in (True, False):
+
+            @pl.when((block < mp) == leftward)
+            def _():
+                target = mp - 1 if leftward else mp + 1
+                copy(jnp.where(block == target, 4, block) if leftward else block, target).start()
+
     def relay(name, half):
         block = mp ^ name
         at = pl.ds(half * half_rows, half_rows)
@@ -858,19 +866,28 @@
             part_out[name, at] = (
                 part_out[name, at].astype(F32) + chain[block, at].astype(F32)
             ).astype(BF16)
-            if half == 1:
-                fresh_copy(name, block, mp ^ 1).wait_recv()
-                fresh[name] = (fresh[name].astype(F32) + fresh_in[block].astype(F32)).astype(BF16)
-
-        for leftward in (True, False):
-
-            @pl.when((block < mp) == leftward)
-            def _():
-                target = mp - 1 if leftward else mp + 1
-                slot = jnp.where(block == target, 4, block) if leftward else block
-                chain_copy(name, half, slot, target).start()
-                if half == 1:
-                    fresh_copy(name, slot, target).start()
+
+        down_the_chain(block, functools.partial(chain_copy, name, half))
+
+    def relay_fresh(name):
+        block = mp ^ name
+
+        @pl.when(inner)
+        def _():
+            fresh_copy(name, block, mp ^ 1).wait_recv()
+            fresh[name] = (fresh[name].astype(F32) + fresh_in[block].astype(F32)).astype(BF16)
+
+        down_the_chain(block, functools.partial(fresh_copy, name))
+
+    def end_fresh(name):
+        @pl.when(~inner)
+        def _():
+            relay_fresh(name)
+
+    def inner_fresh(name):
+        @pl.when(inner)
+        def _():
+            relay_fresh(name)
 
     def finish(name, half):
         at = half_of(name, half)
@@ -918,16 +935,17 @@
 
     lax.fori_loop(0, 4, prepare, 0)
     actions = {
-        1: [(small_step, 1)],
-        2: [(join_far, 3), (join_far, 2), (small_step, 2)],
-        3: [(small_step, 3)],
-        4: [(begin_near, 3), (begin_near, 2), (small_step, 4)],
-        5: [(small_step, 5)],
-        6: [(join_near, 3), (join_near, 2)],
-        7: [(begin_far, 1), (begin_far, 0)],
-        9: [(join_far, 1), (join_far, 0)],
-        11: [(begin_near, 1), (begin_near, 0)],
-        13: [(join_near, 1), (join_near, 0)],
+        2: [(small_step, 1)],
+        3: [(join_far, 3), (join_far, 2)],
+        4: [(small_step, 2)],
+        5: [(begin_near, 3), (begin_near, 2)],
+        6: [(small_step, 3)],
+        8: [(join_near, 3), (join_near, 2), (end_fresh, 3), (begin_far, 1), (begin_far, 0)],
+        9: [(small_step, 4)],
+        10: [(join_far, 1), (join_far, 0)],
+        11: [(small_step, 5)],
+        12: [(end_fresh, 2), (inner_fresh, 2), (begin_near, 1), (begin_near, 0)],
+        15: [(join_near, 1), (join_near, 0), (end_fresh, 1), (inner_fresh, 1)],
     }
 
     def tiles(pairs):
@@ -989,7 +1007,7 @@
                     relay(n, h)
                 add_rows(n, h)
 
-        @pl.when((step == 14) & inner)
+        @pl.when((step == 13) & inner)
         def _():
             relay(3, 0)
 
@@ -1018,6 +1036,7 @@
     @pl.when(inner)
     def _():
         relay(3, 1)
+        relay_fresh(3)
 
     for half in range(2):
 

time: 165 us -> 157 us (0.952); the launches traced: 162 us -> 157 us
  Pallas kernels: 159 us -> 154 us
    pallas_call x1, Pallas kernels: 81.1 us -> 75.3 us  [back_pass(): pl.pallas_call(functools.partial(back_kernel, slots), in_specs=[vmem] * 7...]
where the time goes in v6:
time: 157 us
  Pallas kernels  154 us (98%)
  local copies, waits for them, and re-layouts  2.09 us (1%)
    pallas_call x1, Pallas kernels, back_pass(): pl.pallas_call(functools.partial(back_kernel, slots), in_specs=[vmem] * 7...  75.3 us
    pallas_call x1, Pallas kernels, front(): pl.pallas_call(functools.partial(front_kernel, slots, sub), in_specs=[hbm...  47.9 us
    pallas_call x1, Pallas kernels, middle(): pl.pallas_call(functools.partial(middle_kernel, groups, hidden_cols, bloc...  29 us

profile of v6, /device:TPU:0, one launch (start us, length us, event | category | flops | bytes accessed | tf_op | source)
XLA Modules:
  0.0 156.7 jit_solution(11126389273753970492)
XLA Ops:
  0.7 0.0 copy-start.2
  0.7 0.0 copy-start
  0.7 0.7 copy-done
  1.4 0.0 copy-start.1
  1.4 0.7 copy-done.1
  2.1 0.0 copy-start.8
  2.1 0.7 copy-done.8
  2.7 0.0 copy-start.3
  2.7 0.0 copy-start.4
  2.7 0.0 copy-start.5
  2.7 0.0 copy-start.6
  2.7 0.0 copy-start.7
  2.8 47.9 %front.1 = (bf16[4,8,80,1408]{3,2,1,0:T(8,128)(2,1)S(1)}, bf16[640,576]{1,0:T(8,128)(2,1)S(1)}, f32[4,1,640]{2,1,0:T(1,128)S(1)}, bf16[3,2048,256]{2,1,0:T(8,128...) custom-call(bf16[2048,640]{1,0:T(8,128)(2,1)} %x_hbm.3, ...), custom_call_target="tpu_custom_call" | custom-call | tf_op jit(solution)/shard_map/front/pallas_call | solution.py:345
  50.7 0.0 copy-done.2
  50.7 0.0 copy-done.3
  50.7 0.0 copy-done.4
  50.7 0.0 copy-done.5
  50.7 0.0 copy-done.6
  50.7 0.0 copy-done.7
  50.7 29.0 %middle.1 = (bf16[512,640]{1,0:T(8,128)(2,1)S(1)}, f32[512,640]{1,0:T(8,128)S(1)}, bf16[4,2,384,128]{3,2,1,0:T(8,128)(2,1)S(1)}, bf16[4,4,80,1408]{3,2,1,0:T(8,128)(2,1)S(1)}, f32[16,640]{1,0:T(8,128)S(1)}) custom-call(bf16[2048,640]{1,0:T(8,128)(2,1)} %x_hbm.3, bf16[2048,640]{1,0:T(8,128)(2,1)} %y_ref.1, ...), custom_call_target="tpu_custom_call" | custom-call | tf_op jit(solution)/shard_map/middle/pallas_call | solution.py:718
  79.7 75.3 %back_pass.1 = (bf16[512,640]{1,0:T(8,128)(2,1)S(1)}, f32[3,80,192]{2,1,0:T(8,128)S(1)}, f32[2,192]{1,0:T(2,128)S(1)}, f32[80,560]{1,0:T(8,128)S(1)}, f32[80,560...) custom-call(bf16[3,2048,256]{2,1,0:T(8,128)(2,1)S(1)} %get-tuple-ele, ...), custom_call_target="tpu_custom_call" | custom-call | tf_op jit(solution)/shard_map/back_pass/pallas_call | solution.py:1109
  155.1 1.4 deliver.1
Async XLA Ops:
  0.7 50.0 %copy-start.2 = (f32[640]{0:T(1024)S(1)}, f32[640]{0:T(1024)}, u32[]{:S(2)}) copy-start(f32[640]{0:T(1024)} %v0.1) | copy-start | bytes 7684
  0.7 0.7 copy-start
  1.4 0.7 copy-start.1
  2.1 0.7 copy-start.8
  2.7 47.9 %copy-start.3 = (f32[640]{0:T(1024)S(1)}, f32[640]{0:T(1024)}, u32[]{:S(2)}) copy-start(f32[640]{0:T(1024)} %v1.1) | copy-start | bytes 7684
  2.7 47.9 %copy-start.4 = (f32[640]{0:T(1024)S(1)}, f32[640]{0:T(1024)}, u32[]{:S(2)}) copy-start(f32[640]{0:T(1024)} %v2.1) | copy-start | bytes 7684
  2.7 48.0 %copy-start.5 = (f32[640]{0:T(1024)S(1)}, f32[640]{0:T(1024)}, u32[]{:S(2)}) copy-start(f32[640]{0:T(1024)} %v3.1) | copy-start | bytes 7684
  2.7 48.0 %copy-start.6 = (f32[640]{0:T(1024)S(1)}, f32[640]{0:T(1024)}, u32[]{:S(2)}) copy-start(f32[640]{0:T(1024)} %v4.1) | copy-start | bytes 7684
  2.7 48.0 %copy-start.7 = (f32[640]{0:T(1024)S(1)}, f32[640]{0:T(1024)}, u32[]{:S(2)}) copy-start(f32[640]{0:T(1024)} %v5.1) | copy-start | bytes 7684

commit v7 on v6

--- a/solution.py
+++ b/solution.py
@@ -60,11 +60,15 @@
     kk_ref[rows, :] = made[:, width : 2 * width]
 
 
-def plane_barrier(peers):
-    barrier = pltpu.get_barrier_semaphore()
+def announce(peers):
     for peer in peers:
-        pl.semaphore_signal(barrier, inc=1, device_id=peer, device_id_type=MESH)
-    pl.semaphore_wait(barrier, len(peers))
+        pl.semaphore_signal(
+            pltpu.get_barrier_semaphore(), inc=1, device_id=peer, device_id_type=MESH
+        )
+
+
+def await_peers(count):
+    pl.semaphore_wait(pltpu.get_barrier_semaphore(), count)
 
 
 def remote(src, dst, send, recv, peer):
@@ -102,6 +106,7 @@
     sibling = (dp ^ 1, mp)
     tall = [(dp, mp ^ s) for s in range(1, 4)]
     inner = (mp == 1) | (mp == 2)
+    announce([sibling] + [(d, mp) for d in plane] + tall)
     width = slots * HD
     pairs = ((qkv_hbm, qkv_ref), (up_hbm, up_ref), (down_hbm, down_ref), (out_hbm, out_ref), (x_hbm, x_ref))
     loads = [pltpu.make_async_copy(a, b, loaded.at[i]) for i, (a, b) in enumerate(pairs)]
@@ -122,7 +127,7 @@
     pack_ref[:, HALF + hidden_cols : HALF + hidden_cols + rest] = out_ref[:, gap:]
     spare = pack_ref.shape[1] - HALF - hidden_cols - rest
     pack_ref[:, HALF + hidden_cols + rest :] = jnp.zeros((pack_ref.shape[0], spare), BF16)
-    plane_barrier([sibling] + [(d, mp) for d in plane] + tall)
+    await_peers(7)
     rows = x_ref.shape[0]
     share = rows // 4
 
@@ -536,7 +541,7 @@
         back_own, got, grads, arrived, b_send, b_recv, g_send, g_recv = scratch[10:]
         core = lax.rem(dp, 2)
         sibling = (dp ^ 1, mp)
-        plane_barrier([sibling] + [(dp, mp ^ s) for s in range(1, 4)])
+        announce([sibling] + [(dp, mp ^ s) for s in range(1, 4)])
     else:
         back_own, got, grads = back_ref, got_ref, grad_ref
     out_bias, gain_one, shift_one, down_bias, gain_two, shift_two = (
@@ -552,6 +557,8 @@
     ]
     for copy in loads:
         copy.wait()
+    if linked:
+        await_peers(4)
 
     def send_back(step, s):
         at = step * 3 + s - 1
@@ -765,7 +772,7 @@
     width = slots * HD
     others = [(dp ^ d, mp) for d in range(1, 8)]
     tall = [(dp, mp ^ s) for s in range(1, 4)]
-    plane_barrier(others + tall)
+    announce(others + tall)
     x_peer, y_peer = (dp ^ 2, mp), (dp ^ 4, mp)
 
     def rows_of(name):
@@ -913,9 +920,6 @@
     dv_acc[...] = jnp.zeros_like(dv_acc)
     gq_acc[...] = jnp.zeros_like(gq_acc)
     gb_own[...] = jnp.zeros_like(gb_own)
-    far(3).start()
-    far(2).start()
-    small_step(0)
 
     def prepare(step, carry):
         at = pl.ds(pl.multiple_of(step * share, share), share)
@@ -934,6 +938,10 @@
         return carry
 
     lax.fori_loop(0, 4, prepare, 0)
+    await_peers(10)
+    far(3).start()
+    far(2).start()
+    small_step(0)
     actions = {
         2: [(small_step, 1)],
         3: [(join_far, 3), (join_far, 2)],

time: 157 us -> 155 us (0.987)
  Pallas kernels: 154 us -> 151 us
where the time goes in v7:
time: 155 us; the launch traced here: 154 us
  Pallas kernels  151 us (97%)
  local copies, waits for them, and re-layouts  2.09 us (1%)
    pallas_call x1, Pallas kernels, back_pass(): pl.pallas_call(functools.partial(back_kernel, slots), in_specs=[vmem] * 7...  74.5 us
    pallas_call x1, Pallas kernels, front(): pl.pallas_call(functools.partial(front_kernel, slots, sub), in_specs=[hbm...  46.8 us
    pallas_call x1, Pallas kernels, middle(): pl.pallas_call(functools.partial(middle_kernel, groups, hidden_cols, bloc...  28.3 us

profile of v7, /device:TPU:0, one launch (start us, length us, event | category | flops | bytes accessed | tf_op | source)
XLA Modules:
  0.0 154.0 jit_solution(12372199356024691255)
XLA Ops:
  0.7 0.0 copy-start.2
  0.7 0.0 copy-start
  0.7 0.7 copy-done
  1.4 0.0 copy-start.1
  1.4 0.7 copy-done.1
  2.1 0.0 copy-start.8
  2.1 0.7 copy-done.8
  2.7 0.0 copy-start.3
  2.7 0.0 copy-start.4
  2.7 0.0 copy-start.5
  2.7 0.0 copy-start.6
  2.7 0.0 copy-start.7
  2.8 46.8 %front.1 = (bf16[4,8,80,1408]{3,2,1,0:T(8,128)(2,1)S(1)}, bf16[640,576]{1,0:T(8,128)(2,1)S(1)}, f32[4,1,640]{2,1,0:T(1,128)S(1)}, bf16[3,2048,256]{2,1,0:T(8,128...) custom-call(bf16[2048,640]{1,0:T(8,128)(2,1)} %x_hbm.3, ...), custom_call_target="tpu_custom_call" | custom-call | tf_op jit(solution)/shard_map/front/pallas_call | solution.py:350
  49.5 0.0 copy-done.2
  49.5 0.0 copy-done.3
  49.5 0.0 copy-done.4
  49.6 0.0 copy-done.5
  49.6 0.0 copy-done.6
  49.6 0.0 copy-done.7
  49.6 28.3 %middle.1 = (bf16[512,640]{1,0:T(8,128)(2,1)S(1)}, f32[512,640]{1,0:T(8,128)S(1)}, bf16[4,2,384,128]{3,2,1,0:T(8,128)(2,1)S(1)}, bf16[4,4,80,1408]{3,2,1,0:T(8,128)(2,1)S(1)}, f32[16,640]{1,0:T(8,128)S(1)}) custom-call(bf16[2048,640]{1,0:T(8,128)(2,1)} %x_hbm.3, bf16[2048,640]{1,0:T(8,128)(2,1)} %y_ref.1, ...), custom_call_target="tpu_custom_call" | custom-call | tf_op jit(solution)/shard_map/middle/pallas_call | solution.py:725
  77.8 74.5 %back_pass.1 = (bf16[512,640]{1,0:T(8,128)(2,1)S(1)}, f32[3,80,192]{2,1,0:T(8,128)S(1)}, f32[2,192]{1,0:T(2,128)S(1)}, f32[80,560]{1,0:T(8,128)S(1)}, f32[80,560...) custom-call(bf16[3,2048,256]{2,1,0:T(8,128)(2,1)S(1)} %get-tuple-ele, ...), custom_call_target="tpu_custom_call" | custom-call | tf_op jit(solution)/shard_map/back_pass/pallas_call | solution.py:1117
  152.4 1.4 deliver.1
Async XLA Ops:
  0.7 48.9 %copy-start.2 = (f32[640]{0:T(1024)S(1)}, f32[640]{0:T(1024)}, u32[]{:S(2)}) copy-start(f32[640]{0:T(1024)} %v0.1) | copy-start | bytes 7684
  0.7 0.7 copy-start
  1.4 0.7 copy-start.1
  2.1 0.7 copy-start.8
  2.7 46.8 %copy-start.3 = (f32[640]{0:T(1024)S(1)}, f32[640]{0:T(1024)}, u32[]{:S(2)}) copy-start(f32[640]{0:T(1024)} %v1.1) | copy-start | bytes 7684
  2.7 46.8 %copy-start.4 = (f32[640]{0:T(1024)S(1)}, f32[640]{0:T(1024)}, u32[]{:S(2)}) copy-start(f32[640]{0:T(1024)} %v2.1) | copy-start | bytes 7684
  2.7 46.8 %copy-start.5 = (f32[640]{0:T(1024)S(1)}, f32[640]{0:T(1024)}, u32[]{:S(2)}) copy-start(f32[640]{0:T(1024)} %v3.1) | copy-start | bytes 7684
  2.7 46.8 %copy-start.6 = (f32[640]{0:T(1024)S(1)}, f32[640]{0:T(1024)}, u32[]{:S(2)}) copy-start(f32[640]{0:T(1024)} %v4.1) | copy-start | bytes 7684
  2.7 46.8 %copy-start.7 = (f32[640]{0:T(1024)S(1)}, f32[640]{0:T(1024)}, u32[]{:S(2)}) copy-start(f32[640]{0:T(1024)} %v5.1) | copy-start | bytes 7684

commit v8 on v7

--- a/solution.py
+++ b/solution.py
@@ -114,19 +114,9 @@
         copy.start()
     bias_ref[...] = jnp.zeros_like(bias_ref)
     bias_ref[:, : up_hbm.shape[1]] = ub_ref[...].reshape(1, up_hbm.shape[1])
-    for copy in loads[:4]:
-        copy.wait()
+    loads[0].wait()
     for i in range(3):
         wq_ref[:, i * width : (i + 1) * width] = qkv_ref[i]
-    hidden_cols = up_ref.shape[1]
-    gap = HALF - hidden_cols
-    rest = width - gap
-    pack_ref[:, :hidden_cols] = up_ref[...]
-    pack_ref[:, hidden_cols:HALF] = out_ref[:, :gap]
-    pack_ref[:, HALF : HALF + hidden_cols] = down_ref[...]
-    pack_ref[:, HALF + hidden_cols : HALF + hidden_cols + rest] = out_ref[:, gap:]
-    spare = pack_ref.shape[1] - HALF - hidden_cols - rest
-    pack_ref[:, HALF + hidden_cols + rest :] = jnp.zeros((pack_ref.shape[0], spare), BF16)
     await_peers(7)
     rows = x_ref.shape[0]
     share = rows // 4
@@ -146,6 +136,17 @@
         copy.start()
     shared = [remote(wq_ref, rows_of(dp), q_send.at[3], q_recv.at[3], sibling)]
     shared[0].start()
+    for copy in loads[1:4]:
+        copy.wait()
+    hidden_cols = up_ref.shape[1]
+    gap = HALF - hidden_cols
+    rest = width - gap
+    pack_ref[:, :hidden_cols] = up_ref[...]
+    pack_ref[:, hidden_cols:HALF] = out_ref[:, :gap]
+    pack_ref[:, HALF : HALF + hidden_cols] = down_ref[...]
+    pack_ref[:, HALF + hidden_cols : HALF + hidden_cols + rest] = out_ref[:, gap:]
+    spare = pack_ref.shape[1] - HALF - hidden_cols - rest
+    pack_ref[:, HALF + hidden_cols + rest :] = jnp.zeros((pack_ref.shape[0], spare), BF16)
     own = pltpu.make_async_copy(pack_ref, all_ref.at[mp, dp], here.at[1])
     own.start()
     def lift(at, s, landing, peer):

time: 155 us -> 155 us (level)
  no operation moved by 1% of the time
where the time goes in v8:
time: 155 us; the launch traced here: 154 us
  Pallas kernels  151 us (97%)
  local copies, waits for them, and re-layouts  2.09 us (1%)
    pallas_call x1, Pallas kernels, back_pass(): pl.pallas_call(functools.partial(back_kernel, slots), in_specs=[vmem] * 7...  74.7 us
    pallas_call x1, Pallas kernels, front(): pl.pallas_call(functools.partial(front_kernel, slots, sub), in_specs=[hbm...  46.6 us
    pallas_call x1, Pallas kernels, middle(): pl.pallas_call(functools.partial(middle_kernel, groups, hidden_cols, bloc...  28.3 us

profile of v8, /device:TPU:0, one launch (start us, length us, event | category | flops | bytes accessed | tf_op | source)
XLA Modules:
  0.0 154.0 jit_solution(4773539465617823375)
XLA Ops:
  0.7 0.0 copy-start.2
  0.7 0.0 copy-start
  0.7 0.7 copy-done
  1.4 0.0 copy-start.1
  1.4 0.7 copy-done.1
  2.1 0.0 copy-start.8
  2.1 0.7 copy-done.8
  2.7 0.0 copy-start.3
  2.7 0.0 copy-start.4
  2.7 0.0 copy-start.5
  2.7 0.0 copy-start.6
  2.7 0.0 copy-start.7
  2.8 46.6 %front.1 = (bf16[4,8,80,1408]{3,2,1,0:T(8,128)(2,1)S(1)}, bf16[640,576]{1,0:T(8,128)(2,1)S(1)}, f32[4,1,640]{2,1,0:T(1,128)S(1)}, bf16[3,2048,256]{2,1,0:T(8,128...) custom-call(bf16[2048,640]{1,0:T(8,128)(2,1)} %x_hbm.3, ...), custom_call_target="tpu_custom_call" | custom-call | tf_op jit(solution)/shard_map/front/pallas_call | solution.py:351
  49.3 0.0 copy-done.2
  49.3 0.0 copy-done.3
  49.3 0.0 copy-done.4
  49.4 0.0 copy-done.5
  49.4 0.0 copy-done.6
  49.4 0.0 copy-done.7
  49.4 28.3 %middle.1 = (bf16[512,640]{1,0:T(8,128)(2,1)S(1)}, f32[512,640]{1,0:T(8,128)S(1)}, bf16[4,2,384,128]{3,2,1,0:T(8,128)(2,1)S(1)}, bf16[4,4,80,1408]{3,2,1,0:T(8,128)(2,1)S(1)}, f32[16,640]{1,0:T(8,128)S(1)}) custom-call(bf16[2048,640]{1,0:T(8,128)(2,1)} %x_hbm.3, bf16[2048,640]{1,0:T(8,128)(2,1)} %y_ref.1, ...), custom_call_target="tpu_custom_call" | custom-call | tf_op jit(solution)/shard_map/middle/pallas_call | solution.py:726
  77.7 74.7 %back_pass.1 = (bf16[512,640]{1,0:T(8,128)(2,1)S(1)}, f32[3,80,192]{2,1,0:T(8,128)S(1)}, f32[2,192]{1,0:T(2,128)S(1)}, f32[80,560]{1,0:T(8,128)S(1)}, f32[80,560...) custom-call(bf16[3,2048,256]{2,1,0:T(8,128)(2,1)S(1)} %get-tuple-ele, ...), custom_call_target="tpu_custom_call" | custom-call | tf_op jit(solution)/shard_map/back_pass/pallas_call | solution.py:1118
  152.4 1.4 deliver.1
Async XLA Ops:
  0.7 48.7 %copy-start.2 = (f32[640]{0:T(1024)S(1)}, f32[640]{0:T(1024)}, u32[]{:S(2)}) copy-start(f32[640]{0:T(1024)} %v0.1) | copy-start | bytes 7684
  0.7 0.7 copy-start
  1.4 0.7 copy-start.1
  2.1 0.7 copy-start.8
  2.7 46.6 %copy-start.3 = (f32[640]{0:T(1024)S(1)}, f32[640]{0:T(1024)}, u32[]{:S(2)}) copy-start(f32[640]{0:T(1024)} %v1.1) | copy-start | bytes 7684
  2.7 46.6 %copy-start.4 = (f32[640]{0:T(1024)S(1)}, f32[640]{0:T(1024)}, u32[]{:S(2)}) copy-start(f32[640]{0:T(1024)} %v2.1) | copy-start | bytes 7684
  2.7 46.6 %copy-start.5 = (f32[640]{0:T(1024)S(1)}, f32[640]{0:T(1024)}, u32[]{:S(2)}) copy-start(f32[640]{0:T(1024)} %v3.1) | copy-start | bytes 7684
  2.7 46.6 %copy-start.6 = (f32[640]{0:T(1024)S(1)}, f32[640]{0:T(1024)}, u32[]{:S(2)}) copy-start(f32[640]{0:T(1024)} %v4.1) | copy-start | bytes 7684
  2.7 46.6 %copy-start.7 = (f32[640]{0:T(1024)S(1)}, f32[640]{0:T(1024)}, u32[]{:S(2)}) copy-start(f32[640]{0:T(1024)} %v5.1) | copy-start | bytes 7684
